TPU v7x, 512 devices: a whole 4x8x8 slice. The times are simulated.
512 devices in a mesh: rep: 32 (over x, y), tp: 16 (over z, core).
Axes of the slice: x: 4, y: 8, z: 8, core: 2. Of those that a mesh axis runs over, the one named last changes fastest.
Arguments:
- queries: bfloat16 [416, 48, 4096], P('rep', None, 'tp'), may hold values from -33 to 33
- tree_cache: bfloat16 [416, 2, 48, 4096], P('rep', None, None, 'tp'), may hold values from -11 to 11
- tree_mask: int32 [416, 48, 48], P('rep'), may hold values from 0 to 1, as said below
- dest_group: int32 [416, 1], P('rep'), may hold values from 0 to 31; in each aligned block of 13 rows (0 to 12, 13 to 25, ...) at most 2 rows name the same one
- accepted_path: int32 [416, 8], P('rep'), may hold values from 0 to 47
- prompt_cache: bfloat16 [32, 2, 152, 4096], P('rep', None, None, 'tp'), may hold values from -11 to 11
- first_len: int32 [32], P('rep'), may hold values from 2 to 152
- spill_cache: bfloat16 [32, 2, 152, 4096], P('rep', None, None, 'tp'), may hold values from -6 to 6
- spill_len: int32 [32], P('rep'), may hold values from 76 to 152
- out_weight: bfloat16 [4096, 4096], P(None, 'tp'), may hold values from -0.09375 to 0.09375
Outputs:
- projected: bfloat16 [416, 48, 4096], P('rep', None, 'tp')
- accepted_cache: bfloat16 [416, 2, 8, 4096], P('rep', None, None, 'tp')
Inputs may be any that keep to these rules, and one draw needn't show every extreme that they name: `dest_group`: in each aligned block of 13 requests (those of one index of rep) no group is named more than 2 times. Row t of tree_mask[r] marks token t and its ancestors in a tree whose parents come before their children.
All inputs are finite; a program needn't handle non-finite values.
Results may differ from a plain program's by a relative error of at most 0.014.
Values may be sent and summed in bfloat16 or wider, within the bound.
A program may use at most 64 MiB of HBM per device.

v0:
```python
import math

import jax
import jax.numpy as jnp
from jax import lax
from jax.sharding import PartitionSpec as P

HD = 128
TREE = 48
PCAP = 152


NEG_FILL = -1e30


def swapped(value, axis, apart):
    mask = 2**apart
    pairs = [(source, source ^ mask) for source in range(lax.axis_size(axis))]
    return lax.ppermute(value, axis, pairs)


def attend_part(query_rows, key_rows, value_rows, visible, head_size):
    heads_here = query_rows.shape[2] // head_size
    maxima = []
    totals = []
    partial_sums = []
    for head_index in range(heads_here):
        lower = head_index * head_size
        upper = lower + head_size
        scores = lax.dot_general(
            query_rows[:, :, lower:upper],
            key_rows[:, :, lower:upper],
            (((2,), (2,)), ((0,), (0,))),
            preferred_element_type=jnp.float32,
        ) * (1.0 / math.sqrt(head_size))
        scores = jnp.where(visible, scores, NEG_FILL)
        peaks = jnp.max(scores, axis=2)
        raw_weights = jnp.where(visible, jnp.exp(scores - peaks[:, :, None]), 0.0)
        maxima.append(peaks)
        totals.append(jnp.sum(raw_weights, axis=2))
        partial_sums.append(
            lax.dot_general(
                raw_weights.astype(jnp.bfloat16),
                value_rows[:, :, lower:upper],
                (((2,), (1,)), ((0,), (0,))),
                preferred_element_type=jnp.float32,
            )
        )
    return (
        jnp.stack(maxima, axis=-1),
        jnp.stack(totals, axis=-1),
        jnp.concatenate(partial_sums, axis=-1),
    )


def combine_parts(first_part, second_part, head_size):
    max_first, total_first, accum_first = first_part
    max_second, total_second, accum_second = second_part
    peaks = jnp.maximum(max_first, max_second)
    factor_first = jnp.exp(max_first - peaks)
    factor_second = jnp.exp(max_second - peaks)
    totals = total_first * factor_first + total_second * factor_second
    full_shape = accum_first.shape
    split_shape = full_shape[:-1] + (full_shape[-1] // head_size, head_size)
    accum = (
        accum_first.reshape(split_shape) * factor_first[..., None]
        + accum_second.reshape(split_shape) * factor_second[..., None]
    )
    return (peaks, totals, accum.reshape(full_shape))


def local(
    queries,
    tree_cache,
    tree_mask,
    dest_group,
    accepted_path,
    prompt_cache,
    first_len,
    spill_cache,
    spill_len,
    out_weight,
):
    req_here = queries.shape[0]
    local_cols = queries.shape[2]
    heads_here = local_cols // HD
    groups = lax.axis_size("rep")
    per_group = max(2, (req_here + groups - 1) // groups)
    n_slots = groups * per_group
    target = dest_group[:, 0]
    same_target = target[:, None] == target[None, :]
    earlier = jnp.arange(req_here)[None, :] < jnp.arange(req_here)[:, None]
    rank_index = jnp.sum(jnp.logical_and(same_target, earlier), axis=1)
    slot_index = target * per_group + rank_index
    selector = (jnp.arange(n_slots, dtype=jnp.int32)[:, None] == slot_index[None, :]).astype(
        jnp.bfloat16
    )
    outbound = jnp.einsum(
        "sr,rtc->stc", selector, queries, preferred_element_type=jnp.float32
    ).astype(jnp.bfloat16)
    outbound = outbound.reshape(groups, per_group, TREE, local_cols)
    inbound = lax.all_to_all(outbound, "rep", split_axis=0, concat_axis=0, tiled=True)
    routed_rows = inbound.reshape(1, n_slots * TREE, local_cols)
    positions = jnp.arange(PCAP, dtype=jnp.int32)
    prompt_seen = (positions < first_len[0])[None, None, :]
    prompt_part = attend_part(routed_rows, prompt_cache[:, 0], prompt_cache[:, 1], prompt_seen, HD)
    live_flag = (positions < spill_len[0]).astype(jnp.bfloat16)
    partner_cache, partner_flag = swapped((spill_cache, live_flag), "rep", 0)
    spill_seen = (partner_flag > 0.5)[None, None, :]
    spill_part = attend_part(routed_rows, partner_cache[:, 0], partner_cache[:, 1], spill_seen, HD)
    merged_max, merged_total, merged_accum = combine_parts(prompt_part, spill_part, HD)
    back_max, back_total, back_accum = (
        lax.all_to_all(
            merged_max.reshape(groups, per_group, TREE, heads_here),
            "rep",
            split_axis=0,
            concat_axis=0,
            tiled=True,
        ),
        lax.all_to_all(
            merged_total.reshape(groups, per_group, TREE, heads_here),
            "rep",
            split_axis=0,
            concat_axis=0,
            tiled=True,
        ),
        lax.all_to_all(
            merged_accum.reshape(groups, per_group, TREE, local_cols),
            "rep",
            split_axis=0,
            concat_axis=0,
            tiled=True,
        ),
    )
    remote_part = (
        jnp.take(back_max.reshape(n_slots, TREE, heads_here), slot_index, axis=0),
        jnp.take(back_total.reshape(n_slots, TREE, heads_here), slot_index, axis=0),
        jnp.take(back_accum.reshape(n_slots, TREE, local_cols), slot_index, axis=0),
    )
    tree_seen = tree_mask == 1
    tree_part = attend_part(queries, tree_cache[:, 0], tree_cache[:, 1], tree_seen, HD)
    final_max, final_total, final_accum = combine_parts(remote_part, tree_part, HD)
    attn = final_accum.reshape(req_here, TREE, heads_here, HD) / final_total[..., None]
    attn = attn.reshape(req_here * TREE, local_cols).astype(jnp.bfloat16)
    summed = jnp.dot(
        lax.all_gather(attn, "tp", axis=1, tiled=True),
        out_weight,
        preferred_element_type=jnp.float32,
    )
    projected = summed.astype(jnp.bfloat16).reshape(req_here, TREE, out_weight.shape[1])
    accepted_cache = jnp.take_along_axis(tree_cache, accepted_path[:, None, :, None], axis=2)
    return (projected, accepted_cache)


def solution(mesh):
    return jax.shard_map(
        local,
        mesh=mesh,
        in_specs=(
            P("rep", None, "tp"),
            P("rep", None, None, "tp"),
            P("rep", None, None),
            P("rep", None),
            P("rep", None),
            P("rep", None, None, "tp"),
            P("rep"),
            P("rep", None, None, "tp"),
            P("rep"),
            P(None, "tp"),
        ),
        out_specs=(P("rep", None, "tp"), P("rep", None, None, "tp")),
        check_vma=False,
    )
```

profile of v0, /device:TPU:1, one launch (start us, length us, event | category | flops | bytes accessed | tf_op | source)
XLA Modules:
  0.0 319.3 jit_solution(14354112950949048452)
XLA Ops:
  13.0 10.7 %all-to-all-start = ((bf16[32,2,48,256]{3,2,1,0:T(8,128)(2,1)}), bf16[32,2,48,256]{3,2,1,0:T(8,128)(2,1)}, u32[]{:S(2)}, u32[]{:S(2)}) async-start(bf16[32,2,48,256]{3,2,1,0:T(8,128)(2,1)} %bitcast.162), calls=%async_computation | async-start | bytes 3145728 | tf_op jit(solution)/shard_map/all_to_all | solution.py:102
  23.8 3.1 collective-permute-start.1
  30.5 31.8 %collective-permute-done = bf16[152]{0:T(256)(128)(2,1)S(1)} collective-permute-done((bf16[152]{0:T(256)(128)(2,1)S(1)}, bf16[152]{0:T(256)(128)(2,1)S(1)}, u32[]{:S(2)}, u32[]{:S(2)}) %collective-permute-start) | collective-permute-done | bytes 336 | tf_op jit(solution)/shard_map/ppermute | solution.py:19
  62.3 3.1 fusion.59
  65.3 3.1 fusion.60
  68.4 3.1 fusion.57
  71.5 3.0 fusion.58
  74.8 3.8 %fusion.9 = (f32[3072]{0:T(1024)S(1)}, f32[3072]{0:T(1024)S(1)}, bf16[3072,152]{0,1:T(8,128)(2,1)S(1)}, bf16[3072,152]{0,1:T(8,128)(2,1)}) fusion(f32[3072,152]{0,1:T(8,128)} %get-tuple-element.47, f32[3072]{0:T(1024)S(1)} %get-tuple-element.46, pred[152]{0:T(512)(128)(4,1)S(1)} %broadcast_compare_fusion.1, f32[3072,152]{0,1:T(8,128)} %get-tuple-element.49, ...), kind=kLoop, calls=%fused_computation.24 | loop fusion | flops 3729408 | bytes 5652632 | tf_op jit(solution)/shard_map/reduce_sum | solution.py:40
  82.5 3.3 %fusion.38 = f32[32,2,48,128]{3,2,1,0:T(8,128)} fusion(bf16[32,2,48,152]{3,2,1,0:T(8,128)(2,1)} %bitcast.166, bf16[1,152,256]{2,1,0:T(8,128)(2,1)S(1)} %get-tuple-element.32), kind=kOutput, calls=%fused_computation.74 | convolution fusion | flops 119537664 | bytes 2545664 | tf_op jit(solution)/shard_map/dot_general | solution.py:42
  87.7 3.7 %fusion.5 = (f32[3072]{0:T(1024)S(1)}, f32[3072]{0:T(1024)S(1)}, bf16[3072,152]{0,1:T(8,128)(2,1)S(1)}, bf16[3072,152]{0,1:T(8,128)(2,1)}) fusion(f32[3072,152]{0,1:T(8,128)} %get-tuple-element.43, f32[3072]{0:T(1024)S(1)} %get-tuple-element.42, pred[152]{0:T(512)(128)(4,1)S(1)} %iota_compare_fusion.2, f32[3072,152]{0,1:T(8,128)} %get-tuple-element.45, ...), kind=kLoop, calls=%fused_computation.20 | loop fusion | flops 3729408 | bytes 5652632 | tf_op jit(solution)/shard_map/reduce_sum | solution.py:40
  91.4 2.5 copy.97
  96.8 9.2 %all-to-all-start.2 = ((f32[32,1,192]{2,1,0:T(1,128)}), f32[32,1,192]{2,1,0:T(1,128)S(1)}, u32[]{:S(2)}, u32[]{:S(2)}) async-start(f32[32,1,192]{2,1,0:T(1,128)} %reshape.496), calls=%async_computation.2 | async-start | bytes 65536 | tf_op jit(solution)/shard_map/all_to_all | solution.py:113
  106.1 3.3 %fusion.40 = f32[32,2,48,128]{3,2,1,0:T(8,128)} fusion(bf16[32,2,48,152]{3,2,1,0:T(8,128)(2,1)} %bitcast.164, bf16[1,152,256]{2,1,0:T(8,128)(2,1)S(1)} %get-tuple-element.34), kind=kOutput, calls=%fused_computation.80 | convolution fusion | flops 119537664 | bytes 2545664 | tf_op jit(solution)/shard_map/dot_general | solution.py:42
  112.8 8.1 %mul.105 = f32[3072,2,128]{2,1,0:T(2,128)} broadcast(f32[3072,2]{1,0:T(8,128)} %copy.98), dimensions={0,1} | broadcast | bytes 3170304 | tf_op jit(solution)/shard_map/mul | solution.py:66
  120.9 5.5 %mul.106 = f32[32,2,48,256]{3,2,1,0:T(8,128)} reshape(f32[3072,2,128]{2,1,0:T(2,128)} %mul.105) | data formatting | bytes 6291456 | tf_op jit(solution)/shard_map/mul | solution.py:66
  128.1 8.1 %mul.108 = f32[3072,2,128]{2,1,0:T(2,128)} broadcast(f32[3072,2]{1,0:T(8,128)} %copy.101), dimensions={0,1} | broadcast | bytes 3170304 | tf_op jit(solution)/shard_map/mul | solution.py:67
  136.2 5.5 %mul.109 = f32[32,2,48,256]{3,2,1,0:T(8,128)} reshape(f32[3072,2,128]{2,1,0:T(2,128)} %mul.108) | data formatting | bytes 6291456 | tf_op jit(solution)/shard_map/mul | solution.py:67
  142.6 9.1 %all-to-all-start.3 = ((f32[32,1,192]{2,1,0:T(1,128)}), f32[32,1,192]{2,1,0:T(1,128)S(1)}, u32[]{:S(2)}, u32[]{:S(2)}) async-start(f32[32,1,192]{2,1,0:T(1,128)} %reshape.498), calls=%async_computation.3 | async-start | bytes 65536 | tf_op jit(solution)/shard_map/all_to_all | solution.py:120
  151.6 7.4 %fusion.4 = f32[32,2,48,256]{3,2,1,0:T(8,128)} fusion(f32[32,2,48,256]{3,2,1,0:T(8,128)} %mul.106, f32[32,2,48,128]{3,2,1,0:T(8,128)} %fusion.40, f32[32,2,48,128]{3,2,1,0:T(8,128)} %fusion.41, f32[32,2,48,256]{3,2,1,0:T(8,128)} %mul.109, f32[32,2,48,128]{3,2,1,0:T(8,128)} %fusion.38, f32[32,2,48,128]{3,2,1,0:T(8,128)} %fusion.39), kind=kLoop, calls=%fused_computation.13 | loop fusion | flops 3932160 | bytes 15728640 | tf_op jit(solution)/shard_map/add | solution.py:66
  161.0 8.0 %all-to-all-start.1 = ((f32[32,2,48,256]{3,2,1,0:T(8,128)}), f32[32,2,48,256]{3,2,1,0:T(8,128)}, u32[]{:S(2)}, u32[]{:S(2)}) async-start(f32[32,2,48,256]{3,2,1,0:T(8,128)} %fusion.4), calls=%async_computation.1 | async-start | bytes 6291456 | tf_op jit(solution)/shard_map/all_to_all | solution.py:127
  187.9 51.7 %all-to-all-done.1 = f32[32,2,48,256]{3,2,1,0:T(8,128)} async-done(((f32[32,2,48,256]{3,2,1,0:T(8,128)}), f32[32,2,48,256]{3,2,1,0:T(8,128)}, u32[]{:S(2)}, u32[]{:S(2)}) %all-to-all-start.1) | async-done | bytes 3145760 | tf_op jit(solution)/shard_map/all_to_all | solution.py:127
  239.6 3.4 %gather_fusion = f32[13,48,256]{2,1,0:T(8,128)} fusion(f32[64,48,256]{2,1,0:T(8,128)} %bitcast.38, s32[1024]{0:T(1024)} %pad_clamp_fusion.1), kind=kCustom, calls=%fused_computation.2 | custom fusion | bytes 1278004 | tf_op jit(solution)/shard_map/jit(_take)/gather | solution.py:138
  251.2 56.6 %all-gather.2.cloned.1.call-done = bf16[624,4096]{1,0:T(8,128)(2,1)} async-done(((bf16[624,256]{1,0:T(8,128)(2,1)}), bf16[624,4096]{1,0:T(8,128)(2,1)}) %all-gather.2.cloned.1.call-update) | async-done | bytes 5111824 | tf_op jit(solution)/shard_map/all_gather | solution.py:146
  307.8 4.7 %convolution_convert_fusion.1 = bf16[624,256]{1,0:T(8,128)(2,1)} fusion(bf16[624,4096]{1,0:T(8,128)(2,1)} %all-gather.2.cloned.1.call-done, bf16[4096,256]{1,0:T(8,128)(2,1)S(1)} %copy-done), kind=kOutput, calls=%fused_computation.28 | convolution fusion | flops 1308782592 | bytes 7528448 | tf_op jit(solution)/shard_map/dot_general | solution.py:145
  (118 shorter events, 51.8 us)
Async XLA Ops:
  7.2 300.6 %copy-start = (bf16[4096,256]{1,0:T(8,128)(2,1)S(1)}, bf16[4096,256]{1,0:T(8,128)(2,1)}, u32[]{:S(2)}) copy-start(bf16[4096,256]{1,0:T(8,128)(2,1)} %param.21) | copy-start | bytes 6291460
  13.0 10.8 %copy-start.14 = (bf16[1,2,152,256]{3,2,1,0:T(8,128)(2,1)S(1)}, bf16[1,2,152,256]{3,2,1,0:T(8,128)(2,1)}, u32[]{:S(2)}) copy-start(bf16[1,2,152,256]{3,2,1,0:T(8,128)(2,1)} %param.19) | copy-start | bytes 466948
  13.0 17.4 %copy-start.9 = (bf16[1,2,152,256]{3,2,1,0:T(8,128)(2,1)S(1)}, bf16[1,2,152,256]{3,2,1,0:T(8,128)(2,1)}, u32[]{:S(2)}) copy-start(bf16[1,2,152,256]{3,2,1,0:T(8,128)(2,1)} %param.17) | copy-start | bytes 466948
  13.0 49.2 %all-to-all-start = ((bf16[32,2,48,256]{3,2,1,0:T(8,128)(2,1)}), bf16[32,2,48,256]{3,2,1,0:T(8,128)(2,1)}, u32[]{:S(2)}, u32[]{:S(2)}) async-start(bf16[32,2,48,256]{3,2,1,0:T(8,128)(2,1)} %bitcast.162), calls=%async_computation | async-start | bytes 3145728 | tf_op jit(solution)/shard_map/all_to_all | solution.py:102
  23.8 38.4 %collective-permute-start.1 = (bf16[1,2,152,256]{3,2,1,0:T(8,128)(2,1)S(1)}, bf16[1,2,152,256]{3,2,1,0:T(8,128)(2,1)S(1)}, u32[]{:S(2)}, u32[]{:S(2)}) collective-permute-start(bf16[1,2,152,256]{3,2,1,0:T(8,128)(2,1)S(1)} %copy-done.14), channel_id=1, source_target_pairs={{0,16},{16,0},{32,48},{48,32},{64,80},{80,64},{96,112},{112,96},{1... | collective-permute-start | bytes 466952 | tf_op jit(solution)/shard_map/ppermute | solution.py:19
  27.5 34.7 %collective-permute-start = (bf16[152]{0:T(256)(128)(2,1)S(1)}, bf16[152]{0:T(256)(128)(2,1)S(1)}, u32[]{:S(2)}, u32[]{:S(2)}) collective-permute-start(bf16[152]{0:T(256)(128)(2,1)S(1)} %compare_convert_fusion), channel_id=1, source_target_pairs={{0,16},{16,0},{32,48},{48,32},{64,80},{80,64},{96,112},{112,96},{1... | collective-permute-start | bytes 920 | tf_op jit(solution)/shard_map/ppermute | solution.py:19
  82.5 3.3 %copy-start.2 = (bf16[3072,152]{1,0:T(8,128)(2,1)S(1)}, bf16[3072,152]{1,0:T(8,128)(2,1)}, u32[]{:S(2)}) copy-start(bf16[3072,152]{1,0:T(8,128)(2,1)} %copy.99) | copy-start | bytes 2801668
  96.8 45.7 %all-to-all-start.2 = ((f32[32,1,192]{2,1,0:T(1,128)}), f32[32,1,192]{2,1,0:T(1,128)S(1)}, u32[]{:S(2)}, u32[]{:S(2)}) async-start(f32[32,1,192]{2,1,0:T(1,128)} %reshape.496), calls=%async_computation.2 | async-start | bytes 65536 | tf_op jit(solution)/shard_map/all_to_all | solution.py:113
  106.1 3.4 %copy-start.1 = (bf16[3072,152]{1,0:T(8,128)(2,1)S(1)}, bf16[3072,152]{1,0:T(8,128)(2,1)}, u32[]{:S(2)}) copy-start(bf16[3072,152]{1,0:T(8,128)(2,1)} %copy.96) | copy-start | bytes 2801668
  142.6 17.8 %all-to-all-start.3 = ((f32[32,1,192]{2,1,0:T(1,128)}), f32[32,1,192]{2,1,0:T(1,128)S(1)}, u32[]{:S(2)}, u32[]{:S(2)}) async-start(f32[32,1,192]{2,1,0:T(1,128)} %reshape.498), calls=%async_computation.3 | async-start | bytes 65536 | tf_op jit(solution)/shard_map/all_to_all | solution.py:120
  159.0 10.2 %copy-start.8 = (s32[13,48,48]{2,1,0:T(8,128)S(1)}, s32[13,48,48]{2,1,0:T(8,128)}, u32[]{:S(2)}) copy-start(s32[13,48,48]{2,1,0:T(8,128)} %param.14) | copy-start | bytes 359428
  159.0 10.5 %copy-start.3 = (bf16[13,2,48,256]{3,2,1,0:T(8,128)(2,1)S(1)}, bf16[13,2,48,256]{3,2,1,0:T(8,128)(2,1)}, u32[]{:S(2)}) copy-start(bf16[13,2,48,256]{3,2,1,0:T(8,128)(2,1)} %param.13) | copy-start | bytes 1916932
  160.4 0.6 copy-start.10
  161.0 78.6 %all-to-all-start.1 = ((f32[32,2,48,256]{3,2,1,0:T(8,128)}), f32[32,2,48,256]{3,2,1,0:T(8,128)}, u32[]{:S(2)}, u32[]{:S(2)}) async-start(f32[32,2,48,256]{3,2,1,0:T(8,128)} %fusion.4), calls=%async_computation.1 | async-start | bytes 6291456 | tf_op jit(solution)/shard_map/all_to_all | solution.py:127
  169.0 138.8 %all-gather.2.cloned.1.call-start = ((), (), s32[]{:S(2)}) async-start(), calls=%async_computation.4 | async-start | bytes 5431296 | tf_op jit(solution)/shard_map/all_gather | solution.py:146
  169.5 4.4 %copy-start.13 = (s32[13,1]{0,1:T(1,128)S(1)}, s32[13,1]{0,1:T(1,128)}, u32[]{:S(2)}) copy-start(s32[13,1]{0,1:T(1,128)} %param.15) | copy-start | bytes 160
  170.7 1.5 copy-start.5
  172.0 0.7 copy-start.6
  239.6 7.9 %copy-start.12 = (pred[624]{0:T(1024)(128)(4,1)S(1)}, pred[624]{0:T(1024)(128)(4,1)}, u32[]{:S(2)}) copy-start(pred[624]{0:T(1024)(128)(4,1)} %broadcast_in_dim.103) | copy-start | bytes 1876
  243.0 3.6 %copy-start.7 = (f32[13,48,2]{2,1,0:T(8,128)S(1)}, f32[13,48,2]{2,1,0:T(8,128)}, u32[]{:S(2)}) copy-start(f32[13,48,2]{2,1,0:T(8,128)} %copy.121) | copy-start | bytes 14980
  243.0 4.4 %copy-start.4 = (f32[13,48,256]{2,1,0:T(8,128)S(1)}, f32[13,48,256]{2,1,0:T(8,128)}, u32[]{:S(2)}) copy-start(f32[13,48,256]{2,1,0:T(8,128)} %gather_fusion) | copy-start | bytes 1916932
  247.5 1.0 copy-start.11
Sparse Core Ops, SparseCore 0:
  248.6 59.1 all-gather.1
where the time goes:
time: 321 us; the launch traced here: 319 us
  waiting for transfers between devices  141 us (44%)
  local copies, waits for them, and re-layouts  63.3 us (20%)
  starting transfers between devices  42.5 us (13%)
  matrix products  33.4 us (10%)
  other arithmetic  22.8 us (7%)
  between operations  15.8 us (5%)
    all_gather x1, waiting for transfers between devices, local(): lax.all_gather(attn, 'tp', axis=1, tiled=True)  56.6 us
    all_to_all x1, waiting for transfers between devices, local(): lax.all_to_all(merged_accum.reshape(groups, per_group, TREE, local_cols),...  51.7 us
    ppermute x2, waiting for transfers between devices, swapped(): return lax.ppermute(value, axis, pairs)  31.8 us
    mul x3, local copies, waits for them, and re-layouts, combine_parts(): accum_first.reshape(split_shape) * factor_first[..., None]  15.5 us
    mul x3, local copies, waits for them, and re-layouts, combine_parts(): accum_second.reshape(split_shape) * factor_second[..., None]  15.4 us
    dot_general x6, matrix products, attend_part(): lax.dot_general(query_rows[:, :, lower:upper], key_rows[:, :, lower:upper...  14.7 us
    dot_general x6, matrix products, attend_part(): lax.dot_general(raw_weights.astype(jnp.bfloat16), value_rows[:, :, lower:...  12.4 us
    all_to_all x1, starting transfers between devices, local(): lax.all_to_all(outbound, 'rep', split_axis=0, concat_axis=0, tiled=True)  10.7 us
  transfers between devices with their start and end apart: 7, of which 4 were waited for; matrix products, arithmetic and copies ran while one was open for 20% of the time, Pallas kernels for 0%

commit v1 on v0

v1 whole, which is shorter than its diff:
```python
import math

import jax
import jax.numpy as jnp
from jax import lax
from jax.sharding import PartitionSpec as P

HD = 128
TREE = 48
PCAP = 152


NEG_FILL = -1e30


def swapped(value, axis, apart):
    mask = 2**apart
    pairs = [(source, source ^ mask) for source in range(lax.axis_size(axis))]
    return lax.ppermute(value, axis, pairs)


def split_heads(rows):
    return rows.reshape(rows.shape[:-1] + (rows.shape[-1] // HD, HD))


def prompt_attend(query_rows, key_rows, value_rows, seen):
    q = split_heads(query_rows)
    k = split_heads(key_rows)
    v = split_heads(value_rows)
    scores = jnp.einsum("qhd,khd->hqk", q, k, preferred_element_type=jnp.float32) * (
        1.0 / math.sqrt(HD)
    )
    scores = jnp.where(seen[None, None, :], scores, NEG_FILL)
    peaks = jnp.max(scores, axis=2, keepdims=True)
    raw = jnp.where(seen[None, None, :], jnp.exp(scores - peaks), 0.0)
    totals = jnp.sum(raw, axis=2)
    accum = jnp.einsum(
        "hqk,khd->qhd", raw.astype(jnp.bfloat16), v, preferred_element_type=jnp.float32
    )
    normed = accum / jnp.transpose(totals)[:, :, None]
    lse = jnp.transpose(peaks[:, :, 0] + jnp.log(totals))
    return normed.reshape(query_rows.shape).astype(jnp.bfloat16), lse


def tree_attend(queries, keys, values, seen):
    q = split_heads(queries)
    k = split_heads(keys)
    v = split_heads(values)
    scores = jnp.einsum("rthd,rshd->rhts", q, k, preferred_element_type=jnp.float32) * (
        1.0 / math.sqrt(HD)
    )
    scores = jnp.where(seen[:, None], scores, NEG_FILL)
    peaks = jnp.max(scores, axis=3, keepdims=True)
    raw = jnp.where(seen[:, None], jnp.exp(scores - peaks), 0.0)
    totals = jnp.sum(raw, axis=3)
    accum = jnp.einsum(
        "rhts,rshd->rthd", raw.astype(jnp.bfloat16), v, preferred_element_type=jnp.float32
    )
    return jnp.swapaxes(peaks[..., 0], 1, 2), jnp.swapaxes(totals, 1, 2), accum


def local(
    queries,
    tree_cache,
    tree_mask,
    dest_group,
    accepted_path,
    prompt_cache,
    first_len,
    spill_cache,
    spill_len,
    out_weight,
):
    req_here = queries.shape[0]
    local_cols = queries.shape[2]
    heads_here = local_cols // HD
    groups = lax.axis_size("rep")
    per_group = max(2, (req_here + groups - 1) // groups)
    n_slots = groups * per_group
    positions = jnp.arange(PCAP, dtype=jnp.int32)
    live_flag = (positions < spill_len[0]).astype(jnp.bfloat16)
    partner_cache, partner_flag = swapped((spill_cache, live_flag), "rep", 0)

    target = dest_group[:, 0]
    same_target = target[:, None] == target[None, :]
    earlier = jnp.arange(req_here)[None, :] < jnp.arange(req_here)[:, None]
    rank_index = jnp.sum(jnp.logical_and(same_target, earlier), axis=1)
    slot_index = target * per_group + rank_index
    selector = (jnp.arange(n_slots, dtype=jnp.int32)[:, None] == slot_index[None, :]).astype(
        jnp.bfloat16
    )
    outbound = jnp.einsum(
        "sr,rtc->stc", selector, queries, preferred_element_type=jnp.float32
    ).astype(jnp.bfloat16)
    outbound = outbound.reshape(groups, per_group, TREE, local_cols)
    inbound = lax.all_to_all(outbound, "rep", split_axis=0, concat_axis=0, tiled=True)
    routed_rows = inbound.reshape(n_slots * TREE, local_cols)

    key_rows = jnp.concatenate([prompt_cache[0, 0], partner_cache[0, 0]], axis=0)
    value_rows = jnp.concatenate([prompt_cache[0, 1], partner_cache[0, 1]], axis=0)
    seen = jnp.concatenate([positions < first_len[0], partner_flag > 0.5], axis=0)
    normed, lse = prompt_attend(routed_rows, key_rows, value_rows, seen)

    back_out = lax.all_to_all(
        normed.reshape(groups, per_group, TREE, local_cols),
        "rep",
        split_axis=0,
        concat_axis=0,
        tiled=True,
    ).reshape(n_slots, TREE, local_cols)
    back_lse = lax.all_to_all(
        lse.reshape(groups, per_group, TREE, heads_here),
        "rep",
        split_axis=0,
        concat_axis=0,
        tiled=True,
    ).reshape(n_slots, TREE, heads_here)
    remote_out = split_heads(jnp.take(back_out, slot_index, axis=0)).astype(jnp.float32)
    remote_lse = jnp.take(back_lse, slot_index, axis=0)

    tree_max, tree_total, tree_accum = tree_attend(
        queries, tree_cache[:, 0], tree_cache[:, 1], tree_mask == 1
    )
    peaks = jnp.maximum(remote_lse, tree_max)
    factor_remote = jnp.exp(remote_lse - peaks)
    factor_tree = jnp.exp(tree_max - peaks)
    totals = factor_remote + tree_total * factor_tree
    accum = remote_out * factor_remote[..., None] + tree_accum * factor_tree[..., None]
    attn = (accum / totals[..., None]).reshape(req_here * TREE, local_cols).astype(jnp.bfloat16)
    summed = jnp.dot(
        lax.all_gather(attn, "tp", axis=1, tiled=True),
        out_weight,
        preferred_element_type=jnp.float32,
    )
    projected = summed.astype(jnp.bfloat16).reshape(req_here, TREE, out_weight.shape[1])
    accepted_cache = jnp.take_along_axis(tree_cache, accepted_path[:, None, :, None], axis=2)
    return (projected, accepted_cache)


def solution(mesh):
    return jax.shard_map(
        local,
        mesh=mesh,
        in_specs=(
            P("rep", None, "tp"),
            P("rep", None, None, "tp"),
            P("rep", None, None),
            P("rep", None),
            P("rep", None),
            P("rep", None, None, "tp"),
            P("rep"),
            P("rep", None, None, "tp"),
            P("rep"),
            P(None, "tp"),
        ),
        out_specs=(P("rep", None, "tp"), P("rep", None, None, "tp")),
        check_vma=False,
    )
```

time: 321 us -> 222 us (0.69)
  local copies, waits for them, and re-layouts: 63.3 us -> 28.8 us
  waiting for transfers between devices: 141 us -> 113 us
  matrix products: 33.4 us -> 18.6 us
  other arithmetic: 22.8 us -> 10.1 us
  starting transfers between devices: 42.5 us -> 34.5 us
    mul x6 -> x0, local copies, waits for them, and re-layouts: 30.8 us -> none  [the longest x3 15.5 us: combine_parts(): accum_first.reshape(split_shape) * factor_first[..., None]]
    all_to_all x3 -> x2, waiting for transfers between devices: 53.1 us -> 26.3 us  [the longest x1 26.3 us: local(): lax.all_to_all(normed.reshape(groups, per_group, TREE, local_cols), 'rep'...]
    dot_general x12 -> x4, matrix products: 27.1 us -> 12.3 us  [the longest x1 6.44 us: prompt_attend(): jnp.einsum('hqk,khd->qhd', raw.astype(jnp.bfloat16), v, preferred_element...]
    all_to_all x3 -> x2, starting transfers between devices: 26.3 us -> 18.4 us  [the longest x1 9.33 us: local(): lax.all_to_all(normed.reshape(groups, per_group, TREE, local_cols), 'rep'...]
    add x3, other arithmetic: 8.24 us -> 1.49 us  [the longest x1 0.81 us: local(): totals = factor_remote + tree_total * factor_tree]
    exp x4 -> x0, local copies, waits for them, and re-layouts: 5.17 us -> none  [the longest x2 2.6 us: combine_parts(): factor_second = jnp.exp(max_second - peaks)]
    reduce_sum x3 -> x2, other arithmetic: 7.66 us -> 2.8 us  [the longest x1 2.01 us: prompt_attend(): totals = jnp.sum(raw, axis=2)]
    convert_element_type x4 -> x3, local copies, waits for them, and re-layouts: 8.03 us -> 9 us  [the longest x2 8.75 us: prompt_attend(): return (normed.reshape(query_rows.shape).astype(jnp.bfloat16), lse)]
  transfers between devices with their start and end apart: 7 -> 6, of which waited for: 4 -> 4; matrix products, arithmetic and copies ran while one was open for 20% -> 13% of each run, Pallas kernels for 0% -> 0%
where the time goes in v1:
time: 222 us; the launch traced here: 221 us
  waiting for transfers between devices  113 us (51%)
  starting transfers between devices  34.5 us (16%)
  local copies, waits for them, and re-layouts  28.8 us (13%)
  matrix products  18.6 us (8%)
  between operations  15.6 us (7%)
  other arithmetic  10.1 us (5%)
    all_gather x1, waiting for transfers between devices, local(): lax.all_gather(attn, 'tp', axis=1, tiled=True)  55.3 us
    ppermute x2, waiting for transfers between devices, swapped(): return lax.ppermute(value, axis, pairs)  31.6 us
    all_to_all x1, waiting for transfers between devices, local(): lax.all_to_all(normed.reshape(groups, per_group, TREE, local_cols), 'rep'...  26.3 us
    all_to_all x1, starting transfers between devices, local(): lax.all_to_all(outbound, 'rep', split_axis=0, concat_axis=0, tiled=True)  10.6 us
    all_to_all x1, starting transfers between devices, local(): lax.all_to_all(normed.reshape(groups, per_group, TREE, local_cols), 'rep'...  9.33 us
    all_to_all x1, starting transfers between devices, local(): lax.all_to_all(lse.reshape(groups, per_group, TREE, heads_here), 'rep', s...  9.06 us
    convert_element_type x2, local copies, waits for them, and re-layouts, prompt_attend(): return (normed.reshape(query_rows.shape).astype(jnp.bfloat16), lse)  8.75 us
    dot_general x1, matrix products, prompt_attend(): jnp.einsum('hqk,khd->qhd', raw.astype(jnp.bfloat16), v, preferred_element...  6.44 us
  transfers between devices with their start and end apart: 6, of which 4 were waited for; matrix products, arithmetic and copies ran while one was open for 13% of the time, Pallas kernels for 0%

profile of v1, /device:TPU:1, one launch (start us, length us, event | category | flops | bytes accessed | tf_op | source)
XLA Modules:
  0.0 220.9 jit_solution(4979695363435607490)
XLA Ops:
  8.9 1.7 convolution_convert_fusion
  10.5 2.0 copy.57
  12.6 10.6 %all-to-all-start = ((bf16[32,2,48,256]{3,2,1,0:T(8,128)(2,1)}), bf16[32,2,48,256]{3,2,1,0:T(8,128)(2,1)}, u32[]{:S(2)}, u32[]{:S(2)}) async-start(bf16[32,2,48,256]{3,2,1,0:T(8,128)(2,1)} %bitcast.101), calls=%async_computation | async-start | bytes 3145728 | tf_op jit(solution)/shard_map/all_to_all | solution.py:96
  23.8 3.1 %collective-permute-start.1 = (bf16[152]{0:T(256)(128)(2,1)S(1)}, bf16[152]{0:T(256)(128)(2,1)S(1)}, u32[]{:S(2)}, u32[]{:S(2)}) collective-permute-start(bf16[152]{0:T(256)(128)(2,1)S(1)} %compare_convert_fusion), channel_id=1, source_target_pairs={{0,16},{16,0},{32,48},{48,32},{64,80},{80,64},{96,112},{112,96},{1... | collective-permute-start | bytes 920 | tf_op jit(solution)/shard_map/ppermute | solution.py:19
  26.9 2.2 %collective-permute-start = (bf16[1,2,152,256]{3,2,1,0:T(8,128)(2,1)S(1)}, bf16[1,2,152,256]{3,2,1,0:T(8,128)(2,1)S(1)}, u32[]{:S(2)}, u32[]{:S(2)}) collective-permute-start(bf16[1,2,152,256]{3,2,1,0:T(8,128)(2,1)S(1)} %copy-done.7), channel_id=1, source_target_pairs={{0,16},{16,0},{32,48},{48,32},{64,80},{80,64},{96,112},{112,96},{1... | collective-permute-start | bytes 466952 | tf_op jit(solution)/shard_map/ppermute | solution.py:19
  29.9 26.4 %collective-permute-done.1 = bf16[152]{0:T(256)(128)(2,1)S(1)} collective-permute-done((bf16[152]{0:T(256)(128)(2,1)S(1)}, bf16[152]{0:T(256)(128)(2,1)S(1)}, u32[]{:S(2)}, u32[]{:S(2)}) %collective-permute-start.1) | collective-permute-done | bytes 336 | tf_op jit(solution)/shard_map/ppermute | solution.py:19
  56.4 5.2 %collective-permute-done = bf16[1,2,152,256]{3,2,1,0:T(8,128)(2,1)S(1)} collective-permute-done((bf16[1,2,152,256]{3,2,1,0:T(8,128)(2,1)S(1)}, bf16[1,2,152,256]{3,2,1,0:T(8,128)(2,1)S(1)}, u32[]{:S(2)}, u32[]{:S(2)}) %collective-permute-start) | collective-permute-done | bytes 155680 | tf_op jit(solution)/shard_map/ppermute | solution.py:19
  61.7 3.5 %reshape_reshape.3 = bf16[3072,2,128]{2,1,0:T(2,128)(2,1)} reshape(bf16[32,2,48,256]{3,2,1,0:T(8,128)(2,1)} %all-to-all-done) | data formatting | bytes 3145728 | tf_op jit(solution)/shard_map/reshape;reshape | solution.py:23
  65.3 2.7 %fusion = (f32[2,3072]{1,0:T(2,128)S(1)}, f32[2,3072,304]{1,2,0:T(8,128)S(1)}) fusion(pred[304]{0:T(512)(128)(4,1)S(1)} %pad_add_fusion, bf16[152,2,128]{2,0,1:T(8,128)(2,1)S(1)} %copy.42, bf16[152,2,128]{2,0,1:T(8,128)(2,1)S(1)} %copy.41, bf16[3072,2,128]{2,1,0:T(2,128)(2,1)} %reshape_reshape.3), kind=kOutput, calls=%fused_computation.5 | convolution fusion | flops 484059136 | bytes 9224496 | tf_op jit(solution)/shard_map/qhd,khd->hqk/dot_general | solution.py:30
  67.9 3.0 %copy-done.1 = f32[2,3072,304]{1,2,0:T(8,128)} copy-done((f32[2,3072,304]{1,2,0:T(8,128)}, f32[2,3072,304]{1,2,0:T(8,128)S(1)}, u32[]{:S(2)}) %copy-start.1) | copy-done | bytes 7471128
  70.9 2.0 fusion.1
  73.9 9.1 %all-to-all-start.2 = ((f32[32,1,192]{2,1,0:T(1,128)}), f32[32,1,192]{2,1,0:T(1,128)S(1)}, u32[]{:S(2)}, u32[]{:S(2)}) async-start(f32[32,1,192]{2,1,0:T(1,128)} %reshape.118), calls=%async_computation.2 | async-start | bytes 65536 | tf_op jit(solution)/shard_map/all_to_all | solution.py:111
  83.0 6.4 %divide_convert_fusion = bf16[3072,2,128]{0,2,1:T(8,128)(2,1)} fusion(f32[2,3072,304]{1,2,0:T(8,128)} %copy-done.1, f32[2,3072]{1,0:T(2,128)S(1)} %get-tuple-element.17, pred[304]{0:T(512)(128)(4,1)S(1)} %pad_add_fusion, f32[3072,2]{0,1:T(2,128)S(1)} %bitcast.106, bf16[152,2,128]{2,0,1:T(8,128)(2,1)S(1)} %copy.38, bf16[152,2,128]{2,0,1:T(8,128)(2,1)S(1)} %copy.37), kind=kOutput, calls=%fused_computation.14 | convolution fusion | flops 489373696 | bytes 9249072 | tf_op jit(solution)/shard_map/hqk,khd->qhd/dot_general | solution.py:37
  89.4 5.0 %copy.44 = bf16[3072,2,128]{2,1,0:T(2,128)(2,1)} copy(bf16[3072,2,128]{0,2,1:T(8,128)(2,1)} %divide_convert_fusion) | data formatting | bytes 3145728 | tf_op jit(solution)/shard_map/convert_element_type | solution.py:42
  94.4 3.8 %convert_element_type.40 = bf16[32,2,48,256]{3,2,1,0:T(8,128)(2,1)} reshape(bf16[3072,2,128]{2,1,0:T(2,128)(2,1)} %copy.44) | data formatting | bytes 3145728 | tf_op jit(solution)/shard_map/convert_element_type | solution.py:42
  98.2 9.3 %all-to-all-start.1 = ((bf16[32,2,48,256]{3,2,1,0:T(8,128)(2,1)}), bf16[32,2,48,256]{3,2,1,0:T(8,128)(2,1)}, u32[]{:S(2)}, u32[]{:S(2)}) async-start(bf16[32,2,48,256]{3,2,1,0:T(8,128)(2,1)} %convert_element_type.40), calls=%async_computation.1 | async-start | bytes 3145728 | tf_op jit(solution)/shard_map/all_to_all | solution.py:104
  110.9 1.4 fusion.54
  113.6 2.0 reduce
  118.0 26.3 %all-to-all-done.1 = bf16[32,2,48,256]{3,2,1,0:T(8,128)(2,1)} async-done(((bf16[32,2,48,256]{3,2,1,0:T(8,128)(2,1)}), bf16[32,2,48,256]{3,2,1,0:T(8,128)(2,1)}, u32[]{:S(2)}, u32[]{:S(2)}) %all-to-all-start.1) | async-done | bytes 1572896 | tf_op jit(solution)/shard_map/all_to_all | solution.py:104
  144.4 2.8 %gather_fusion = bf16[13,48,256]{2,1,0:T(8,128)(2,1)} fusion(bf16[64,48,256]{2,1,0:T(8,128)(2,1)} %bitcast.9, s32[1024]{0:T(1024)} %pad_clamp_fusion), kind=kCustom, calls=%fused_computation | custom fusion | bytes 639028 | tf_op jit(solution)/shard_map/jit(_take)/gather | solution.py:118
  147.2 1.8 fusion.17
  150.9 1.6 gather_fusion.2
  154.1 55.3 %all-gather.2.cloned.1.call-done = bf16[624,4096]{1,0:T(8,128)(2,1)} async-done(((bf16[624,256]{1,0:T(8,128)(2,1)}), bf16[624,4096]{1,0:T(8,128)(2,1)}) %all-gather.2.cloned.1.call-update) | async-done | bytes 5111824 | tf_op jit(solution)/shard_map/all_gather | solution.py:131
  209.4 4.7 %convolution_convert_fusion.1 = bf16[624,256]{1,0:T(8,128)(2,1)} fusion(bf16[624,4096]{1,0:T(8,128)(2,1)} %all-gather.2.cloned.1.call-done, bf16[4096,256]{1,0:T(8,128)(2,1)S(1)} %copy-done), kind=kOutput, calls=%fused_computation.25 | convolution fusion | flops 1308782592 | bytes 7528448 | tf_op jit(solution)/shard_map/dot_general | solution.py:130
  (60 shorter events, 13.4 us)
Async XLA Ops:
  7.2 202.3 %copy-start = (bf16[4096,256]{1,0:T(8,128)(2,1)S(1)}, bf16[4096,256]{1,0:T(8,128)(2,1)}, u32[]{:S(2)}) copy-start(bf16[4096,256]{1,0:T(8,128)(2,1)} %param.19) | copy-start | bytes 6291460
  7.2 19.8 %copy-start.7 = (bf16[1,2,152,256]{3,2,1,0:T(8,128)(2,1)S(1)}, bf16[1,2,152,256]{3,2,1,0:T(8,128)(2,1)}, u32[]{:S(2)}) copy-start(bf16[1,2,152,256]{3,2,1,0:T(8,128)(2,1)} %param.17) | copy-start | bytes 466948
  7.2 22.6 %copy-start.4 = (bf16[1,2,152,256]{3,2,1,0:T(8,128)(2,1)S(1)}, bf16[1,2,152,256]{3,2,1,0:T(8,128)(2,1)}, u32[]{:S(2)}) copy-start(bf16[1,2,152,256]{3,2,1,0:T(8,128)(2,1)} %param.15) | copy-start | bytes 466948
  12.6 49.2 %all-to-all-start = ((bf16[32,2,48,256]{3,2,1,0:T(8,128)(2,1)}), bf16[32,2,48,256]{3,2,1,0:T(8,128)(2,1)}, u32[]{:S(2)}, u32[]{:S(2)}) async-start(bf16[32,2,48,256]{3,2,1,0:T(8,128)(2,1)} %bitcast.101), calls=%async_computation | async-start | bytes 3145728 | tf_op jit(solution)/shard_map/all_to_all | solution.py:96
  23.8 32.5 %collective-permute-start.1 = (bf16[152]{0:T(256)(128)(2,1)S(1)}, bf16[152]{0:T(256)(128)(2,1)S(1)}, u32[]{:S(2)}, u32[]{:S(2)}) collective-permute-start(bf16[152]{0:T(256)(128)(2,1)S(1)} %compare_convert_fusion), channel_id=1, source_target_pairs={{0,16},{16,0},{32,48},{48,32},{64,80},{80,64},{96,112},{112,96},{1... | collective-permute-start | bytes 920 | tf_op jit(solution)/shard_map/ppermute | solution.py:19
  26.9 34.7 %collective-permute-start = (bf16[1,2,152,256]{3,2,1,0:T(8,128)(2,1)S(1)}, bf16[1,2,152,256]{3,2,1,0:T(8,128)(2,1)S(1)}, u32[]{:S(2)}, u32[]{:S(2)}) collective-permute-start(bf16[1,2,152,256]{3,2,1,0:T(8,128)(2,1)S(1)} %copy-done.7), channel_id=1, source_target_pairs={{0,16},{16,0},{32,48},{48,32},{64,80},{80,64},{96,112},{112,96},{1... | collective-permute-start | bytes 466952 | tf_op jit(solution)/shard_map/ppermute | solution.py:19
  67.9 3.0 %copy-start.1 = (f32[2,3072,304]{1,2,0:T(8,128)}, f32[2,3072,304]{1,2,0:T(8,128)S(1)}, u32[]{:S(2)}) copy-start(f32[2,3072,304]{1,2,0:T(8,128)S(1)} %get-tuple-element.18) | copy-start | bytes 22413316
  73.9 24.3 %all-to-all-start.2 = ((f32[32,1,192]{2,1,0:T(1,128)}), f32[32,1,192]{2,1,0:T(1,128)S(1)}, u32[]{:S(2)}, u32[]{:S(2)}) async-start(f32[32,1,192]{2,1,0:T(1,128)} %reshape.118), calls=%async_computation.2 | async-start | bytes 65536 | tf_op jit(solution)/shard_map/all_to_all | solution.py:111
  89.4 18.3 %copy-start.3 = (s32[13,48,48]{2,1,0:T(8,128)S(1)}, s32[13,48,48]{2,1,0:T(8,128)}, u32[]{:S(2)}) copy-start(s32[13,48,48]{2,1,0:T(8,128)} %param.12) | copy-start | bytes 359428
  89.4 18.6 %copy-start.2 = (bf16[13,2,48,256]{3,2,1,0:T(8,128)(2,1)S(1)}, bf16[13,2,48,256]{3,2,1,0:T(8,128)(2,1)}, u32[]{:S(2)}) copy-start(bf16[13,2,48,256]{3,2,1,0:T(8,128)(2,1)} %param.11) | copy-start | bytes 1916932
  94.4 15.3 %copy-start.6 = (s32[13,1]{0,1:T(1,128)S(1)}, s32[13,1]{0,1:T(1,128)}, u32[]{:S(2)}) copy-start(s32[13,1]{0,1:T(1,128)} %param.13) | copy-start | bytes 160
  98.2 9.3 %copy-start.5 = (f32[32,1,192]{2,1,0:T(1,128)}, f32[32,1,192]{2,1,0:T(1,128)S(1)}, u32[]{:S(2)}) copy-start(f32[32,1,192]{2,1,0:T(1,128)S(1)} %all-to-all-done.2) | copy-start | bytes 73732
  98.2 46.1 %all-to-all-start.1 = ((bf16[32,2,48,256]{3,2,1,0:T(8,128)(2,1)}), bf16[32,2,48,256]{3,2,1,0:T(8,128)(2,1)}, u32[]{:S(2)}, u32[]{:S(2)}) async-start(bf16[32,2,48,256]{3,2,1,0:T(8,128)(2,1)} %convert_element_type.40), calls=%async_computation.1 | async-start | bytes 3145728 | tf_op jit(solution)/shard_map/all_to_all | solution.py:104
  107.6 101.9 %all-gather.2.cloned.1.call-start = ((), (), s32[]{:S(2)}) async-start(), calls=%async_computation.3 | async-start | bytes 5431296 | tf_op jit(solution)/shard_map/all_gather | solution.py:131
Sparse Core Ops, SparseCore 0:
  150.2 59.2 all-gather.1

commit v2 on v1

--- a/solution.py
+++ b/solution.py
@@ -3,7 +3,11 @@
 import jax
 import jax.numpy as jnp
 from jax import lax
+from jax.experimental import pallas as pl
+from jax.experimental.pallas import tpu as pltpu
 from jax.sharding import PartitionSpec as P
+
+MESH = pl.DeviceIdType.MESH
 
 HD = 128
 TREE = 48
@@ -17,6 +21,57 @@
     mask = 2**apart
     pairs = [(source, source ^ mask) for source in range(lax.axis_size(axis))]
     return lax.ppermute(value, axis, pairs)
+
+
+def exchange_kernel(n, count, *refs):
+    sources = refs[:count]
+    targets = refs[count : 2 * count]
+    send_sem, recv_sem, local_sem = refs[2 * count :]
+    me = lax.axis_index("rep")
+    barrier = pltpu.get_barrier_semaphore()
+    for offset in range(1, n):
+        pl.semaphore_signal(
+            barrier, inc=1, device_id={"rep": lax.rem(me + offset, n)}, device_id_type=MESH
+        )
+    pl.semaphore_wait(barrier, n - 1)
+    copies = []
+    for index in range(count):
+        local = pltpu.make_async_copy(
+            sources[index].at[me], targets[index].at[me], local_sem.at[index]
+        )
+        local.start()
+        copies.append(local)
+        for offset in range(1, n):
+            peer = lax.rem(me + offset, n)
+            remote = pltpu.make_async_remote_copy(
+                src_ref=sources[index].at[peer],
+                dst_ref=targets[index].at[me],
+                send_sem=send_sem.at[index, offset],
+                recv_sem=recv_sem.at[index, offset],
+                device_id={"rep": peer},
+                device_id_type=MESH,
+            )
+            remote.start()
+            copies.append(remote)
+    for copy in copies:
+        copy.wait()
+
+
+def exchange(arrays, tag):
+    n = lax.axis_size("rep")
+    count = len(arrays)
+    return pl.pallas_call(
+        lambda *refs: exchange_kernel(n, count, *refs),
+        out_shape=[jax.ShapeDtypeStruct(a.shape, a.dtype) for a in arrays],
+        in_specs=[pl.BlockSpec(memory_space=pl.ANY)] * count,
+        out_specs=[pl.BlockSpec(memory_space=pl.ANY)] * count,
+        scratch_shapes=[
+            pltpu.SemaphoreType.DMA((count, n)),
+            pltpu.SemaphoreType.DMA((count, n)),
+            pltpu.SemaphoreType.DMA((count,)),
+        ],
+        compiler_params=pltpu.CompilerParams(collective_id=tag, has_side_effects=True),
+    )(*arrays)
 
 
 def split_heads(rows):
@@ -93,7 +148,7 @@
         "sr,rtc->stc", selector, queries, preferred_element_type=jnp.float32
     ).astype(jnp.bfloat16)
     outbound = outbound.reshape(groups, per_group, TREE, local_cols)
-    inbound = lax.all_to_all(outbound, "rep", split_axis=0, concat_axis=0, tiled=True)
+    (inbound,) = exchange([outbound], 0)
     routed_rows = inbound.reshape(n_slots * TREE, local_cols)
 
     key_rows = jnp.concatenate([prompt_cache[0, 0], partner_cache[0, 0]], axis=0)
@@ -101,20 +156,15 @@
     seen = jnp.concatenate([positions < first_len[0], partner_flag > 0.5], axis=0)
     normed, lse = prompt_attend(routed_rows, key_rows, value_rows, seen)
 
-    back_out = lax.all_to_all(
-        normed.reshape(groups, per_group, TREE, local_cols),
-        "rep",
-        split_axis=0,
-        concat_axis=0,
-        tiled=True,
-    ).reshape(n_slots, TREE, local_cols)
-    back_lse = lax.all_to_all(
-        lse.reshape(groups, per_group, TREE, heads_here),
-        "rep",
-        split_axis=0,
-        concat_axis=0,
-        tiled=True,
-    ).reshape(n_slots, TREE, heads_here)
+    back_out, back_lse = exchange(
+        [
+            normed.reshape(groups, per_group, TREE, local_cols),
+            lse.reshape(groups, per_group, TREE, heads_here),
+        ],
+        1,
+    )
+    back_out = back_out.reshape(n_slots, TREE, local_cols)
+    back_lse = back_lse.reshape(n_slots, TREE, heads_here)
     remote_out = split_heads(jnp.take(back_out, slot_index, axis=0)).astype(jnp.float32)
     remote_lse = jnp.take(back_lse, slot_index, axis=0)
 

time: 222 us -> 255 us (1.15)
  Pallas kernels: 0 us -> 118 us
  waiting for transfers between devices: 113 us -> 58 us
  starting transfers between devices: 34.5 us -> 6 us
  matrix products: 18.6 us -> 15.4 us
    pallas_call x0 -> x2, Pallas kernels: none -> 118 us  [exchange(): pl.pallas_call(lambda *refs: exchange_kernel(n, count, *refs), out_shape=...]
    ppermute x2, waiting for transfers between devices: 31.6 us -> 0.01 us  [swapped(): return lax.ppermute(value, axis, pairs)]
    all_to_all x3 -> x0, starting transfers between devices: 29 us -> none  [the longest x1 10.6 us: local(): lax.all_to_all(outbound, 'rep', split_axis=0, concat_axis=0, tiled=True)]
    all_to_all x3 -> x0, waiting for transfers between devices: 26.3 us -> none  [the longest x1 26.3 us: local(): lax.all_to_all(normed.reshape(groups, per_group, TREE, local_cols), 'rep'...]
    unnamed x20 -> x14, local copies, waits for them, and re-layouts: 6.05 us -> 2.29 us
    dot_general x1, matrix products: 6.44 us -> 3.22 us  [prompt_attend(): jnp.einsum('hqk,khd->qhd', raw.astype(jnp.bfloat16), v, preferred_element...]
    all_gather x1, waiting for transfers between devices: 55.3 us -> 58 us  [local(): lax.all_gather(attn, 'tp', axis=1, tiled=True)]
  transfers between devices with their start and end apart: 6 -> 3, of which waited for: 4 -> 1; matrix products, arithmetic and copies ran while one was open for 13% -> 9% of each run, Pallas kernels for 0% -> 17%
where the time goes in v2:
time: 255 us; the launch traced here: 254 us
  Pallas kernels  118 us (46%)
  waiting for transfers between devices  58 us (23%)
  local copies, waits for them, and re-layouts  30.6 us (12%)
  between operations  15.7 us (6%)
  matrix products  15.4 us (6%)
  other arithmetic  10.4 us (4%)
  starting transfers between devices  6 us (2%)
    pallas_call x2, Pallas kernels, exchange(): pl.pallas_call(lambda *refs: exchange_kernel(n, count, *refs), out_shape=...  118 us
    all_gather x1, waiting for transfers between devices, local(): lax.all_gather(attn, 'tp', axis=1, tiled=True)  58 us
    convert_element_type x2, local copies, waits for them, and re-layouts, prompt_attend(): return (normed.reshape(query_rows.shape).astype(jnp.bfloat16), lse)  8.73 us
    ppermute x2, starting transfers between devices, swapped(): return lax.ppermute(value, axis, pairs)  5.96 us
    another operation x3, local copies, waits for them, and re-layouts, split_heads(): return rows.reshape(rows.shape[:-1] + (rows.shape[-1] // HD, HD))  5.29 us
  transfers between devices with their start and end apart: 3, of which 1 were waited for; matrix products, arithmetic and copies ran while one was open for 9% of the time, Pallas kernels for 17%

profile of v2, /device:TPU:1, one launch (start us, length us, event | category | flops | bytes accessed | tf_op | source)
XLA Modules:
  0.0 254.5 jit_solution(14175162215492158489)
XLA Ops:
  8.0 4.0 %collective-permute-start.1 = (bf16[152]{0:T(256)(128)(2,1)S(1)}, bf16[152]{0:T(256)(128)(2,1)}, u32[]{:S(2)}, u32[]{:S(2)}) collective-permute-start(bf16[152]{0:T(256)(128)(2,1)S(1)} %compare_convert_fusion), channel_id=1, source_target_pairs={{0,16},{16,0},{32,48},{48,32},{64,80},{80,64},{96,112},{112,96},{1... | collective-permute-start | bytes 920 | tf_op jit(solution)/shard_map/ppermute | solution.py:23
  12.1 1.9 collective-permute-start
  14.0 0.9 convert_reduce_fusion
  15.6 1.2 and_bitcast_fusion
  18.0 1.7 convolution_convert_fusion
  19.7 2.1 copy.93
  21.7 43.7 %shard_map.113 = bf16[32,2,48,256]{3,2,1,0:T(8,128)(2,1)} custom-call(bf16[32,2,48,256]{3,2,1,0:T(8,128)(2,1)} %bitcast.97), custom_call_target="tpu_custom_call" | custom-call | tf_op jit(solution)/shard_map/pallas_call | solution.py:63
  65.5 3.7 %reshape_reshape.3 = bf16[3072,2,128]{2,1,0:T(2,128)(2,1)} reshape(bf16[32,2,48,256]{3,2,1,0:T(8,128)(2,1)} %shard_map.113) | data formatting | bytes 3145728 | tf_op jit(solution)/shard_map/reshape;reshape | solution.py:78
  71.5 1.4 fusion.54
  74.6 0.9 copy.94
  77.7 0.9 fusion.53
  78.7 2.7 %fusion = (f32[2,3072]{1,0:T(2,128)S(1)}, f32[2,3072,304]{1,2,0:T(8,128)S(1)}) fusion(pred[304]{0:T(512)(128)(4,1)S(1)} %pad_add_fusion, bf16[152,2,128]{2,0,1:T(8,128)(2,1)S(1)} %copy.95, bf16[152,2,128]{2,0,1:T(8,128)(2,1)S(1)} %copy.94, bf16[3072,2,128]{2,1,0:T(2,128)(2,1)} %reshape_reshape.3), kind=kOutput, calls=%fused_computation.5 | convolution fusion | flops 484059136 | bytes 9224496 | tf_op jit(solution)/shard_map/qhd,khd->hqk/dot_general | solution.py:85
  81.4 2.0 fusion.1
  83.4 3.2 %divide_convert_fusion = bf16[3072,2,128]{0,2,1:T(8,128)(2,1)} fusion(f32[2,3072,304]{1,2,0:T(8,128)S(1)} %get-tuple-element.26, f32[2,3072]{1,0:T(2,128)S(1)} %get-tuple-element.25, pred[304]{0:T(512)(128)(4,1)S(1)} %pad_add_fusion, f32[3072,2]{0,1:T(2,128)S(1)} %bitcast.101, bf16[152,2,128]{2,0,1:T(8,128)(2,1)S(1)} %copy.91, ...), kind=kOutput, calls=%fused_computation.14 | convolution fusion | flops 489373696 | bytes 9249072 | tf_op jit(solution)/shard_map/hqk,khd->qhd/dot_general | solution.py:92
  86.7 4.9 %copy.97 = bf16[3072,2,128]{2,1,0:T(2,128)(2,1)} copy(bf16[3072,2,128]{0,2,1:T(8,128)(2,1)} %divide_convert_fusion) | data formatting | bytes 3145728 | tf_op jit(solution)/shard_map/convert_element_type | solution.py:97
  91.6 3.8 %convert_element_type.40.refs_0_ = bf16[32,2,48,256]{3,2,1,0:T(8,128)(2,1)} reshape(bf16[3072,2,128]{2,1,0:T(2,128)(2,1)} %copy.97) | data formatting | bytes 3145728 | tf_op jit(solution)/shard_map/convert_element_type | solution.py:97
  95.4 1.7 copy.98
  97.1 74.6 %shard_map.114 = (bf16[32,2,48,256]{3,2,1,0:T(8,128)(2,1)}, f32[32,2,48,2]{3,2,1,0:T(8,128)}) custom-call(bf16[32,2,48,256]{3,2,1,0:T(8,128)(2,1)} %convert_element_type.40.refs_0_, f32[32,2,48,2]{3,2,1,0:T(8,128)} %bitcast.96), custom_call_target="tpu_custom_call" | custom-call | tf_op jit(solution)/shard_map/pallas_call | solution.py:63
  171.7 2.0 copy.100
  174.4 2.8 %gather_fusion = bf16[13,48,256]{2,1,0:T(8,128)(2,1)} fusion(bf16[64,48,256]{2,1,0:T(8,128)(2,1)} %bitcast.102, s32[1024]{0:T(1024)} %pad_clamp_fusion), kind=kCustom, calls=%fused_computation | custom fusion | bytes 639028 | tf_op jit(solution)/shard_map/jit(_take)/gather | solution.py:168
  178.1 1.8 fusion.17
  181.8 1.6 gather_fusion.2
  185.0 58.0 %all-gather.2.cloned.1.call-done = bf16[624,4096]{1,0:T(8,128)(2,1)} async-done(((bf16[624,256]{1,0:T(8,128)(2,1)}), bf16[624,4096]{1,0:T(8,128)(2,1)}) %all-gather.2.cloned.1.call-update) | async-done | bytes 5111824 | tf_op jit(solution)/shard_map/all_gather | solution.py:181
  243.0 4.7 %convolution_convert_fusion.1 = bf16[624,256]{1,0:T(8,128)(2,1)} fusion(bf16[624,4096]{1,0:T(8,128)(2,1)} %all-gather.2.cloned.1.call-done, bf16[4096,256]{1,0:T(8,128)(2,1)S(1)} %copy-done), kind=kOutput, calls=%fused_computation.25 | convolution fusion | flops 1308782592 | bytes 7528448 | tf_op jit(solution)/shard_map/dot_general | solution.py:180
  (48 shorter events, 12.5 us)
Async XLA Ops:
  7.2 235.8 %copy-start = (bf16[4096,256]{1,0:T(8,128)(2,1)S(1)}, bf16[4096,256]{1,0:T(8,128)(2,1)}, u32[]{:S(2)}) copy-start(bf16[4096,256]{1,0:T(8,128)(2,1)} %param.19) | copy-start | bytes 6291460
  7.2 235.8 %all-gather.2.cloned.1.call-start = ((), (), s32[]{:S(2)}) async-start(), calls=%async_computation | async-start | bytes 5431296 | tf_op jit(solution)/shard_map/all_gather | solution.py:181
  8.0 68.3 %collective-permute-start.1 = (bf16[152]{0:T(256)(128)(2,1)S(1)}, bf16[152]{0:T(256)(128)(2,1)}, u32[]{:S(2)}, u32[]{:S(2)}) collective-permute-start(bf16[152]{0:T(256)(128)(2,1)S(1)} %compare_convert_fusion), channel_id=1, source_target_pairs={{0,16},{16,0},{32,48},{48,32},{64,80},{80,64},{96,112},{112,96},{1... | collective-permute-start | bytes 920 | tf_op jit(solution)/shard_map/ppermute | solution.py:23
  12.1 65.6 %collective-permute-start = (bf16[1,2,152,256]{3,2,1,0:T(8,128)(2,1)}, bf16[1,2,152,256]{3,2,1,0:T(8,128)(2,1)}, u32[]{:S(2)}, u32[]{:S(2)}) collective-permute-start(bf16[1,2,152,256]{3,2,1,0:T(8,128)(2,1)} %param.17), channel_id=1, source_target_pairs={{0,16},{16,0},{32,48},{48,32},{64,80},{80,64},{96,112},{112,96},{1... | collective-permute-start | bytes 466952 | tf_op jit(solution)/shard_map/ppermute | solution.py:23
  19.6 49.5 %copy-start.5 = (bf16[1,2,152,256]{3,2,1,0:T(8,128)(2,1)S(1)}, bf16[1,2,152,256]{3,2,1,0:T(8,128)(2,1)}, u32[]{:S(2)}) copy-start(bf16[1,2,152,256]{3,2,1,0:T(8,128)(2,1)} %param.15) | copy-start | bytes 466948
  19.6 50.8 %copy-start.4 = (s32[13,48,48]{2,1,0:T(8,128)S(1)}, s32[13,48,48]{2,1,0:T(8,128)}, u32[]{:S(2)}) copy-start(s32[13,48,48]{2,1,0:T(8,128)} %param.12) | copy-start | bytes 359428
  19.7 51.0 %copy-start.1 = (bf16[13,2,48,256]{3,2,1,0:T(8,128)(2,1)S(1)}, bf16[13,2,48,256]{3,2,1,0:T(8,128)(2,1)}, u32[]{:S(2)}) copy-start(bf16[13,2,48,256]{3,2,1,0:T(8,128)(2,1)} %param.11) | copy-start | bytes 1916932
  72.9 0.8 copy-start.2
  91.6 86.5 %copy-start.3 = (f32[13,2,48,48]{2,3,1,0:T(8,128)S(1)}, f32[13,2,48,48]{2,3,1,0:T(8,128)}, u32[]{:S(2)}) copy-start(f32[13,2,48,48]{2,3,1,0:T(8,128)} %copy-done.2) | copy-start | bytes 718852
Sparse Core Ops, SparseCore 0:
  181.1 61.8 all-gather.1

commit v3 on v2

--- a/solution.py
+++ b/solution.py
@@ -156,15 +156,18 @@
     seen = jnp.concatenate([positions < first_len[0], partner_flag > 0.5], axis=0)
     normed, lse = prompt_attend(routed_rows, key_rows, value_rows, seen)
 
+    lse_width = per_group * TREE * heads_here
+    lse_tile = -(-lse_width // 1024) * 1024
+    lse_block = jnp.pad(lse.reshape(groups, lse_width), ((0, 0), (0, lse_tile - lse_width)))
     back_out, back_lse = exchange(
         [
             normed.reshape(groups, per_group, TREE, local_cols),
-            lse.reshape(groups, per_group, TREE, heads_here),
+            lse_block.reshape(groups, lse_tile // 128, 128),
         ],
         1,
     )
     back_out = back_out.reshape(n_slots, TREE, local_cols)
-    back_lse = back_lse.reshape(n_slots, TREE, heads_here)
+    back_lse = back_lse.reshape(groups, lse_tile)[:, :lse_width].reshape(n_slots, TREE, heads_here)
     remote_out = split_heads(jnp.take(back_out, slot_index, axis=0)).astype(jnp.float32)
     remote_lse = jnp.take(back_lse, slot_index, axis=0)
 

time: 255 us -> 231 us (0.906)
  Pallas kernels: 118 us -> 90.4 us
  local copies, waits for them, and re-layouts: 30.6 us -> 39 us
  waiting for transfers between devices: 58 us -> 55.3 us
    pallas_call x2, Pallas kernels: 118 us -> 90.4 us  [exchange(): pl.pallas_call(lambda *refs: exchange_kernel(n, count, *refs), out_shape=...]
    reshape x1 -> x3, local copies, waits for them, and re-layouts: 2 us -> 6.92 us  [the longest x2 4.7 us: local(): back_lse.reshape(groups, lse_tile)[:, :lse_width]]
    all_gather x1, waiting for transfers between devices: 58 us -> 55.2 us  [local(): lax.all_gather(attn, 'tp', axis=1, tiled=True)]
  transfers between devices with their start and end apart: 3 -> 3, of which waited for: 1 -> 1; matrix products, arithmetic and copies ran while one was open for 9% -> 10% of each run, Pallas kernels for 17% -> 19%
where the time goes in v3:
time: 231 us; the launch traced here: 230 us
  Pallas kernels  90.4 us (39%)
  waiting for transfers between devices  55.3 us (24%)
  local copies, waits for them, and re-layouts  39 us (17%)
  between operations  15.7 us (7%)
  matrix products  15.4 us (7%)
  other arithmetic  8.59 us (4%)
  starting transfers between devices  6 us (3%)
    pallas_call x2, Pallas kernels, exchange(): pl.pallas_call(lambda *refs: exchange_kernel(n, count, *refs), out_shape=...  90.4 us
    all_gather x1, waiting for transfers between devices, local(): lax.all_gather(attn, 'tp', axis=1, tiled=True)  55.2 us
    convert_element_type x2, local copies, waits for them, and re-layouts, prompt_attend(): return (normed.reshape(query_rows.shape).astype(jnp.bfloat16), lse)  8.65 us
    ppermute x2, starting transfers between devices, swapped(): return lax.ppermute(value, axis, pairs)  5.96 us
    another operation x3, local copies, waits for them, and re-layouts, split_heads(): return rows.reshape(rows.shape[:-1] + (rows.shape[-1] // HD, HD))  5.11 us
    reshape x2, local copies, waits for them, and re-layouts, local(): back_lse.reshape(groups, lse_tile)[:, :lse_width]  4.7 us
    dot_general x1, matrix products, local(): jnp.dot(lax.all_gather(attn, 'tp', axis=1, tiled=True), out_weight, prefe...  4.66 us
  transfers between devices with their start and end apart: 3, of which 1 were waited for; matrix products, arithmetic and copies ran while one was open for 10% of the time, Pallas kernels for 19%

profile of v3, /device:TPU:1, one launch (start us, length us, event | category | flops | bytes accessed | tf_op | source)
XLA Modules:
  0.0 230.3 jit_solution(14756045115244807474)
XLA Ops:
  8.0 4.0 %collective-permute-start.1 = (bf16[152]{0:T(256)(128)(2,1)S(1)}, bf16[152]{0:T(256)(128)(2,1)S(1)}, u32[]{:S(2)}, u32[]{:S(2)}) collective-permute-start(bf16[152]{0:T(256)(128)(2,1)S(1)} %compare_convert_fusion), channel_id=1, source_target_pairs={{0,16},{16,0},{32,48},{48,32},{64,80},{80,64},{96,112},{112,96},{1... | collective-permute-start | bytes 920 | tf_op jit(solution)/shard_map/ppermute | solution.py:23
  12.1 1.9 collective-permute-start
  15.6 1.2 and_bitcast_fusion
  17.4 1.7 convolution_convert_fusion
  19.1 2.0 copy.66
  21.2 43.7 %shard_map.113 = bf16[32,2,48,256]{3,2,1,0:T(8,128)(2,1)} custom-call(bf16[32,2,48,256]{3,2,1,0:T(8,128)(2,1)} %bitcast.101), custom_call_target="tpu_custom_call" | custom-call | tf_op jit(solution)/shard_map/pallas_call | solution.py:63
  64.9 3.5 %reshape_reshape.3 = bf16[3072,2,128]{2,1,0:T(2,128)(2,1)} reshape(bf16[32,2,48,256]{3,2,1,0:T(8,128)(2,1)} %shard_map.113) | data formatting | bytes 3145728 | tf_op jit(solution)/shard_map/reshape;reshape | solution.py:78
  71.4 1.4 fusion.54
  77.8 0.9 fusion.53
  78.8 2.7 %fusion = (f32[2,3072]{1,0:T(2,128)S(1)}, f32[2,3072,304]{1,2,0:T(8,128)S(1)}) fusion(pred[304]{0:T(512)(128)(4,1)S(1)} %pad_add_fusion, bf16[152,2,128]{2,0,1:T(8,128)(2,1)S(1)} %copy.68, bf16[152,2,128]{2,0,1:T(8,128)(2,1)S(1)} %copy.67, bf16[3072,2,128]{2,1,0:T(2,128)(2,1)} %reshape_reshape.3), kind=kOutput, calls=%fused_computation.5 | convolution fusion | flops 484059136 | bytes 9224496 | tf_op jit(solution)/shard_map/qhd,khd->hqk/dot_general | solution.py:85
  81.5 2.0 fusion.1
  83.6 3.2 %divide_convert_fusion = bf16[3072,2,128]{0,2,1:T(8,128)(2,1)} fusion(f32[2,3072,304]{1,2,0:T(8,128)S(1)} %get-tuple-element.24, f32[2,3072]{1,0:T(2,128)S(1)} %get-tuple-element.23, pred[304]{0:T(512)(128)(4,1)S(1)} %pad_add_fusion, f32[3072,2]{0,1:T(2,128)S(1)} %bitcast.107, bf16[152,2,128]{2,0,1:T(8,128)(2,1)S(1)} %copy.64, ...), kind=kOutput, calls=%fused_computation.14 | convolution fusion | flops 489373696 | bytes 9249072 | tf_op jit(solution)/shard_map/hqk,khd->qhd/dot_general | solution.py:92
  86.8 4.9 %copy.70 = bf16[3072,2,128]{2,1,0:T(2,128)(2,1)} copy(bf16[3072,2,128]{0,2,1:T(8,128)(2,1)} %divide_convert_fusion) | data formatting | bytes 3145728 | tf_op jit(solution)/shard_map/convert_element_type | solution.py:97
  91.7 3.7 %convert_element_type.42.refs_0_ = bf16[32,2,48,256]{3,2,1,0:T(8,128)(2,1)} reshape(bf16[3072,2,128]{2,1,0:T(2,128)(2,1)} %copy.70) | data formatting | bytes 3145728 | tf_op jit(solution)/shard_map/convert_element_type | solution.py:97
  95.4 1.7 copy.71
  97.1 2.2 reshape.90
  100.0 46.6 %shard_map.114 = (bf16[32,2,48,256]{3,2,1,0:T(8,128)(2,1)}, f32[32,8,128]{2,1,0:T(8,128)}) custom-call(bf16[32,2,48,256]{3,2,1,0:T(8,128)(2,1)} %convert_element_type.42.refs_0_, f32[32,8,128]{2,1,0:T(8,128)} %bitcast.104), custom_call_target="tpu_custom_call" | custom-call | tf_op jit(solution)/shard_map/pallas_call | solution.py:63
  147.6 2.7 %reshape.94 = f32[64,48,2]{2,1,0:T(8,128)} reshape(f32[32,192]{1,0:T(8,128)S(1)} %slice.36) | data formatting | bytes 49152 | tf_op jit(solution)/shard_map/reshape | solution.py:170
  150.3 2.0 copy.73
  153.0 2.8 %gather_fusion = bf16[13,48,256]{2,1,0:T(8,128)(2,1)} fusion(bf16[64,48,256]{2,1,0:T(8,128)(2,1)} %bitcast.108, s32[1024]{0:T(1024)} %pad_clamp_fusion), kind=kCustom, calls=%fused_computation | custom fusion | bytes 639028 | tf_op jit(solution)/shard_map/jit(_take)/gather | solution.py:171
  156.7 1.8 fusion.17
  160.4 1.6 gather_fusion.2
  163.6 55.2 %all-gather.2.cloned.1.call-done = bf16[624,4096]{1,0:T(8,128)(2,1)} async-done(((bf16[624,256]{1,0:T(8,128)(2,1)}), bf16[624,4096]{1,0:T(8,128)(2,1)}) %all-gather.2.cloned.1.call-update) | async-done | bytes 5111824 | tf_op jit(solution)/shard_map/all_gather | solution.py:184
  218.8 4.7 %convolution_convert_fusion.1 = bf16[624,256]{1,0:T(8,128)(2,1)} fusion(bf16[624,4096]{1,0:T(8,128)(2,1)} %all-gather.2.cloned.1.call-done, bf16[4096,256]{1,0:T(8,128)(2,1)S(1)} %copy-done), kind=kOutput, calls=%fused_computation.25 | convolution fusion | flops 1308782592 | bytes 7528448 | tf_op jit(solution)/shard_map/dot_general | solution.py:183
  (56 shorter events, 16.3 us)
Async XLA Ops:
  7.2 211.7 %copy-start = (bf16[4096,256]{1,0:T(8,128)(2,1)S(1)}, bf16[4096,256]{1,0:T(8,128)(2,1)}, u32[]{:S(2)}) copy-start(bf16[4096,256]{1,0:T(8,128)(2,1)} %param.19) | copy-start | bytes 6291460
  7.2 211.6 %all-gather.2.cloned.1.call-start = ((), (), s32[]{:S(2)}) async-start(), calls=%async_computation | async-start | bytes 5431296 | tf_op jit(solution)/shard_map/all_gather | solution.py:184
  8.0 69.7 %collective-permute-start.1 = (bf16[152]{0:T(256)(128)(2,1)S(1)}, bf16[152]{0:T(256)(128)(2,1)S(1)}, u32[]{:S(2)}, u32[]{:S(2)}) collective-permute-start(bf16[152]{0:T(256)(128)(2,1)S(1)} %compare_convert_fusion), channel_id=1, source_target_pairs={{0,16},{16,0},{32,48},{48,32},{64,80},{80,64},{96,112},{112,96},{1... | collective-permute-start | bytes 920 | tf_op jit(solution)/shard_map/ppermute | solution.py:23
  12.1 65.7 %collective-permute-start = (bf16[1,2,152,256]{3,2,1,0:T(8,128)(2,1)}, bf16[1,2,152,256]{3,2,1,0:T(8,128)(2,1)}, u32[]{:S(2)}, u32[]{:S(2)}) collective-permute-start(bf16[1,2,152,256]{3,2,1,0:T(8,128)(2,1)} %param.17), channel_id=1, source_target_pairs={{0,16},{16,0},{32,48},{48,32},{64,80},{80,64},{96,112},{112,96},{1... | collective-permute-start | bytes 466952 | tf_op jit(solution)/shard_map/ppermute | solution.py:23
  19.1 49.3 %copy-start.5 = (bf16[1,2,152,256]{3,2,1,0:T(8,128)(2,1)S(1)}, bf16[1,2,152,256]{3,2,1,0:T(8,128)(2,1)}, u32[]{:S(2)}) copy-start(bf16[1,2,152,256]{3,2,1,0:T(8,128)(2,1)} %param.15) | copy-start | bytes 466948
  19.1 51.2 %copy-start.4 = (s32[13,48,48]{2,1,0:T(8,128)S(1)}, s32[13,48,48]{2,1,0:T(8,128)}, u32[]{:S(2)}) copy-start(s32[13,48,48]{2,1,0:T(8,128)} %param.12) | copy-start | bytes 359428
  19.1 51.4 %copy-start.1 = (bf16[13,2,48,256]{3,2,1,0:T(8,128)(2,1)S(1)}, bf16[13,2,48,256]{3,2,1,0:T(8,128)(2,1)}, u32[]{:S(2)}) copy-start(bf16[13,2,48,256]{3,2,1,0:T(8,128)(2,1)} %param.11) | copy-start | bytes 1916932
  72.8 0.9 copy-start.2
  81.5 2.1 copy-start.6
  95.4 61.2 %copy-start.3 = (f32[13,2,48,48]{2,3,1,0:T(8,128)S(1)}, f32[13,2,48,48]{2,3,1,0:T(8,128)}, u32[]{:S(2)}) copy-start(f32[13,2,48,48]{2,3,1,0:T(8,128)} %copy-done.2) | copy-start | bytes 718852
Sparse Core Ops, SparseCore 0:
  159.6 59.1 all-gather.1

commit v4 on v3

--- a/solution.py
+++ b/solution.py
@@ -78,23 +78,56 @@
     return rows.reshape(rows.shape[:-1] + (rows.shape[-1] // HD, HD))
 
 
+def prompt_kernel(q_ref, k_ref, v_ref, seen_ref, o_ref, lse_ref):
+    rows = q_ref.shape[0]
+    heads = q_ref.shape[1] // HD
+    visible = seen_ref[...] > 0.5
+    column = lax.broadcasted_iota(jnp.int32, (rows, 128), 1)
+    lse_cols = jnp.zeros((rows, 128), jnp.float32)
+    for head in range(heads):
+        cols = slice(head * HD, (head + 1) * HD)
+        scores = lax.dot_general(
+            q_ref[:, cols],
+            k_ref[:, cols],
+            (((1,), (1,)), ((), ())),
+            preferred_element_type=jnp.float32,
+        ) * (1.0 / math.sqrt(HD))
+        scores = jnp.where(visible, scores, NEG_FILL)
+        peaks = jnp.max(scores, axis=1, keepdims=True)
+        raw = jnp.where(visible, jnp.exp(scores - peaks), 0.0)
+        totals = jnp.sum(raw, axis=1, keepdims=True)
+        accum = jnp.dot(raw.astype(jnp.bfloat16), v_ref[:, cols], preferred_element_type=jnp.float32)
+        o_ref[:, cols] = (accum / totals).astype(o_ref.dtype)
+        lse_cols = jnp.where(column == head, peaks + jnp.log(totals), lse_cols)
+    lse_ref[...] = jnp.transpose(lse_cols)[0:8, :]
+
+
 def prompt_attend(query_rows, key_rows, value_rows, seen):
-    q = split_heads(query_rows)
-    k = split_heads(key_rows)
-    v = split_heads(value_rows)
-    scores = jnp.einsum("qhd,khd->hqk", q, k, preferred_element_type=jnp.float32) * (
-        1.0 / math.sqrt(HD)
-    )
-    scores = jnp.where(seen[None, None, :], scores, NEG_FILL)
-    peaks = jnp.max(scores, axis=2, keepdims=True)
-    raw = jnp.where(seen[None, None, :], jnp.exp(scores - peaks), 0.0)
-    totals = jnp.sum(raw, axis=2)
-    accum = jnp.einsum(
-        "hqk,khd->qhd", raw.astype(jnp.bfloat16), v, preferred_element_type=jnp.float32
-    )
-    normed = accum / jnp.transpose(totals)[:, :, None]
-    lse = jnp.transpose(peaks[:, :, 0] + jnp.log(totals))
-    return normed.reshape(query_rows.shape).astype(jnp.bfloat16), lse
+    n_rows, cols = query_rows.shape
+    n_keys = key_rows.shape[0]
+    padded = -(-n_keys // 128) * 128
+    key_rows = jnp.pad(key_rows, ((0, padded - n_keys), (0, 0)))
+    value_rows = jnp.pad(value_rows, ((0, padded - n_keys), (0, 0)))
+    seen_row = jnp.pad(seen.astype(jnp.float32), (0, padded - n_keys)).reshape(1, padded)
+    block = 384
+    return pl.pallas_call(
+        prompt_kernel,
+        out_shape=[
+            jax.ShapeDtypeStruct((n_rows, cols), jnp.bfloat16),
+            jax.ShapeDtypeStruct((8, n_rows), jnp.float32),
+        ],
+        grid=(n_rows // block,),
+        in_specs=[
+            pl.BlockSpec((block, cols), lambda i: (i, 0)),
+            pl.BlockSpec((padded, cols), lambda i: (0, 0)),
+            pl.BlockSpec((padded, cols), lambda i: (0, 0)),
+            pl.BlockSpec((1, padded), lambda i: (0, 0)),
+        ],
+        out_specs=[
+            pl.BlockSpec((block, cols), lambda i: (i, 0)),
+            pl.BlockSpec((8, block), lambda i: (0, i)),
+        ],
+    )(query_rows, key_rows, value_rows, seen_row)
 
 
 def tree_attend(queries, keys, values, seen):
@@ -158,6 +191,7 @@
 
     lse_width = per_group * TREE * heads_here
     lse_tile = -(-lse_width // 1024) * 1024
+    lse = jnp.swapaxes(lse[:heads_here].reshape(heads_here, groups, per_group * TREE), 0, 1)
     lse_block = jnp.pad(lse.reshape(groups, lse_width), ((0, 0), (0, lse_tile - lse_width)))
     back_out, back_lse = exchange(
         [
@@ -167,7 +201,9 @@
         1,
     )
     back_out = back_out.reshape(n_slots, TREE, local_cols)
-    back_lse = back_lse.reshape(groups, lse_tile)[:, :lse_width].reshape(n_slots, TREE, heads_here)
+    back_lse = back_lse.reshape(groups, lse_tile)[:, :lse_width]
+    back_lse = jnp.moveaxis(back_lse.reshape(groups, heads_here, per_group, TREE), 1, 3)
+    back_lse = back_lse.reshape(n_slots, TREE, heads_here)
     remote_out = split_heads(jnp.take(back_out, slot_index, axis=0)).astype(jnp.float32)
     remote_lse = jnp.take(back_lse, slot_index, axis=0)
 

time: 231 us -> 211 us (0.913)
  local copies, waits for them, and re-layouts: 39 us -> 17.9 us
  Pallas kernels: 90.4 us -> 99.7 us
  matrix products: 15.4 us -> 8.51 us
    pallas_call x0 -> x1, Pallas kernels: none -> 9.21 us  [prompt_attend(): pl.pallas_call(prompt_kernel, out_shape=[jax.ShapeDtypeStruct((n_rows, co...]
    convert_element_type x2 -> x0, local copies, waits for them, and re-layouts: 8.65 us -> none  [prompt_attend(): return (normed.reshape(query_rows.shape).astype(jnp.bfloat16), lse)]
    dot_general x2 -> x0, matrix products: 5.88 us -> none  [the longest x1 3.21 us: prompt_attend(): jnp.einsum('hqk,khd->qhd', raw.astype(jnp.bfloat16), v, preferred_element...]
    reshape x2 -> x4, local copies, waits for them, and re-layouts: 4.7 us -> 0.85 us  [the longest x1 0.59 us: prompt_attend(): jnp.pad(seen.astype(jnp.float32), (0, padded - n_keys)).reshape(1, padded)]
    another operation x3 -> x2, local copies, waits for them, and re-layouts: 5.11 us -> 1.6 us  [split_heads(): return rows.reshape(rows.shape[:-1] + (rows.shape[-1] // HD, HD))]
    concatenate x8 -> x0, local copies, waits for them, and re-layouts: 3.17 us -> none  [the longest x4 1.6 us: local(): jnp.concatenate([prompt_cache[0, 1], partner_cache[0, 1]], axis=0)]
    squeeze x0 -> x2, local copies, waits for them, and re-layouts: none -> 2.5 us  [the longest x1 1.57 us: local(): prompt_cache[0, 1]]
  transfers between devices with their start and end apart: 3 -> 3, of which waited for: 1 -> 1; matrix products, arithmetic and copies ran while one was open for 10% -> 8% of each run, Pallas kernels for 19% -> 21%
where the time goes in v4:
time: 211 us
  Pallas kernels  99.7 us (47%)
  waiting for transfers between devices  56.7 us (27%)
  local copies, waits for them, and re-layouts  17.9 us (8%)
  between operations  15.6 us (7%)
  matrix products  8.51 us (4%)
  other arithmetic  6.32 us (3%)
  starting transfers between devices  6.11 us (3%)
    pallas_call x2, Pallas kernels, exchange(): pl.pallas_call(lambda *refs: exchange_kernel(n, count, *refs), out_shape=...  90.5 us
    all_gather x1, waiting for transfers between devices, local(): lax.all_gather(attn, 'tp', axis=1, tiled=True)  56.6 us
    pallas_call x1, Pallas kernels, prompt_attend(): pl.pallas_call(prompt_kernel, out_shape=[jax.ShapeDtypeStruct((n_rows, co...  9.21 us
    ppermute x2, starting transfers between devices, swapped(): return lax.ppermute(value, axis, pairs)  6.08 us
    dot_general x1, matrix products, local(): jnp.dot(lax.all_gather(attn, 'tp', axis=1, tiled=True), out_weight, prefe...  4.66 us
  transfers between devices with their start and end apart: 3, of which 1 were waited for; matrix products, arithmetic and copies ran while one was open for 8% of the time, Pallas kernels for 21%

profile of v4, /device:TPU:1, one launch (start us, length us, event | category | flops | bytes accessed | tf_op | source)
XLA Modules:
  0.0 210.7 jit_solution(2272812176093802992)
XLA Ops:
  7.2 4.2 %collective-permute-start = (bf16[1,2,152,256]{3,2,1,0:T(8,128)(2,1)}, bf16[1,2,152,256]{3,2,1,0:T(8,128)(2,1)}, u32[]{:S(2)}, u32[]{:S(2)}) collective-permute-start(bf16[1,2,152,256]{3,2,1,0:T(8,128)(2,1)} %param.17), channel_id=1, source_target_pairs={{0,16},{16,0},{32,48},{48,32},{64,80},{80,64},{96,112},{112,96},{1... | collective-permute-start | bytes 466952 | tf_op jit(solution)/shard_map/ppermute | solution.py:23
  12.6 1.9 collective-permute-start.1
  14.6 0.9 convert_reduce_fusion
  16.1 1.3 and_bitcast_fusion
  17.4 1.6 slice_bitcast_fusion.2
  19.6 1.0 broadcast_compare_fusion
  20.8 1.1 fusion.33
  22.0 0.8 reshape_squeeze.6
  23.5 1.3 fusion.34
  25.0 2.0 copy.50
  27.0 43.9 %shard_map.113 = bf16[32,2,48,256]{3,2,1,0:T(8,128)(2,1)} custom-call(bf16[32,2,48,256]{3,2,1,0:T(8,128)(2,1)} %bitcast.97), custom_call_target="tpu_custom_call" | custom-call | tf_op jit(solution)/shard_map/pallas_call | solution.py:63
  70.9 0.8 reshape_squeeze.7
  73.0 0.9 slice_bitcast_fusion
  73.9 0.8 fusion.20
  74.7 9.2 %shard_map.114 = (bf16[3072,256]{1,0:T(8,128)(2,1)}, f32[8,3072]{1,0:T(8,128)}) custom-call(bf16[3072,256]{1,0:T(8,128)(2,1)} %bitcast.96, bf16[384,256]{1,0:T(8,128)(2,1)} %get-tuple-element.29.k_ref, bf16[384,256]{1,0:T(8,128)(2,1)} %get-tuple-element.30.v_ref, f32[1,384]{1,0:T(1,128)} %reshape.105.seen_ref), custom_call_target="tpu_custom_call" | custom-call | tf_op jit(solution)/shard_map/pallas_call | solution.py:113
  83.9 0.9 slice.28
  85.7 46.6 %shard_map.115 = (bf16[32,2,48,256]{3,2,1,0:T(8,128)(2,1)}, f32[32,8,128]{2,1,0:T(8,128)}) custom-call(bf16[32,2,48,256]{3,2,1,0:T(8,128)(2,1)} %bitcast.98, f32[32,8,128]{2,1,0:T(8,128)} %bitcast.101), custom_call_target="tpu_custom_call" | custom-call | tf_op jit(solution)/shard_map/pallas_call | solution.py:63
  132.4 0.9 copy.88
  134.1 2.7 %gather_fusion = bf16[13,48,256]{2,1,0:T(8,128)(2,1)} fusion(bf16[64,48,256]{2,1,0:T(8,128)(2,1)} %bitcast.107, s32[1024]{0:T(1024)S(1)} %pad_clamp_fusion), kind=kCustom, calls=%fused_computation | custom fusion | bytes 639028 | tf_op jit(solution)/shard_map/jit(_take)/gather | solution.py:207
  136.9 1.9 fusion.4
  139.1 0.8 copy.87
  140.1 1.6 gather_fusion.2
  142.6 56.6 %all-gather.2.cloned.1.call-done = bf16[624,4096]{1,0:T(8,128)(2,1)} async-done(((bf16[624,256]{1,0:T(8,128)(2,1)}), bf16[624,4096]{1,0:T(8,128)(2,1)}) %all-gather.2.cloned.1.call-update) | async-done | bytes 5111824 | tf_op jit(solution)/shard_map/all_gather | solution.py:220
  199.2 4.7 %convolution_convert_fusion.1 = bf16[624,256]{1,0:T(8,128)(2,1)} fusion(bf16[624,4096]{1,0:T(8,128)(2,1)} %all-gather.2.cloned.1.call-done, bf16[4096,256]{1,0:T(8,128)(2,1)S(1)} %copy-done), kind=kOutput, calls=%fused_computation.11 | convolution fusion | flops 1308782592 | bytes 7528448 | tf_op jit(solution)/shard_map/dot_general | solution.py:219
  (46 shorter events, 6.8 us)
Async XLA Ops:
  7.2 192.1 %copy-start = (bf16[4096,256]{1,0:T(8,128)(2,1)S(1)}, bf16[4096,256]{1,0:T(8,128)(2,1)}, u32[]{:S(2)}) copy-start(bf16[4096,256]{1,0:T(8,128)(2,1)} %param.19) | copy-start | bytes 6291460
  7.2 15.6 %copy-start.2 = (bf16[13,48,256]{2,1,0:T(8,128)(2,1)S(1)}, bf16[13,48,256]{2,1,0:T(8,128)(2,1)}, u32[]{:S(2)}) copy-start(bf16[13,48,256]{2,1,0:T(8,128)(2,1)} %param.10) | copy-start | bytes 958468
  7.2 192.0 %all-gather.2.cloned.1.call-start = ((), (), s32[]{:S(2)}) async-start(), calls=%async_computation | async-start | bytes 5431296 | tf_op jit(solution)/shard_map/all_gather | solution.py:220
  7.2 65.7 %collective-permute-start = (bf16[1,2,152,256]{3,2,1,0:T(8,128)(2,1)}, bf16[1,2,152,256]{3,2,1,0:T(8,128)(2,1)}, u32[]{:S(2)}, u32[]{:S(2)}) collective-permute-start(bf16[1,2,152,256]{3,2,1,0:T(8,128)(2,1)} %param.17), channel_id=1, source_target_pairs={{0,16},{16,0},{32,48},{48,32},{64,80},{80,64},{96,112},{112,96},{1... | collective-permute-start | bytes 466952 | tf_op jit(solution)/shard_map/ppermute | solution.py:23
  12.6 59.0 %collective-permute-start.1 = (bf16[152]{0:T(256)(128)(2,1)}, bf16[152]{0:T(256)(128)(2,1)}, u32[]{:S(2)}, u32[]{:S(2)}) collective-permute-start(bf16[152]{0:T(256)(128)(2,1)} %compare_convert_fusion), channel_id=1, source_target_pairs={{0,16},{16,0},{32,48},{48,32},{64,80},{80,64},{96,112},{112,96},{1... | collective-permute-start | bytes 920 | tf_op jit(solution)/shard_map/ppermute | solution.py:23
  27.0 46.9 %copy-start.3 = (bf16[152,256]{1,0:T(8,128)(2,1)S(1)}, bf16[152,256]{1,0:T(8,128)(2,1)}, u32[]{:S(2)}) copy-start(bf16[152,256]{1,0:T(8,128)(2,1)} %get-tuple-element.24) | copy-start | bytes 233476
  84.9 51.9 %copy-start.5 = (pred[13]{0:T(512)(128)(4,1)S(1)}, pred[13]{0:T(512)(128)(4,1)}, u32[]{:S(2)}) copy-start(pred[13]{0:T(512)(128)(4,1)} %get-tuple-element.19) | copy-start | bytes 43
  136.9 3.0 %copy-start.4 = (s32[13,8]{0,1:T(8,128)S(1)}, s32[13,8]{0,1:T(8,128)}, u32[]{:S(2)}) copy-start(s32[13,8]{0,1:T(8,128)} %param.14) | copy-start | bytes 1252
  136.9 3.1 %copy-start.1 = (bf16[13,2,48,256]{3,2,1,0:T(8,128)(2,1)S(1)}, bf16[13,2,48,256]{3,2,1,0:T(8,128)(2,1)}, u32[]{:S(2)}) copy-start(bf16[13,2,48,256]{3,2,1,0:T(8,128)(2,1)} %param.11) | copy-start | bytes 1916932
Sparse Core Ops, SparseCore 0:
  140.0 59.1 all-gather.1

commit v5 on v4

--- a/solution.py
+++ b/solution.py
@@ -23,10 +23,10 @@
     return lax.ppermute(value, axis, pairs)
 
 
-def exchange_kernel(n, count, *refs):
+def exchange_kernel(n, count, extra, *refs):
     sources = refs[:count]
-    targets = refs[count : 2 * count]
-    send_sem, recv_sem, local_sem = refs[2 * count :]
+    targets = refs[count + extra : 2 * count + extra]
+    send_sem, recv_sem, local_sem = refs[2 * count + extra :]
     me = lax.axis_index("rep")
     barrier = pltpu.get_barrier_semaphore()
     for offset in range(1, n):
@@ -57,13 +57,14 @@
         copy.wait()
 
 
-def exchange(arrays, tag):
+def exchange(arrays, tag, after=()):
     n = lax.axis_size("rep")
     count = len(arrays)
+    extra = len(after)
     return pl.pallas_call(
-        lambda *refs: exchange_kernel(n, count, *refs),
+        lambda *refs: exchange_kernel(n, count, extra, *refs),
         out_shape=[jax.ShapeDtypeStruct(a.shape, a.dtype) for a in arrays],
-        in_specs=[pl.BlockSpec(memory_space=pl.ANY)] * count,
+        in_specs=[pl.BlockSpec(memory_space=pl.ANY)] * (count + extra),
         out_specs=[pl.BlockSpec(memory_space=pl.ANY)] * count,
         scratch_shapes=[
             pltpu.SemaphoreType.DMA((count, n)),
@@ -71,7 +72,7 @@
             pltpu.SemaphoreType.DMA((count,)),
         ],
         compiler_params=pltpu.CompilerParams(collective_id=tag, has_side_effects=True),
-    )(*arrays)
+    )(*arrays, *after)
 
 
 def split_heads(rows):
@@ -97,7 +98,7 @@
         raw = jnp.where(visible, jnp.exp(scores - peaks), 0.0)
         totals = jnp.sum(raw, axis=1, keepdims=True)
         accum = jnp.dot(raw.astype(jnp.bfloat16), v_ref[:, cols], preferred_element_type=jnp.float32)
-        o_ref[:, cols] = (accum / totals).astype(o_ref.dtype)
+        o_ref[head] = (accum / totals).astype(o_ref.dtype)
         lse_cols = jnp.where(column == head, peaks + jnp.log(totals), lse_cols)
     lse_ref[...] = jnp.transpose(lse_cols)[0:8, :]
 
@@ -113,7 +114,7 @@
     return pl.pallas_call(
         prompt_kernel,
         out_shape=[
-            jax.ShapeDtypeStruct((n_rows, cols), jnp.bfloat16),
+            jax.ShapeDtypeStruct((cols // HD, n_rows, HD), jnp.bfloat16),
             jax.ShapeDtypeStruct((8, n_rows), jnp.float32),
         ],
         grid=(n_rows // block,),
@@ -124,7 +125,7 @@
             pl.BlockSpec((1, padded), lambda i: (0, 0)),
         ],
         out_specs=[
-            pl.BlockSpec((block, cols), lambda i: (i, 0)),
+            pl.BlockSpec((cols // HD, block, HD), lambda i: (0, i, 0)),
             pl.BlockSpec((8, block), lambda i: (0, i)),
         ],
     )(query_rows, key_rows, value_rows, seen_row)
@@ -189,38 +190,42 @@
     seen = jnp.concatenate([positions < first_len[0], partner_flag > 0.5], axis=0)
     normed, lse = prompt_attend(routed_rows, key_rows, value_rows, seen)
 
-    lse_width = per_group * TREE * heads_here
+    lse_width = per_group * TREE
     lse_tile = -(-lse_width // 1024) * 1024
-    lse = jnp.swapaxes(lse[:heads_here].reshape(heads_here, groups, per_group * TREE), 0, 1)
-    lse_block = jnp.pad(lse.reshape(groups, lse_width), ((0, 0), (0, lse_tile - lse_width)))
-    back_out, back_lse = exchange(
-        [
-            normed.reshape(groups, per_group, TREE, local_cols),
-            lse_block.reshape(groups, lse_tile // 128, 128),
-        ],
-        1,
-    )
-    back_out = back_out.reshape(n_slots, TREE, local_cols)
-    back_lse = back_lse.reshape(groups, lse_tile)[:, :lse_width]
-    back_lse = jnp.moveaxis(back_lse.reshape(groups, heads_here, per_group, TREE), 1, 3)
-    back_lse = back_lse.reshape(n_slots, TREE, heads_here)
-    remote_out = split_heads(jnp.take(back_out, slot_index, axis=0)).astype(jnp.float32)
-    remote_lse = jnp.take(back_lse, slot_index, axis=0)
+    lse = lse[:heads_here].reshape(heads_here, groups, lse_width)
+    lse = jnp.pad(lse, ((0, 0), (0, 0), (0, lse_tile - lse_width)))
+    lse = lse.reshape(heads_here, groups, lse_tile // 128, 128)
 
     tree_max, tree_total, tree_accum = tree_attend(
         queries, tree_cache[:, 0], tree_cache[:, 1], tree_mask == 1
     )
-    peaks = jnp.maximum(remote_lse, tree_max)
-    factor_remote = jnp.exp(remote_lse - peaks)
-    factor_tree = jnp.exp(tree_max - peaks)
-    totals = factor_remote + tree_total * factor_tree
-    accum = remote_out * factor_remote[..., None] + tree_accum * factor_tree[..., None]
-    attn = (accum / totals[..., None]).reshape(req_here * TREE, local_cols).astype(jnp.bfloat16)
-    summed = jnp.dot(
-        lax.all_gather(attn, "tp", axis=1, tiled=True),
-        out_weight,
-        preferred_element_type=jnp.float32,
-    )
+    tp_size = lax.axis_size("tp")
+    weight_rows = out_weight.reshape(tp_size, heads_here, HD, out_weight.shape[1])
+    summed = None
+    previous = ()
+    for head in range(heads_here):
+        back_out, back_lse = exchange(
+            [normed[head].reshape(groups, per_group, TREE, HD), lse[head]], 1 + head, previous
+        )
+        back_lse = back_lse.reshape(groups, lse_tile)[:, :lse_width].reshape(n_slots, TREE)
+        remote_out = jnp.take(back_out.reshape(n_slots, TREE, HD), slot_index, axis=0)
+        remote_lse = jnp.take(back_lse, slot_index, axis=0)
+        peaks = jnp.maximum(remote_lse, tree_max[..., head])
+        factor_remote = jnp.exp(remote_lse - peaks)
+        factor_tree = jnp.exp(tree_max[..., head] - peaks)
+        totals = factor_remote + tree_total[..., head] * factor_tree
+        accum = (
+            remote_out.astype(jnp.float32) * factor_remote[..., None]
+            + tree_accum[:, :, head] * factor_tree[..., None]
+        )
+        attn = (accum / totals[..., None]).reshape(req_here * TREE, HD).astype(jnp.bfloat16)
+        previous = (attn,)
+        part = jnp.dot(
+            lax.all_gather(attn, "tp", axis=1, tiled=True),
+            weight_rows[:, head].reshape(tp_size * HD, out_weight.shape[1]),
+            preferred_element_type=jnp.float32,
+        )
+        summed = part if summed is None else summed + part
     projected = summed.astype(jnp.bfloat16).reshape(req_here, TREE, out_weight.shape[1])
     accepted_cache = jnp.take_along_axis(tree_cache, accepted_path[:, None, :, None], axis=2)
     return (projected, accepted_cache)

time: 211 us -> 221 us (1.047)
  Pallas kernels: 99.7 us -> 110 us
    pallas_call x3 -> x4, Pallas kernels: 99.7 us -> 110 us  [the longest x3 101 us: exchange(): pl.pallas_call(lambda *refs: exchange_kernel(n, count, extra, *refs), out...]
    slice x2 -> x5, local copies, waits for them, and re-layouts: 0.9 us -> 5.19 us  [the longest x1 2.61 us: local(): normed[head].reshape(groups, per_group, TREE, HD)]
    dot_general x1 -> x2, matrix products: 4.66 us -> 5.83 us  [local(): jnp.dot(lax.all_gather(attn, 'tp', axis=1, tiled=True), weight_rows[:, he...]
    all_gather x1 -> x2, waiting for transfers between devices: 56.6 us -> 56.7 us  [local(): lax.all_gather(attn, 'tp', axis=1, tiled=True)]
  transfers between devices with their start and end apart: 3 -> 4, of which waited for: 1 -> 2; matrix products, arithmetic and copies ran while one was open for 8% -> 9% of each run, Pallas kernels for 21% -> 32%
where the time goes in v5:
time: 221 us; the launch traced here: 220 us
  Pallas kernels  110 us (50%)
  waiting for transfers between devices  56.8 us (26%)
  local copies, waits for them, and re-layouts  20 us (9%)
  between operations  15.6 us (7%)
  matrix products  7.17 us (3%)
  starting transfers between devices  6.17 us (3%)
  other arithmetic  4.55 us (2%)
    pallas_call x3, Pallas kernels, exchange(): pl.pallas_call(lambda *refs: exchange_kernel(n, count, extra, *refs), out...  101 us
    all_gather x2, waiting for transfers between devices, local(): lax.all_gather(attn, 'tp', axis=1, tiled=True)  56.7 us
    pallas_call x1, Pallas kernels, prompt_attend(): pl.pallas_call(prompt_kernel, out_shape=[jax.ShapeDtypeStruct((cols // HD...  9.19 us
    ppermute x2, starting transfers between devices, swapped(): return lax.ppermute(value, axis, pairs)  6.09 us
    dot_general x2, matrix products, local(): jnp.dot(lax.all_gather(attn, 'tp', axis=1, tiled=True), weight_rows[:, he...  5.83 us
  transfers between devices with their start and end apart: 4, of which 2 were waited for; matrix products, arithmetic and copies ran while one was open for 9% of the time, Pallas kernels for 32%

profile of v5, /device:TPU:1, one launch (start us, length us, event | category | flops | bytes accessed | tf_op | source)
XLA Modules:
  0.0 220.4 jit_solution(5987466935035857652)
XLA Ops:
  7.2 4.2 %collective-permute-start = (bf16[1,2,152,256]{3,2,1,0:T(8,128)(2,1)}, bf16[1,2,152,256]{3,2,1,0:T(8,128)(2,1)S(1)}, u32[]{:S(2)}, u32[]{:S(2)}) collective-permute-start(bf16[1,2,152,256]{3,2,1,0:T(8,128)(2,1)} %param.21), channel_id=1, source_target_pairs={{0,16},{16,0},{32,48},{48,32},{64,80},{80,64},{96,112},{112,96},{1... | collective-permute-start | bytes 466952 | tf_op jit(solution)/shard_map/ppermute | solution.py:23
  12.1 1.9 collective-permute-start.1
  14.0 1.1 fusion.49
  15.2 1.0 broadcast_compare_fusion
  19.0 2.1 copy.44
  21.1 43.7 %shard_map.113 = bf16[32,2,48,256]{3,2,1,0:T(8,128)(2,1)} custom-call(bf16[32,2,48,256]{3,2,1,0:T(8,128)(2,1)} %bitcast.128), custom_call_target="tpu_custom_call" | custom-call | tf_op jit(solution)/shard_map/pallas_call | solution.py:64
  65.5 0.8 fusion.25
  66.3 9.2 %shard_map.114 = (bf16[2,3072,128]{2,1,0:T(8,128)(2,1)}, f32[8,3072]{1,0:T(8,128)}) custom-call(bf16[3072,256]{1,0:T(8,128)(2,1)} %bitcast.127, bf16[384,256]{1,0:T(8,128)(2,1)} %get-tuple-element.44.k_ref, bf16[384,256]{1,0:T(8,128)(2,1)} %get-tuple-element.45.v_ref, f32[1,384]{1,0:T(1,128)} %reshape.117.seen_ref), custom_call_target="tpu_custom_call" | custom-call | tf_op jit(solution)/shard_map/pallas_call | solution.py:114
  75.5 2.6 %fusion.48 = (bf16[1,3072,128]{2,1,0:T(8,128)(2,1)}, bf16[1,3072,128]{2,1,0:T(8,128)(2,1)}) fusion(bf16[2,3072,128]{2,1,0:T(8,128)(2,1)} %get-tuple-element.10), kind=kLoop, calls=%fused_computation.90 | loop fusion | bytes 3145728 | tf_op jit(solution)/shard_map/slice | solution.py:208
  78.1 0.9 slice.72
  79.8 30.4 %shard_map.115 = (bf16[32,2,48,128]{3,2,1,0:T(8,128)(2,1)}, f32[32,8,128]{2,1,0:T(8,128)}) custom-call(bf16[32,2,48,128]{3,2,1,0:T(8,128)(2,1)} %bitcast.129, f32[32,8,128]{2,1,0:T(8,128)} %bitcast.138), custom_call_target="tpu_custom_call" | custom-call | tf_op jit(solution)/shard_map/pallas_call | solution.py:64
  110.2 0.9 copy.80
  111.2 1.7 gather_fusion.1
  113.6 1.0 fusion.22
  115.4 26.7 %shard_map.116 = (bf16[32,2,48,128]{3,2,1,0:T(8,128)(2,1)}, f32[32,8,128]{2,1,0:T(8,128)}) custom-call(bf16[32,2,48,128]{3,2,1,0:T(8,128)(2,1)} %bitcast.130, f32[32,8,128]{2,1,0:T(8,128)} %bitcast.137, bf16[624,128]{1,0:T(8,128)(2,1)} %bitcast.133), custom_call_target="tpu_custom_call" | custom-call | tf_op jit(solution)/shard_map/pallas_call | solution.py:64
  142.1 1.7 gather_fusion.3
  143.9 0.9 copy.79
  145.5 1.0 fusion.23
  146.8 1.6 gather_fusion
  149.3 1.7 fusion.47
  150.9 12.5 %all-gather.3.cloned.1.call-done = bf16[624,2048]{1,0:T(8,128)(2,1)} async-done(((bf16[624,128]{1,0:T(8,128)(2,1)}), bf16[624,2048]{1,0:T(8,128)(2,1)}) %all-gather.3.cloned.1.call-update) | async-done | bytes 2555920 | tf_op jit(solution)/shard_map/all_gather | solution.py:224
  163.4 2.5 %fusion.51 = f32[624,256]{1,0:T(8,128)S(1)} fusion(bf16[624,2048]{1,0:T(8,128)(2,1)} %all-gather.3.cloned.1.call-done, bf16[2048,256]{1,0:T(8,128)(2,1)S(1)} %bitcast.135), kind=kOutput, calls=%fused_computation.93 | convolution fusion | flops 654311424 | bytes 4243456 | tf_op jit(solution)/shard_map/dot_general | solution.py:223
  166.0 44.2 %all-gather.5.cloned.1.call-done = bf16[624,2048]{1,0:T(8,128)(2,1)} async-done(((bf16[624,128]{1,0:T(8,128)(2,1)}), bf16[624,2048]{1,0:T(8,128)(2,1)}) %all-gather.5.cloned.1.call-update) | async-done | bytes 2555920 | tf_op jit(solution)/shard_map/all_gather | solution.py:224
  210.2 3.3 %fusion.1 = bf16[624,256]{1,0:T(8,128)(2,1)} fusion(f32[624,256]{1,0:T(8,128)S(1)} %fusion.51, bf16[624,2048]{1,0:T(8,128)(2,1)} %all-gather.5.cloned.1.call-done, bf16[2048,256]{1,0:T(8,128)(2,1)S(1)} %bitcast.134), kind=kOutput, calls=%fused_computation.10 | convolution fusion | flops 654630912 | bytes 4562944 | tf_op jit(solution)/shard_map/dot_general | solution.py:223
  (55 shorter events, 6.9 us)
Async XLA Ops:
  7.2 9.6 %copy-start = (bf16[13,48,256]{2,1,0:T(8,128)(2,1)S(1)}, bf16[13,48,256]{2,1,0:T(8,128)(2,1)}, u32[]{:S(2)}) copy-start(bf16[13,48,256]{2,1,0:T(8,128)(2,1)} %param.14) | copy-start | bytes 958468
  7.2 9.3 %copy-start.4 = (s32[13,1]{0,1:T(1,128)S(1)}, s32[13,1]{0,1:T(1,128)}, u32[]{:S(2)}) copy-start(s32[13,1]{0,1:T(1,128)} %param.17) | copy-start | bytes 160
  7.2 156.3 %all-gather.3.cloned.1.call-start = ((), (), s32[]{:S(2)}) async-start(), calls=%async_computation | async-start | bytes 2715648 | tf_op jit(solution)/shard_map/all_gather | solution.py:224
  7.2 58.3 %collective-permute-start = (bf16[1,2,152,256]{3,2,1,0:T(8,128)(2,1)}, bf16[1,2,152,256]{3,2,1,0:T(8,128)(2,1)S(1)}, u32[]{:S(2)}, u32[]{:S(2)}) collective-permute-start(bf16[1,2,152,256]{3,2,1,0:T(8,128)(2,1)} %param.21), channel_id=1, source_target_pairs={{0,16},{16,0},{32,48},{48,32},{64,80},{80,64},{96,112},{112,96},{1... | collective-permute-start | bytes 466952 | tf_op jit(solution)/shard_map/ppermute | solution.py:23
  12.1 52.7 %collective-permute-start.1 = (bf16[152]{0:T(256)(128)(2,1)S(1)}, bf16[152]{0:T(256)(128)(2,1)S(1)}, u32[]{:S(2)}, u32[]{:S(2)}) collective-permute-start(bf16[152]{0:T(256)(128)(2,1)S(1)} %compare_convert_fusion), channel_id=1, source_target_pairs={{0,16},{16,0},{32,48},{48,32},{64,80},{80,64},{96,112},{112,96},{1... | collective-permute-start | bytes 920 | tf_op jit(solution)/shard_map/ppermute | solution.py:23
  16.7 1.6 copy-start.2
  79.8 66.8 %copy-start.3 = (s32[13,8]{0,1:T(8,128)S(1)}, s32[13,8]{0,1:T(8,128)}, u32[]{:S(2)}) copy-start(s32[13,8]{0,1:T(8,128)} %param.18) | copy-start | bytes 1252
  79.8 67.0 %copy-start.1 = (bf16[13,2,48,256]{3,2,1,0:T(8,128)(2,1)S(1)}, bf16[13,2,48,256]{3,2,1,0:T(8,128)(2,1)}, u32[]{:S(2)}) copy-start(bf16[13,2,48,256]{3,2,1,0:T(8,128)(2,1)} %param.15) | copy-start | bytes 1916932
  114.6 95.6 %all-gather.5.cloned.1.call-start = ((), (), s32[]{:S(2)}) async-start(), calls=%async_computation.1 | async-start | bytes 2715648 | tf_op jit(solution)/shard_map/all_gather | solution.py:224
Sparse Core Ops, SparseCore 0:
  114.8 48.6 all-gather.2
  165.5 44.7 all-gather.4

commit v6 on v4

--- a/solution.py
+++ b/solution.py
@@ -74,6 +74,88 @@
     )(*arrays)
 
 
+def gather_project_kernel(n_z, a_ref, w_ref, o_ref, slots, send_sem, recv_sem):
+    me = lax.axis_index("tp")
+    z = me // 2
+    core = me % 2
+    step_z = 1 - 2 * core
+    ring_next = lax.rem(z + step_z + n_z, n_z) * 2 + core
+    ring_prev = lax.rem(z - step_z + n_z, n_z) * 2 + core
+    sibling = z * 2 + (1 - core)
+    barrier = pltpu.get_barrier_semaphore()
+    for peer in (ring_next, ring_prev, sibling):
+        pl.semaphore_signal(barrier, inc=1, device_id={"tp": peer}, device_id_type=MESH)
+    pl.semaphore_wait(barrier, 3)
+    slots[me] = a_ref[...]
+
+    def origin(step):
+        return lax.rem(z - step * step_z + 2 * n_z, n_z) * 2 + core
+
+    sends = []
+    for step in range(n_z):
+        slot = origin(step)
+        if step == 0:
+            source = a_ref
+        else:
+            source = slots.at[slot]
+            pltpu.make_async_remote_copy(
+                src_ref=slots.at[slot],
+                dst_ref=slots.at[slot],
+                send_sem=send_sem.at[0, step],
+                recv_sem=recv_sem.at[slot],
+                device_id={"tp": ring_prev},
+                device_id_type=MESH,
+            ).wait_recv()
+        targets = [(1, sibling)] + ([(0, ring_next)] if step < n_z - 1 else [])
+        for kind, peer in targets:
+            copy = pltpu.make_async_remote_copy(
+                src_ref=source,
+                dst_ref=slots.at[slot],
+                send_sem=send_sem.at[kind, step],
+                recv_sem=recv_sem.at[slot],
+                device_id={"tp": peer},
+                device_id_type=MESH,
+            )
+            copy.start()
+            sends.append(copy)
+    for step in range(n_z):
+        slot = lax.rem(z - step * step_z + 2 * n_z, n_z) * 2 + (1 - core)
+        pltpu.make_async_remote_copy(
+            src_ref=slots.at[slot],
+            dst_ref=slots.at[slot],
+            send_sem=send_sem.at[1, step],
+            recv_sem=recv_sem.at[slot],
+            device_id={"tp": sibling},
+            device_id_type=MESH,
+        ).wait_recv()
+    for copy in sends:
+        copy.wait_send()
+    width = a_ref.shape[1]
+    total = jnp.zeros(o_ref.shape, jnp.float32)
+    for index in range(slots.shape[0]):
+        total = total + jnp.dot(
+            slots[index], w_ref[index * width : (index + 1) * width, :], preferred_element_type=jnp.float32
+        )
+    o_ref[...] = total.astype(o_ref.dtype)
+
+
+def gather_project(attn, weight):
+    tp_size = lax.axis_size("tp")
+    rows, width = attn.shape
+    return pl.pallas_call(
+        lambda *refs: gather_project_kernel(tp_size // 2, *refs),
+        out_shape=jax.ShapeDtypeStruct((rows, weight.shape[1]), jnp.bfloat16),
+        in_specs=[pl.BlockSpec(memory_space=pltpu.VMEM)] * 2,
+        out_specs=pl.BlockSpec(memory_space=pltpu.VMEM),
+        scratch_shapes=[
+            pltpu.VMEM((tp_size, rows, width), jnp.bfloat16),
+            pltpu.SemaphoreType.DMA((2, tp_size // 2)),
+            pltpu.SemaphoreType.DMA((tp_size,)),
+        ],
+        compiler_params=pltpu.CompilerParams(collective_id=3, has_side_effects=True),
+    )(attn, weight)
+
+
 def split_heads(rows):
     return rows.reshape(rows.shape[:-1] + (rows.shape[-1] // HD, HD))
 
@@ -216,12 +298,7 @@
     totals = factor_remote + tree_total * factor_tree
     accum = remote_out * factor_remote[..., None] + tree_accum * factor_tree[..., None]
     attn = (accum / totals[..., None]).reshape(req_here * TREE, local_cols).astype(jnp.bfloat16)
-    summed = jnp.dot(
-        lax.all_gather(attn, "tp", axis=1, tiled=True),
-        out_weight,
-        preferred_element_type=jnp.float32,
-    )
-    projected = summed.astype(jnp.bfloat16).reshape(req_here, TREE, out_weight.shape[1])
+    projected = gather_project(attn, out_weight).reshape(req_here, TREE, out_weight.shape[1])
     accepted_cache = jnp.take_along_axis(tree_cache, accepted_path[:, None, :, None], axis=2)
     return (projected, accepted_cache)
 

time: 211 us -> 188 us (0.89)
  waiting for transfers between devices: 56.7 us -> 0.01 us
  Pallas kernels: 99.7 us -> 155 us
  between operations: 15.6 us -> 2.14 us
  matrix products: 8.51 us -> 1.76 us
    all_gather x1 -> x0, waiting for transfers between devices: 56.6 us -> none  [local(): lax.all_gather(attn, 'tp', axis=1, tiled=True)]
    pallas_call x0 -> x1, Pallas kernels: none -> 55.7 us  [gather_project(): pl.pallas_call(lambda *refs: gather_project_kernel(tp_size // 2, *refs),...]
    dot_general x1 -> x0, matrix products: 4.66 us -> none  [local(): jnp.dot(lax.all_gather(attn, 'tp', axis=1, tiled=True), out_weight, prefe...]
    unnamed x17 -> x10, local copies, waits for them, and re-layouts: 3.06 us -> 4.77 us
  transfers between devices with their start and end apart: 3 -> 2, of which waited for: 1 -> 0; matrix products, arithmetic and copies ran while one was open for 8% -> 7% of each run, Pallas kernels for 21% -> 23%
where the time goes in v6:
time: 188 us; the launch traced here: 187 us
  Pallas kernels  155 us (82%)
  local copies, waits for them, and re-layouts  15.8 us (8%)
  starting transfers between devices  6.09 us (3%)
  other arithmetic  5.89 us (3%)
  between operations  2.14 us (1%)
    pallas_call x2, Pallas kernels, exchange(): pl.pallas_call(lambda *refs: exchange_kernel(n, count, *refs), out_shape=...  90.3 us
    pallas_call x1, Pallas kernels, gather_project(): pl.pallas_call(lambda *refs: gather_project_kernel(tp_size // 2, *refs),...  55.7 us
    pallas_call x1, Pallas kernels, prompt_attend(): pl.pallas_call(prompt_kernel, out_shape=[jax.ShapeDtypeStruct((n_rows, co...  9.21 us
    ppermute x2, starting transfers between devices, swapped(): return lax.ppermute(value, axis, pairs)  6.09 us
    unnamed x10, local copies, waits for them, and re-layouts  4.77 us
  transfers between devices with their start and end apart: 2, of which 0 were waited for; matrix products, arithmetic and copies ran while one was open for 7% of the time, Pallas kernels for 23%

profile of v6, /device:TPU:1, one launch (start us, length us, event | category | flops | bytes accessed | tf_op | source)
XLA Modules:
  0.0 187.0 jit_solution(6703677199113515585)
XLA Ops:
  0.7 4.2 %collective-permute-start = (bf16[1,2,152,256]{3,2,1,0:T(8,128)(2,1)}, bf16[1,2,152,256]{3,2,1,0:T(8,128)(2,1)S(1)}, u32[]{:S(2)}, u32[]{:S(2)}) collective-permute-start(bf16[1,2,152,256]{3,2,1,0:T(8,128)(2,1)} %param.17), channel_id=1, source_target_pairs={{0,16},{16,0},{32,48},{48,32},{64,80},{80,64},{96,112},{112,96},{1... | collective-permute-start | bytes 466952 | tf_op jit(solution)/shard_map/ppermute | solution.py:23
  5.5 1.9 %collective-permute-start.1 = (bf16[152]{0:T(256)(128)(2,1)S(1)}, bf16[152]{0:T(256)(128)(2,1)S(1)}, u32[]{:S(2)}, u32[]{:S(2)}) collective-permute-start(bf16[152]{0:T(256)(128)(2,1)S(1)} %compare_convert_fusion), channel_id=1, source_target_pairs={{0,16},{16,0},{32,48},{48,32},{64,80},{80,64},{96,112},{112,96},{1... | collective-permute-start | bytes 920 | tf_op jit(solution)/shard_map/ppermute | solution.py:23
  7.4 0.9 convert_reduce_fusion
  9.0 0.7 and_bitcast_fusion
  9.7 0.7 bitcast_or_fusion
  10.3 0.7 compare_and_fusion
  11.0 0.9 slice_bitcast_fusion.2
  12.7 1.0 broadcast_compare_fusion
  13.9 1.1 fusion.33
  15.3 1.6 gather_fusion.2
  17.0 0.7 convolution_convert_fusion
  18.3 2.1 %copy.51 = bf16[64,48,256]{2,1,0:T(8,128)(2,1)} copy(bf16[64,48,256]{2,0,1:T(8,128)(2,1)S(1)} %convolution_convert_fusion) | data formatting | bytes 3145728 | tf_op jit(solution)/shard_map/convert_element_type | solution.py:264
  20.4 43.7 %shard_map.113 = bf16[32,2,48,256]{3,2,1,0:T(8,128)(2,1)} custom-call(bf16[32,2,48,256]{3,2,1,0:T(8,128)(2,1)} %bitcast.95), custom_call_target="tpu_custom_call" | custom-call | tf_op jit(solution)/shard_map/pallas_call | solution.py:63
  65.6 0.8 fusion.20
  66.3 9.2 %shard_map.114 = (bf16[3072,256]{1,0:T(8,128)(2,1)}, f32[8,3072]{1,0:T(8,128)}) custom-call(bf16[3072,256]{1,0:T(8,128)(2,1)} %bitcast.94, bf16[384,256]{1,0:T(8,128)(2,1)} %get-tuple-element.29.k_ref, bf16[384,256]{1,0:T(8,128)(2,1)} %get-tuple-element.30.v_ref, f32[1,384]{1,0:T(1,128)} %reshape.105.seen_ref), custom_call_target="tpu_custom_call" | custom-call | tf_op jit(solution)/shard_map/pallas_call | solution.py:195
  75.5 0.9 slice.28
  76.7 0.7 copy.68
  77.3 46.6 %shard_map.115 = (bf16[32,2,48,256]{3,2,1,0:T(8,128)(2,1)}, f32[32,8,128]{2,1,0:T(8,128)}) custom-call(bf16[32,2,48,256]{3,2,1,0:T(8,128)(2,1)} %bitcast.96, f32[32,8,128]{2,1,0:T(8,128)} %bitcast.100), custom_call_target="tpu_custom_call" | custom-call | tf_op jit(solution)/shard_map/pallas_call | solution.py:63
  124.0 0.9 copy.89
  125.7 2.0 %gather_fusion = bf16[13,48,256]{2,1,0:T(8,128)(2,1)S(1)} fusion(bf16[64,48,256]{2,1,0:T(8,128)(2,1)} %bitcast.106, s32[1024]{0:T(1024)S(1)} %pad_clamp_fusion), kind=kCustom, calls=%fused_computation | custom fusion | bytes 639028 | tf_op jit(solution)/shard_map/jit(_take)/gather | solution.py:289
  127.8 0.7 fusion.4
  128.8 0.8 copy.88
  129.6 55.7 %shard_map.116 = bf16[624,256]{1,0:T(8,128)(2,1)} custom-call(bf16[624,256]{1,0:T(8,128)(2,1)} %bitcast.98, bf16[4096,256]{1,0:T(8,128)(2,1)} %refs_1_.1), custom_call_target="tpu_custom_call" | custom-call | tf_op jit(solution)/shard_map/pallas_call | solution.py:145
  185.2 1.7 copy.93
  (36 shorter events, 4.6 us)
Async XLA Ops:
  0.6 16.4 %copy-start = (bf16[13,48,256]{2,1,0:T(8,128)(2,1)S(1)}, bf16[13,48,256]{2,1,0:T(8,128)(2,1)}, u32[]{:S(2)}) copy-start(bf16[13,48,256]{2,1,0:T(8,128)(2,1)} %param.10) | copy-start | bytes 958468
  0.6 14.6 %copy-start.1 = (bf16[13,2,48,256]{3,2,1,0:T(8,128)(2,1)S(1)}, bf16[13,2,48,256]{3,2,1,0:T(8,128)(2,1)}, u32[]{:S(2)}) copy-start(bf16[13,2,48,256]{3,2,1,0:T(8,128)(2,1)} %param.11) | copy-start | bytes 1916932
  0.7 64.9 %collective-permute-start = (bf16[1,2,152,256]{3,2,1,0:T(8,128)(2,1)}, bf16[1,2,152,256]{3,2,1,0:T(8,128)(2,1)S(1)}, u32[]{:S(2)}, u32[]{:S(2)}) collective-permute-start(bf16[1,2,152,256]{3,2,1,0:T(8,128)(2,1)} %param.17), channel_id=1, source_target_pairs={{0,16},{16,0},{32,48},{48,32},{64,80},{80,64},{96,112},{112,96},{1... | collective-permute-start | bytes 466952 | tf_op jit(solution)/shard_map/ppermute | solution.py:23
  5.5 59.4 %collective-permute-start.1 = (bf16[152]{0:T(256)(128)(2,1)S(1)}, bf16[152]{0:T(256)(128)(2,1)S(1)}, u32[]{:S(2)}, u32[]{:S(2)}) collective-permute-start(bf16[152]{0:T(256)(128)(2,1)S(1)} %compare_convert_fusion), channel_id=1, source_target_pairs={{0,16},{16,0},{32,48},{48,32},{64,80},{80,64},{96,112},{112,96},{1... | collective-permute-start | bytes 920 | tf_op jit(solution)/shard_map/ppermute | solution.py:23

commit v7 on v4

--- a/solution.py
+++ b/solution.py
@@ -74,6 +74,85 @@
     )(*arrays)
 
 
+def gather_project_kernel(n_z, a_ref, w_ref, o_ref, slots, send_sem, recv_sem):
+    me = lax.axis_index("tp")
+    z = me // 2
+    core = me % 2
+    up = lax.rem(z + 1, n_z) * 2 + core
+    down = lax.rem(z + n_z - 1, n_z) * 2 + core
+    sibling = z * 2 + (1 - core)
+    barrier = pltpu.get_barrier_semaphore()
+    for peer in (up, down, sibling):
+        pl.semaphore_signal(barrier, inc=1, device_id={"tp": peer}, device_id_type=MESH)
+    pl.semaphore_wait(barrier, 3)
+    slots[me] = a_ref[...]
+    chains = ((0, 1, up, down), (1, -1, down, up))
+
+    def arrival(slot, half, sender):
+        pltpu.make_async_remote_copy(
+            src_ref=slots.at[slot, half],
+            dst_ref=slots.at[slot, half],
+            send_sem=send_sem.at[half, 0],
+            recv_sem=recv_sem.at[slot, half],
+            device_id={"tp": sender},
+            device_id_type=MESH,
+        ).wait_recv()
+
+    sends = []
+    for step in range(n_z):
+        for half, direction, ahead, behind in chains:
+            slot = lax.rem(z - step * direction + 2 * n_z, n_z) * 2 + core
+            if step == 0:
+                source = a_ref.at[half]
+            else:
+                arrival(slot, half, behind)
+                source = slots.at[slot, half]
+            targets = ([(half, ahead)] if step < n_z - 1 else []) + [(2 + half, sibling)]
+            for kind, peer in targets:
+                copy = pltpu.make_async_remote_copy(
+                    src_ref=source,
+                    dst_ref=slots.at[slot, half],
+                    send_sem=send_sem.at[kind, step],
+                    recv_sem=recv_sem.at[slot, half],
+                    device_id={"tp": peer},
+                    device_id_type=MESH,
+                )
+                copy.start()
+                sends.append(copy)
+    for step in range(n_z):
+        for half, direction, ahead, behind in chains:
+            slot = lax.rem(z - step * direction + 2 * n_z, n_z) * 2 + (1 - core)
+            arrival(slot, half, sibling)
+    for copy in sends:
+        copy.wait_send()
+    width = a_ref.shape[2]
+    total = jnp.zeros(o_ref.shape, jnp.float32)
+    for index in range(slots.shape[0]):
+        for half in range(slots.shape[1]):
+            row = (index * slots.shape[1] + half) * width
+            total = total + jnp.dot(
+                slots[index, half], w_ref[row : row + width, :], preferred_element_type=jnp.float32
+            )
+    o_ref[...] = total.astype(o_ref.dtype)
+
+
+def gather_project(attn, weight):
+    tp_size = lax.axis_size("tp")
+    halves, rows, width = attn.shape
+    return pl.pallas_call(
+        lambda *refs: gather_project_kernel(tp_size // 2, *refs),
+        out_shape=jax.ShapeDtypeStruct((rows, weight.shape[1]), jnp.bfloat16),
+        in_specs=[pl.BlockSpec(memory_space=pltpu.VMEM)] * 2,
+        out_specs=pl.BlockSpec(memory_space=pltpu.VMEM),
+        scratch_shapes=[
+            pltpu.VMEM((tp_size, halves, rows, width), jnp.bfloat16),
+            pltpu.SemaphoreType.DMA((4, tp_size // 2)),
+            pltpu.SemaphoreType.DMA((tp_size, halves)),
+        ],
+        compiler_params=pltpu.CompilerParams(collective_id=3, has_side_effects=True),
+    )(attn, weight)
+
+
 def split_heads(rows):
     return rows.reshape(rows.shape[:-1] + (rows.shape[-1] // HD, HD))
 
@@ -215,13 +294,9 @@
     factor_tree = jnp.exp(tree_max - peaks)
     totals = factor_remote + tree_total * factor_tree
     accum = remote_out * factor_remote[..., None] + tree_accum * factor_tree[..., None]
-    attn = (accum / totals[..., None]).reshape(req_here * TREE, local_cols).astype(jnp.bfloat16)
-    summed = jnp.dot(
-        lax.all_gather(attn, "tp", axis=1, tiled=True),
-        out_weight,
-        preferred_element_type=jnp.float32,
-    )
-    projected = summed.astype(jnp.bfloat16).reshape(req_here, TREE, out_weight.shape[1])
+    attn = jnp.moveaxis(accum / totals[..., None], 2, 0).astype(jnp.bfloat16)
+    attn = attn.reshape(heads_here, req_here * TREE, HD)
+    projected = gather_project(attn, out_weight).reshape(req_here, TREE, out_weight.shape[1])
     accepted_cache = jnp.take_along_axis(tree_cache, accepted_path[:, None, :, None], axis=2)
     return (projected, accepted_cache)
 

time: 211 us -> 186 us (0.88)
  waiting for transfers between devices: 56.7 us -> 0.01 us
  Pallas kernels: 99.7 us -> 154 us
  between operations: 15.6 us -> 2.13 us
  matrix products: 8.51 us -> 1.76 us
  local copies, waits for them, and re-layouts: 17.9 us -> 15.6 us
    all_gather x1 -> x0, waiting for transfers between devices: 56.6 us -> none  [local(): lax.all_gather(attn, 'tp', axis=1, tiled=True)]
    pallas_call x0 -> x1, Pallas kernels: none -> 54.5 us  [gather_project(): pl.pallas_call(lambda *refs: gather_project_kernel(tp_size // 2, *refs),...]
    dot_general x1 -> x0, matrix products: 4.66 us -> none  [local(): jnp.dot(lax.all_gather(attn, 'tp', axis=1, tiled=True), out_weight, prefe...]
  transfers between devices with their start and end apart: 3 -> 2, of which waited for: 1 -> 0; matrix products, arithmetic and copies ran while one was open for 8% -> 7% of each run, Pallas kernels for 21% -> 24%
where the time goes in v7:
time: 186 us; the launch traced here: 185 us
  Pallas kernels  154 us (83%)
  local copies, waits for them, and re-layouts  15.6 us (8%)
  starting transfers between devices  6.09 us (3%)
  other arithmetic  5.89 us (3%)
  between operations  2.13 us (1%)
    pallas_call x2, Pallas kernels, exchange(): pl.pallas_call(lambda *refs: exchange_kernel(n, count, *refs), out_shape=...  90.3 us
    pallas_call x1, Pallas kernels, gather_project(): pl.pallas_call(lambda *refs: gather_project_kernel(tp_size // 2, *refs),...  54.5 us
    pallas_call x1, Pallas kernels, prompt_attend(): pl.pallas_call(prompt_kernel, out_shape=[jax.ShapeDtypeStruct((n_rows, co...  9.21 us
    ppermute x2, starting transfers between devices, swapped(): return lax.ppermute(value, axis, pairs)  6.09 us
    unnamed x9, local copies, waits for them, and re-layouts  4 us
  transfers between devices with their start and end apart: 2, of which 0 were waited for; matrix products, arithmetic and copies ran while one was open for 7% of the time, Pallas kernels for 24%

profile of v7, /device:TPU:1, one launch (start us, length us, event | category | flops | bytes accessed | tf_op | source)
XLA Modules:
  0.0 185.5 jit_solution(6364065390821943683)
XLA Ops:
  0.7 4.2 %collective-permute-start = (bf16[1,2,152,256]{3,2,1,0:T(8,128)(2,1)}, bf16[1,2,152,256]{3,2,1,0:T(8,128)(2,1)S(1)}, u32[]{:S(2)}, u32[]{:S(2)}) collective-permute-start(bf16[1,2,152,256]{3,2,1,0:T(8,128)(2,1)} %param.17), channel_id=1, source_target_pairs={{0,16},{16,0},{32,48},{48,32},{64,80},{80,64},{96,112},{112,96},{1... | collective-permute-start | bytes 466952 | tf_op jit(solution)/shard_map/ppermute | solution.py:23
  5.5 1.9 %collective-permute-start.1 = (bf16[152]{0:T(256)(128)(2,1)S(1)}, bf16[152]{0:T(256)(128)(2,1)S(1)}, u32[]{:S(2)}, u32[]{:S(2)}) collective-permute-start(bf16[152]{0:T(256)(128)(2,1)S(1)} %compare_convert_fusion), channel_id=1, source_target_pairs={{0,16},{16,0},{32,48},{48,32},{64,80},{80,64},{96,112},{112,96},{1... | collective-permute-start | bytes 920 | tf_op jit(solution)/shard_map/ppermute | solution.py:23
  7.4 0.9 convert_reduce_fusion
  9.0 0.7 and_bitcast_fusion
  9.7 0.7 bitcast_or_fusion
  10.3 0.7 compare_and_fusion
  11.0 0.9 slice_bitcast_fusion.2
  12.7 1.0 broadcast_compare_fusion
  13.9 1.1 fusion.34
  15.3 1.6 gather_fusion.2
  17.0 0.7 convolution_convert_fusion
  18.3 2.1 %copy.51 = bf16[64,48,256]{2,1,0:T(8,128)(2,1)} copy(bf16[64,48,256]{2,0,1:T(8,128)(2,1)S(1)} %convolution_convert_fusion) | data formatting | bytes 3145728 | tf_op jit(solution)/shard_map/convert_element_type | solution.py:261
  20.4 43.7 %shard_map.113 = bf16[32,2,48,256]{3,2,1,0:T(8,128)(2,1)} custom-call(bf16[32,2,48,256]{3,2,1,0:T(8,128)(2,1)} %bitcast.95), custom_call_target="tpu_custom_call" | custom-call | tf_op jit(solution)/shard_map/pallas_call | solution.py:63
  65.6 0.8 fusion.21
  66.3 9.2 %shard_map.114 = (bf16[3072,256]{1,0:T(8,128)(2,1)}, f32[8,3072]{1,0:T(8,128)}) custom-call(bf16[3072,256]{1,0:T(8,128)(2,1)} %bitcast.94, bf16[384,256]{1,0:T(8,128)(2,1)} %get-tuple-element.29.k_ref, bf16[384,256]{1,0:T(8,128)(2,1)} %get-tuple-element.30.v_ref, f32[1,384]{1,0:T(1,128)} %reshape.107.seen_ref), custom_call_target="tpu_custom_call" | custom-call | tf_op jit(solution)/shard_map/pallas_call | solution.py:192
  75.5 0.9 slice.28
  76.7 0.7 copy.68
  77.3 46.6 %shard_map.115 = (bf16[32,2,48,256]{3,2,1,0:T(8,128)(2,1)}, f32[32,8,128]{2,1,0:T(8,128)}) custom-call(bf16[32,2,48,256]{3,2,1,0:T(8,128)(2,1)} %bitcast.96, f32[32,8,128]{2,1,0:T(8,128)} %bitcast.99), custom_call_target="tpu_custom_call" | custom-call | tf_op jit(solution)/shard_map/pallas_call | solution.py:63
  124.0 0.9 copy.86
  125.7 2.0 %gather_fusion = bf16[13,48,256]{2,1,0:T(8,128)(2,1)S(1)} fusion(bf16[64,48,256]{2,1,0:T(8,128)(2,1)} %bitcast.105, s32[1024]{0:T(1024)S(1)} %pad_clamp_fusion), kind=kCustom, calls=%fused_computation | custom fusion | bytes 639028 | tf_op jit(solution)/shard_map/jit(_take)/gather | solution.py:286
  127.8 0.7 fusion.5
  128.5 0.7 copy.61
  129.3 54.5 %shard_map.116 = bf16[624,256]{1,0:T(8,128)(2,1)} custom-call(bf16[2,624,128]{2,1,0:T(8,128)(2,1)} %bitcast.97, bf16[4096,256]{1,0:T(8,128)(2,1)} %refs_1_.1), custom_call_target="tpu_custom_call" | custom-call | tf_op jit(solution)/shard_map/pallas_call | solution.py:142
  183.8 1.7 copy.90
  (35 shorter events, 4.4 us)
Async XLA Ops:
  0.6 16.4 %copy-start = (bf16[13,48,256]{2,1,0:T(8,128)(2,1)S(1)}, bf16[13,48,256]{2,1,0:T(8,128)(2,1)}, u32[]{:S(2)}) copy-start(bf16[13,48,256]{2,1,0:T(8,128)(2,1)} %param.10) | copy-start | bytes 958468
  0.6 14.6 %copy-start.1 = (bf16[13,2,48,256]{3,2,1,0:T(8,128)(2,1)S(1)}, bf16[13,2,48,256]{3,2,1,0:T(8,128)(2,1)}, u32[]{:S(2)}) copy-start(bf16[13,2,48,256]{3,2,1,0:T(8,128)(2,1)} %param.11) | copy-start | bytes 1916932
  0.7 64.9 %collective-permute-start = (bf16[1,2,152,256]{3,2,1,0:T(8,128)(2,1)}, bf16[1,2,152,256]{3,2,1,0:T(8,128)(2,1)S(1)}, u32[]{:S(2)}, u32[]{:S(2)}) collective-permute-start(bf16[1,2,152,256]{3,2,1,0:T(8,128)(2,1)} %param.17), channel_id=1, source_target_pairs={{0,16},{16,0},{32,48},{48,32},{64,80},{80,64},{96,112},{112,96},{1... | collective-permute-start | bytes 466952 | tf_op jit(solution)/shard_map/ppermute | solution.py:23
  5.5 59.4 %collective-permute-start.1 = (bf16[152]{0:T(256)(128)(2,1)S(1)}, bf16[152]{0:T(256)(128)(2,1)S(1)}, u32[]{:S(2)}, u32[]{:S(2)}) collective-permute-start(bf16[152]{0:T(256)(128)(2,1)S(1)} %compare_convert_fusion), channel_id=1, source_target_pairs={{0,16},{16,0},{32,48},{48,32},{64,80},{80,64},{96,112},{112,96},{1... | collective-permute-start | bytes 920 | tf_op jit(solution)/shard_map/ppermute | solution.py:23

commit v8 on v7

--- a/solution.py
+++ b/solution.py
@@ -17,17 +17,14 @@
 NEG_FILL = -1e30
 
 
-def swapped(value, axis, apart):
-    mask = 2**apart
-    pairs = [(source, source ^ mask) for source in range(lax.axis_size(axis))]
-    return lax.ppermute(value, axis, pairs)
-
-
-def exchange_kernel(n, count, *refs):
+def exchange_kernel(n, count, paired, *refs):
     sources = refs[:count]
-    targets = refs[count : 2 * count]
-    send_sem, recv_sem, local_sem = refs[2 * count :]
+    pair_sources = refs[count : count + paired]
+    targets = refs[count + paired : 2 * count + paired]
+    pair_targets = refs[2 * count + paired : 2 * count + 2 * paired]
+    send_sem, recv_sem, local_sem, pair_send, pair_recv = refs[2 * count + 2 * paired :]
     me = lax.axis_index("rep")
+    partner = me + 1 - 2 * (me % 2)
     barrier = pltpu.get_barrier_semaphore()
     for offset in range(1, n):
         pl.semaphore_signal(
@@ -35,6 +32,17 @@
         )
     pl.semaphore_wait(barrier, n - 1)
     copies = []
+    for index in range(paired):
+        remote = pltpu.make_async_remote_copy(
+            src_ref=pair_sources[index],
+            dst_ref=pair_targets[index],
+            send_sem=pair_send.at[index],
+            recv_sem=pair_recv.at[index],
+            device_id={"rep": partner},
+            device_id_type=MESH,
+        )
+        remote.start()
+        copies.append(remote)
     for index in range(count):
         local = pltpu.make_async_copy(
             sources[index].at[me], targets[index].at[me], local_sem.at[index]
@@ -57,21 +65,26 @@
         copy.wait()
 
 
-def exchange(arrays, tag):
+def exchange(arrays, tag, pairs=()):
     n = lax.axis_size("rep")
     count = len(arrays)
-    return pl.pallas_call(
-        lambda *refs: exchange_kernel(n, count, *refs),
-        out_shape=[jax.ShapeDtypeStruct(a.shape, a.dtype) for a in arrays],
-        in_specs=[pl.BlockSpec(memory_space=pl.ANY)] * count,
-        out_specs=[pl.BlockSpec(memory_space=pl.ANY)] * count,
+    paired = len(pairs)
+    every = list(arrays) + list(pairs)
+    outs = pl.pallas_call(
+        lambda *refs: exchange_kernel(n, count, paired, *refs),
+        out_shape=[jax.ShapeDtypeStruct(a.shape, a.dtype) for a in every],
+        in_specs=[pl.BlockSpec(memory_space=pl.ANY)] * len(every),
+        out_specs=[pl.BlockSpec(memory_space=pl.ANY)] * len(every),
         scratch_shapes=[
             pltpu.SemaphoreType.DMA((count, n)),
             pltpu.SemaphoreType.DMA((count, n)),
             pltpu.SemaphoreType.DMA((count,)),
+            pltpu.SemaphoreType.DMA((max(paired, 1),)),
+            pltpu.SemaphoreType.DMA((max(paired, 1),)),
         ],
         compiler_params=pltpu.CompilerParams(collective_id=tag, has_side_effects=True),
-    )(*arrays)
+    )(*every)
+    return outs[:count], outs[count:]
 
 
 def gather_project_kernel(n_z, a_ref, w_ref, o_ref, slots, send_sem, recv_sem):
@@ -87,6 +100,14 @@
     pl.semaphore_wait(barrier, 3)
     slots[me] = a_ref[...]
     chains = ((0, 1, up, down), (1, -1, down, up))
+    width = a_ref.shape[2]
+    halves = slots.shape[1]
+
+    def product(slot, half, block):
+        row = pl.multiple_of((slot * halves + half) * width, width)
+        return jnp.dot(block, w_ref[pl.ds(row, width), :], preferred_element_type=jnp.float32)
+
+    total = jnp.zeros(o_ref.shape, jnp.float32)
 
     def arrival(slot, half, sender):
         pltpu.make_async_remote_copy(
@@ -119,20 +140,14 @@
                 )
                 copy.start()
                 sends.append(copy)
+            total = total + product(slot, half, source[...])
     for step in range(n_z):
         for half, direction, ahead, behind in chains:
             slot = lax.rem(z - step * direction + 2 * n_z, n_z) * 2 + (1 - core)
             arrival(slot, half, sibling)
+            total = total + product(slot, half, slots[slot, half])
     for copy in sends:
         copy.wait_send()
-    width = a_ref.shape[2]
-    total = jnp.zeros(o_ref.shape, jnp.float32)
-    for index in range(slots.shape[0]):
-        for half in range(slots.shape[1]):
-            row = (index * slots.shape[1] + half) * width
-            total = total + jnp.dot(
-                slots[index, half], w_ref[row : row + width, :], preferred_element_type=jnp.float32
-            )
     o_ref[...] = total.astype(o_ref.dtype)
 
 
@@ -245,8 +260,7 @@
     per_group = max(2, (req_here + groups - 1) // groups)
     n_slots = groups * per_group
     positions = jnp.arange(PCAP, dtype=jnp.int32)
-    live_flag = (positions < spill_len[0]).astype(jnp.bfloat16)
-    partner_cache, partner_flag = swapped((spill_cache, live_flag), "rep", 0)
+    own_len = jnp.full((8, 128), spill_len[0], jnp.float32)
 
     target = dest_group[:, 0]
     same_target = target[:, None] == target[None, :]
@@ -260,19 +274,19 @@
         "sr,rtc->stc", selector, queries, preferred_element_type=jnp.float32
     ).astype(jnp.bfloat16)
     outbound = outbound.reshape(groups, per_group, TREE, local_cols)
-    (inbound,) = exchange([outbound], 0)
+    (inbound,), (partner_cache, partner_len) = exchange([outbound], 0, (spill_cache, own_len))
     routed_rows = inbound.reshape(n_slots * TREE, local_cols)
 
     key_rows = jnp.concatenate([prompt_cache[0, 0], partner_cache[0, 0]], axis=0)
     value_rows = jnp.concatenate([prompt_cache[0, 1], partner_cache[0, 1]], axis=0)
-    seen = jnp.concatenate([positions < first_len[0], partner_flag > 0.5], axis=0)
+    seen = jnp.concatenate([positions < first_len[0], positions.astype(jnp.float32) < partner_len[0, 0]], axis=0)
     normed, lse = prompt_attend(routed_rows, key_rows, value_rows, seen)
 
     lse_width = per_group * TREE * heads_here
     lse_tile = -(-lse_width // 1024) * 1024
     lse = jnp.swapaxes(lse[:heads_here].reshape(heads_here, groups, per_group * TREE), 0, 1)
     lse_block = jnp.pad(lse.reshape(groups, lse_width), ((0, 0), (0, lse_tile - lse_width)))
-    back_out, back_lse = exchange(
+    (back_out, back_lse), _ = exchange(
         [
             normed.reshape(groups, per_group, TREE, local_cols),
             lse_block.reshape(groups, lse_tile // 128, 128),

time: 186 us -> 180 us (0.968)
  starting transfers between devices: 6.09 us -> 0 us
  other arithmetic: 5.89 us -> 3.53 us
    ppermute x2 -> x0, starting transfers between devices: 6.09 us -> none  [swapped(): return lax.ppermute(value, axis, pairs)]
    pallas_call x2, Pallas kernels: 90.3 us -> 93.6 us  [exchange(): pl.pallas_call(lambda *refs: exchange_kernel(n, count, paired, *refs), ou...]
    unnamed x9 -> x19, local copies, waits for them, and re-layouts: 4 us -> 3.03 us
  transfers between devices with their start and end apart: 2 -> 0, of which waited for: 0 -> 0; matrix products, arithmetic and copies ran while one was open for 7% -> 0% of each run, Pallas kernels for 24% -> 0%
where the time goes in v8:
time: 180 us; the launch traced here: 178 us
  Pallas kernels  155 us (86%)
  local copies, waits for them, and re-layouts  15.3 us (8%)
  other arithmetic  3.53 us (2%)
  between operations  2.22 us (1%)
    pallas_call x2, Pallas kernels, exchange(): pl.pallas_call(lambda *refs: exchange_kernel(n, count, paired, *refs), ou...  93.6 us
    pallas_call x1, Pallas kernels, gather_project(): pl.pallas_call(lambda *refs: gather_project_kernel(tp_size // 2, *refs),...  52.7 us
    pallas_call x1, Pallas kernels, prompt_attend(): pl.pallas_call(prompt_kernel, out_shape=[jax.ShapeDtypeStruct((n_rows, co...  9.2 us

profile of v8, /device:TPU:1, one launch (start us, length us, event | category | flops | bytes accessed | tf_op | source)
XLA Modules:
  0.0 178.3 jit_solution(18238722159692639722)
XLA Ops:
  0.6 0.9 convert_reduce_fusion
  1.6 0.7 multiply_add_fusion
  2.2 0.7 convolution_convert_fusion
  2.9 2.0 %copy.51 = bf16[64,48,256]{2,1,0:T(8,128)(2,1)} copy(bf16[64,48,256]{2,0,1:T(8,128)(2,1)S(1)} %convolution_convert_fusion) | data formatting | bytes 3145728 | tf_op jit(solution)/shard_map/convert_element_type | solution.py:275
  5.6 0.6 broadcast_in_dim.61.refs_2_
  6.2 48.4 %shard_map.113 = (bf16[32,2,48,256]{3,2,1,0:T(8,128)(2,1)}, bf16[1,2,152,256]{3,2,1,0:T(8,128)(2,1)}, f32[8,128]{1,0:T(8,128)}) custom-call(bf16[32,2,48,256]{3,2,1,0:T(8,128)(2,1)} %bitcast.94, bf16[1,2,152,256]{3,2,1,0:T(8,128)(2,1)} %refs_1_.2, f32[8,128]{1,0:T(8,128)} %broadcast_in_dim.61.refs_2_), custom_call_target="tpu_custom_call" | custom-call | tf_op jit(solution)/shard_map/pallas_call | solution.py:73
  54.6 0.9 slice_bitcast_fusion
  55.6 0.8 fusion.21
  56.4 1.2 slice.31
  58.2 0.7 convert_compare_fusion
  59.0 0.6 reshape.108.seen_ref
  59.5 9.2 %shard_map.114 = (bf16[3072,256]{1,0:T(8,128)(2,1)}, f32[8,3072]{1,0:T(8,128)}) custom-call(bf16[3072,256]{1,0:T(8,128)(2,1)} %bitcast.95, bf16[384,256]{1,0:T(8,128)(2,1)} %get-tuple-element.35.k_ref, bf16[384,256]{1,0:T(8,128)(2,1)} %get-tuple-element.36.v_ref, f32[1,384]{1,0:T(1,128)} %reshape.108.seen_ref), custom_call_target="tpu_custom_call" | custom-call | tf_op jit(solution)/shard_map/pallas_call | solution.py:207
  68.7 0.9 slice.32
  69.9 0.7 copy.68
  70.6 45.2 %shard_map.115 = (bf16[32,2,48,256]{3,2,1,0:T(8,128)(2,1)}, f32[32,8,128]{2,1,0:T(8,128)}) custom-call(bf16[32,2,48,256]{3,2,1,0:T(8,128)(2,1)} %bitcast.96, f32[32,8,128]{2,1,0:T(8,128)} %bitcast.99), custom_call_target="tpu_custom_call" | custom-call | tf_op jit(solution)/shard_map/pallas_call | solution.py:73
  115.8 0.9 copy.86
  117.0 0.6 gather_fusion.1
  118.6 2.0 %gather_fusion = bf16[13,48,256]{2,1,0:T(8,128)(2,1)S(1)} fusion(bf16[64,48,256]{2,1,0:T(8,128)(2,1)} %bitcast.105, s32[1024]{0:T(1024)S(1)} %pad_clamp_fusion), kind=kCustom, calls=%fused_computation | custom fusion | bytes 639028 | tf_op jit(solution)/shard_map/jit(_take)/gather | solution.py:300
  120.7 0.7 fusion.5
  121.4 0.7 copy.61
  122.2 52.7 %shard_map.116 = bf16[624,256]{1,0:T(8,128)(2,1)} custom-call(bf16[2,624,128]{2,1,0:T(8,128)(2,1)} %bitcast.98, bf16[4096,256]{1,0:T(8,128)(2,1)} %refs_1_.3), custom_call_target="tpu_custom_call" | custom-call | tf_op jit(solution)/shard_map/pallas_call | solution.py:157
  175.1 1.6 gather_fusion.2
  176.9 0.7 copy.64
  177.6 0.7 copy.90
  (41 shorter events, 2.0 us)
Async XLA Ops:
  0.6 1.6 copy-start
  4.9 50.6 %copy-start.4 = (bf16[1,2,152,256]{3,2,1,0:T(8,128)(2,1)S(1)}, bf16[1,2,152,256]{3,2,1,0:T(8,128)(2,1)}, u32[]{:S(2)}) copy-start(bf16[1,2,152,256]{3,2,1,0:T(8,128)(2,1)} %param.15) | copy-start | bytes 466948
  68.7 48.2 %copy-start.6 = (s32[13,1]{0,1:T(1,128)S(1)}, s32[13,1]{0,1:T(1,128)}, u32[]{:S(2)}) copy-start(s32[13,1]{0,1:T(1,128)} %param.13) | copy-start | bytes 160
  70.6 47.0 %copy-start.3 = (s32[13,48,48]{2,1,0:T(8,128)S(1)}, s32[13,48,48]{2,1,0:T(8,128)}, u32[]{:S(2)}) copy-start(s32[13,48,48]{2,1,0:T(8,128)} %param.12) | copy-start | bytes 359428
  70.6 47.3 %copy-start.1 = (bf16[13,2,48,256]{3,2,1,0:T(8,128)(2,1)S(1)}, bf16[13,2,48,256]{3,2,1,0:T(8,128)(2,1)}, u32[]{:S(2)}) copy-start(bf16[13,2,48,256]{3,2,1,0:T(8,128)(2,1)} %param.11) | copy-start | bytes 1916932
  121.4 53.5 %copy-start.5 = (s32[13,8]{0,1:T(8,128)S(1)}, s32[13,8]{0,1:T(8,128)}, u32[]{:S(2)}) copy-start(s32[13,8]{0,1:T(8,128)} %param.14) | copy-start | bytes 1252
  174.9 2.7 %copy-start.2 = (bf16[624,256]{1,0:T(8,128)(2,1)S(1)}, bf16[624,256]{1,0:T(8,128)(2,1)}, u32[]{:S(2)}) copy-start(bf16[624,256]{1,0:T(8,128)(2,1)} %shard_map.116) | copy-start | bytes 958468

commit v9 on v5

--- a/solution.py
+++ b/solution.py
@@ -17,17 +17,14 @@
 NEG_FILL = -1e30
 
 
-def swapped(value, axis, apart):
-    mask = 2**apart
-    pairs = [(source, source ^ mask) for source in range(lax.axis_size(axis))]
-    return lax.ppermute(value, axis, pairs)
-
-
-def exchange_kernel(n, count, extra, *refs):
+def exchange_kernel(n, count, paired, *refs):
     sources = refs[:count]
-    targets = refs[count + extra : 2 * count + extra]
-    send_sem, recv_sem, local_sem = refs[2 * count + extra :]
+    pair_sources = refs[count : count + paired]
+    targets = refs[count + paired : 2 * count + paired]
+    pair_targets = refs[2 * count + paired : 2 * count + 2 * paired]
+    send_sem, recv_sem, local_sem, pair_send, pair_recv = refs[2 * count + 2 * paired :]
     me = lax.axis_index("rep")
+    partner = me + 1 - 2 * (me % 2)
     barrier = pltpu.get_barrier_semaphore()
     for offset in range(1, n):
         pl.semaphore_signal(
@@ -35,6 +32,17 @@
         )
     pl.semaphore_wait(barrier, n - 1)
     copies = []
+    for index in range(paired):
+        remote = pltpu.make_async_remote_copy(
+            src_ref=pair_sources[index],
+            dst_ref=pair_targets[index],
+            send_sem=pair_send.at[index],
+            recv_sem=pair_recv.at[index],
+            device_id={"rep": partner},
+            device_id_type=MESH,
+        )
+        remote.start()
+        copies.append(remote)
     for index in range(count):
         local = pltpu.make_async_copy(
             sources[index].at[me], targets[index].at[me], local_sem.at[index]
@@ -57,22 +65,155 @@
         copy.wait()
 
 
-def exchange(arrays, tag, after=()):
+def exchange(arrays, tag, pairs=()):
     n = lax.axis_size("rep")
     count = len(arrays)
-    extra = len(after)
-    return pl.pallas_call(
-        lambda *refs: exchange_kernel(n, count, extra, *refs),
-        out_shape=[jax.ShapeDtypeStruct(a.shape, a.dtype) for a in arrays],
-        in_specs=[pl.BlockSpec(memory_space=pl.ANY)] * (count + extra),
-        out_specs=[pl.BlockSpec(memory_space=pl.ANY)] * count,
+    paired = len(pairs)
+    every = list(arrays) + list(pairs)
+    outs = pl.pallas_call(
+        lambda *refs: exchange_kernel(n, count, paired, *refs),
+        out_shape=[jax.ShapeDtypeStruct(a.shape, a.dtype) for a in every],
+        in_specs=[pl.BlockSpec(memory_space=pl.ANY)] * len(every),
+        out_specs=[pl.BlockSpec(memory_space=pl.ANY)] * len(every),
         scratch_shapes=[
             pltpu.SemaphoreType.DMA((count, n)),
             pltpu.SemaphoreType.DMA((count, n)),
             pltpu.SemaphoreType.DMA((count,)),
+            pltpu.SemaphoreType.DMA((max(paired, 1),)),
+            pltpu.SemaphoreType.DMA((max(paired, 1),)),
         ],
         compiler_params=pltpu.CompilerParams(collective_id=tag, has_side_effects=True),
-    )(*arrays, *after)
+    )(*every)
+    return outs[:count], outs[count:]
+
+
+def ring_exchange_kernel(n_rep, n_z, count, head, has_partial, *refs):
+    sources = refs[:count]
+    a_ref, w_ref = refs[count : count + 2]
+    partial_ref = refs[count + 2] if has_partial else None
+    rest = refs[count + 2 + has_partial :]
+    targets = rest[:count]
+    o_ref = rest[count]
+    scratch = rest[count + 1 :]
+    if count:
+        ex_send, ex_recv, ex_local = scratch[:3]
+        scratch = scratch[3:]
+    slots, send_sem, recv_sem = scratch
+    me_rep = lax.axis_index("rep")
+    me = lax.axis_index("tp")
+    z = me // 2
+    core = me % 2
+    step_z = 1 - 2 * core
+    ring_next = lax.rem(z + step_z + n_z, n_z) * 2 + core
+    ring_prev = lax.rem(z - step_z + n_z, n_z) * 2 + core
+    sibling = z * 2 + (1 - core)
+    barrier = pltpu.get_barrier_semaphore()
+    for peer in (ring_next, ring_prev, sibling):
+        pl.semaphore_signal(barrier, inc=1, device_id={"tp": peer}, device_id_type=MESH)
+    if count:
+        for offset in range(1, n_rep):
+            pl.semaphore_signal(
+                barrier, inc=1, device_id={"rep": lax.rem(me_rep + offset, n_rep)}, device_id_type=MESH
+            )
+    pl.semaphore_wait(barrier, 3 + (n_rep - 1 if count else 0))
+    copies = []
+    for index in range(count):
+        local = pltpu.make_async_copy(
+            sources[index].at[me_rep], targets[index].at[me_rep], ex_local.at[index]
+        )
+        local.start()
+        copies.append(local)
+        for offset in range(1, n_rep):
+            peer = lax.rem(me_rep + offset, n_rep)
+            remote = pltpu.make_async_remote_copy(
+                src_ref=sources[index].at[peer],
+                dst_ref=targets[index].at[me_rep],
+                send_sem=ex_send.at[index, offset],
+                recv_sem=ex_recv.at[index, offset],
+                device_id={"rep": peer},
+                device_id_type=MESH,
+            )
+            remote.start()
+            copies.append(remote)
+    slots[me] = a_ref[...]
+    width = a_ref.shape[1]
+
+    def product(slot, block):
+        row = pl.multiple_of(slot * 2 * width + head * width, width)
+        return jnp.dot(block, w_ref[pl.ds(row, width), :], preferred_element_type=jnp.float32)
+
+    def arrival(slot, sender):
+        pltpu.make_async_remote_copy(
+            src_ref=slots.at[slot],
+            dst_ref=slots.at[slot],
+            send_sem=send_sem.at[0, 0],
+            recv_sem=recv_sem.at[slot],
+            device_id={"tp": sender},
+            device_id_type=MESH,
+        ).wait_recv()
+
+    total = partial_ref[...] if has_partial else jnp.zeros(o_ref.shape, jnp.float32)
+    for step in range(n_z):
+        slot = lax.rem(z - step * step_z + 2 * n_z, n_z) * 2 + core
+        if step == 0:
+            source = a_ref
+        else:
+            arrival(slot, ring_prev)
+            source = slots.at[slot]
+        targets_here = ([(0, ring_next)] if step < n_z - 1 else []) + [(1, sibling)]
+        for kind, peer in targets_here:
+            copy = pltpu.make_async_remote_copy(
+                src_ref=source,
+                dst_ref=slots.at[slot],
+                send_sem=send_sem.at[kind, step],
+                recv_sem=recv_sem.at[slot],
+                device_id={"tp": peer},
+                device_id_type=MESH,
+            )
+            copy.start()
+            copies.append(copy)
+        total = total + product(slot, source[...])
+    for step in range(n_z):
+        slot = lax.rem(z - step * step_z + 2 * n_z, n_z) * 2 + (1 - core)
+        arrival(slot, sibling)
+        total = total + product(slot, slots[slot])
+    o_ref[...] = total.astype(o_ref.dtype)
+    for copy in copies[: count * n_rep]:
+        copy.wait()
+    for copy in copies[count * n_rep :]:
+        copy.wait_send()
+
+
+def ring_exchange(arrays, attn, weight, head, tag, partial=None, out_dtype=jnp.float32):
+    n_rep = lax.axis_size("rep")
+    tp_size = lax.axis_size("tp")
+    count = len(arrays)
+    rows, width = attn.shape
+    extra = [] if partial is None else [partial]
+    scratch = []
+    if count:
+        scratch += [
+            pltpu.SemaphoreType.DMA((count, n_rep)),
+            pltpu.SemaphoreType.DMA((count, n_rep)),
+            pltpu.SemaphoreType.DMA((count,)),
+        ]
+    scratch += [
+        pltpu.VMEM((tp_size, rows, width), jnp.bfloat16),
+        pltpu.SemaphoreType.DMA((2, tp_size // 2)),
+        pltpu.SemaphoreType.DMA((tp_size,)),
+    ]
+    outs = pl.pallas_call(
+        lambda *refs: ring_exchange_kernel(n_rep, tp_size // 2, count, head, len(extra), *refs),
+        out_shape=[jax.ShapeDtypeStruct(a.shape, a.dtype) for a in arrays]
+        + [jax.ShapeDtypeStruct((rows, weight.shape[1]), out_dtype)],
+        in_specs=[pl.BlockSpec(memory_space=pl.ANY)] * count
+        + [pl.BlockSpec(memory_space=pltpu.VMEM)] * (2 + len(extra)),
+        out_specs=[pl.BlockSpec(memory_space=pl.ANY)] * count
+        + [pl.BlockSpec(memory_space=pltpu.VMEM)],
+        scratch_shapes=scratch,
+        compiler_params=pltpu.CompilerParams(collective_id=tag, has_side_effects=True),
+    )(*arrays, attn, weight, *extra)
+    return outs[:count], outs[count]
 
 
 def split_heads(rows):
@@ -167,8 +308,7 @@
     per_group = max(2, (req_here + groups - 1) // groups)
     n_slots = groups * per_group
     positions = jnp.arange(PCAP, dtype=jnp.int32)
-    live_flag = (positions < spill_len[0]).astype(jnp.bfloat16)
-    partner_cache, partner_flag = swapped((spill_cache, live_flag), "rep", 0)
+    own_len = jnp.full((8, 128), spill_len[0], jnp.float32)
 
     target = dest_group[:, 0]
     same_target = target[:, None] == target[None, :]
@@ -182,12 +322,12 @@
         "sr,rtc->stc", selector, queries, preferred_element_type=jnp.float32
     ).astype(jnp.bfloat16)
     outbound = outbound.reshape(groups, per_group, TREE, local_cols)
-    (inbound,) = exchange([outbound], 0)
+    (inbound,), (partner_cache, partner_len) = exchange([outbound], 0, (spill_cache, own_len))
     routed_rows = inbound.reshape(n_slots * TREE, local_cols)
 
     key_rows = jnp.concatenate([prompt_cache[0, 0], partner_cache[0, 0]], axis=0)
     value_rows = jnp.concatenate([prompt_cache[0, 1], partner_cache[0, 1]], axis=0)
-    seen = jnp.concatenate([positions < first_len[0], partner_flag > 0.5], axis=0)
+    seen = jnp.concatenate([positions < first_len[0], positions.astype(jnp.float32) < partner_len[0, 0]], axis=0)
     normed, lse = prompt_attend(routed_rows, key_rows, value_rows, seen)
 
     lse_width = per_group * TREE
@@ -199,14 +339,11 @@
     tree_max, tree_total, tree_accum = tree_attend(
         queries, tree_cache[:, 0], tree_cache[:, 1], tree_mask == 1
     )
-    tp_size = lax.axis_size("tp")
-    weight_rows = out_weight.reshape(tp_size, heads_here, HD, out_weight.shape[1])
-    summed = None
-    previous = ()
-    for head in range(heads_here):
-        back_out, back_lse = exchange(
-            [normed[head].reshape(groups, per_group, TREE, HD), lse[head]], 1 + head, previous
-        )
+
+    def returned(head):
+        return [normed[head].reshape(groups, per_group, TREE, HD), lse[head]]
+
+    def combined(head, back_out, back_lse):
         back_lse = back_lse.reshape(groups, lse_tile)[:, :lse_width].reshape(n_slots, TREE)
         remote_out = jnp.take(back_out.reshape(n_slots, TREE, HD), slot_index, axis=0)
         remote_lse = jnp.take(back_lse, slot_index, axis=0)
@@ -218,15 +355,17 @@
             remote_out.astype(jnp.float32) * factor_remote[..., None]
             + tree_accum[:, :, head] * factor_tree[..., None]
         )
-        attn = (accum / totals[..., None]).reshape(req_here * TREE, HD).astype(jnp.bfloat16)
-        previous = (attn,)
-        part = jnp.dot(
-            lax.all_gather(attn, "tp", axis=1, tiled=True),
-            weight_rows[:, head].reshape(tp_size * HD, out_weight.shape[1]),
-            preferred_element_type=jnp.float32,
-        )
-        summed = part if summed is None else summed + part
-    projected = summed.astype(jnp.bfloat16).reshape(req_here, TREE, out_weight.shape[1])
+        return (accum / totals[..., None]).reshape(req_here * TREE, HD).astype(jnp.bfloat16)
+
+    assert heads_here == 2
+    (back_out, back_lse), _ = exchange(returned(0), 1)
+    attn_first = combined(0, back_out, back_lse)
+    (back_out, back_lse), partial = ring_exchange(returned(1), attn_first, out_weight, 0, 2)
+    attn_second = combined(1, back_out, back_lse)
+    _, projected = ring_exchange(
+        [], attn_second, out_weight, 1, 3, partial=partial, out_dtype=jnp.bfloat16
+    )
+    projected = projected.reshape(req_here, TREE, out_weight.shape[1])
     accepted_cache = jnp.take_along_axis(tree_cache, accepted_path[:, None, :, None], axis=2)
     return (projected, accepted_cache)
 

time: 221 us -> 205 us (0.928)
  Pallas kernels: 110 us -> 174 us
  waiting for transfers between devices: 56.8 us -> 0 us
  between operations: 15.6 us -> 2.2 us
  starting transfers between devices: 6.17 us -> 0 us
  matrix products: 7.17 us -> 1.34 us
    pallas_call x3 -> x4, Pallas kernels: 101 us -> 165 us  [the longest x2 89.1 us: ring_exchange(): pl.pallas_call(lambda *refs: ring_exchange_kernel(n_rep, tp_size // 2, co...]
    all_gather x2 -> x0, waiting for transfers between devices: 56.7 us -> none  [local(): lax.all_gather(attn, 'tp', axis=1, tiled=True)]
    ppermute x2 -> x0, starting transfers between devices: 6.09 us -> none  [swapped(): return lax.ppermute(value, axis, pairs)]
    dot_general x2 -> x0, matrix products: 5.83 us -> none  [local(): jnp.dot(lax.all_gather(attn, 'tp', axis=1, tiled=True), weight_rows[:, he...]
    unnamed x16 -> x19, local copies, waits for them, and re-layouts: 3.91 us -> 4.63 us
  transfers between devices with their start and end apart: 4 -> 0, of which waited for: 2 -> 0; matrix products, arithmetic and copies ran while one was open for 9% -> 0% of each run, Pallas kernels for 32% -> 0%
where the time goes in v9:
time: 205 us; the launch traced here: 204 us
  Pallas kernels  174 us (85%)
  local copies, waits for them, and re-layouts  20.6 us (10%)
  other arithmetic  5.62 us (3%)
  between operations  2.2 us (1%)
    pallas_call x2, Pallas kernels, ring_exchange(): pl.pallas_call(lambda *refs: ring_exchange_kernel(n_rep, tp_size // 2, co...  89.1 us
    pallas_call x2, Pallas kernels, exchange(): pl.pallas_call(lambda *refs: exchange_kernel(n, count, paired, *refs), ou...  76 us
    pallas_call x1, Pallas kernels, prompt_attend(): pl.pallas_call(prompt_kernel, out_shape=[jax.ShapeDtypeStruct((cols // HD...  9.18 us
    unnamed x19, local copies, waits for them, and re-layouts  4.63 us

profile of v9, /device:TPU:1, one launch (start us, length us, event | category | flops | bytes accessed | tf_op | source)
XLA Modules:
  0.0 204.1 jit_solution(10841315120699300251)
XLA Ops:
  0.6 0.9 convert_reduce_fusion
  1.6 0.7 compare_and_fusion.1
  2.2 0.7 convolution_convert_fusion
  2.9 2.0 copy.44
  6.2 48.4 %shard_map.113 = (bf16[32,2,48,256]{3,2,1,0:T(8,128)(2,1)}, bf16[1,2,152,256]{3,2,1,0:T(8,128)(2,1)}, f32[8,128]{1,0:T(8,128)}) custom-call(bf16[32,2,48,256]{3,2,1,0:T(8,128)(2,1)} %bitcast.120, bf16[1,2,152,256]{3,2,1,0:T(8,128)(2,1)} %refs_1_.2, f32[8,128]{1,0:T(8,128)} %broadcast_in_dim.61.refs_2_), custom_call_target="tpu_custom_call" | custom-call | tf_op jit(solution)/shard_map/pallas_call | solution.py:73
  54.6 0.9 slice_bitcast_fusion.2
  55.6 0.8 fusion.24
  56.4 1.2 slice.68
  59.5 9.2 %shard_map.114 = (bf16[2,3072,128]{2,1,0:T(8,128)(2,1)}, f32[8,3072]{1,0:T(8,128)}) custom-call(bf16[3072,256]{1,0:T(8,128)(2,1)} %bitcast.123, bf16[384,256]{1,0:T(8,128)(2,1)} %get-tuple-element.50.k_ref, bf16[384,256]{1,0:T(8,128)(2,1)} %get-tuple-element.51.v_ref, f32[1,384]{1,0:T(1,128)} %reshape.114.seen_ref), custom_call_target="tpu_custom_call" | custom-call | tf_op jit(solution)/shard_map/pallas_call | solution.py:255
  68.7 2.6 %fusion.46 = (bf16[1,3072,128]{2,1,0:T(8,128)(2,1)}, bf16[1,3072,128]{2,1,0:T(8,128)(2,1)}) fusion(bf16[2,3072,128]{2,1,0:T(8,128)(2,1)} %get-tuple-element.17), kind=kLoop, calls=%fused_computation.86 | loop fusion | bytes 3145728 | tf_op jit(solution)/shard_map/slice | solution.py:344
  71.3 1.0 slice.70
  72.4 0.7 copy.58
  73.1 27.6 %shard_map.115 = (bf16[32,2,48,128]{3,2,1,0:T(8,128)(2,1)}, f32[32,8,128]{2,1,0:T(8,128)}) custom-call(bf16[32,2,48,128]{3,2,1,0:T(8,128)(2,1)} %bitcast.121, f32[32,8,128]{2,1,0:T(8,128)} %bitcast.128), custom_call_target="tpu_custom_call" | custom-call | tf_op jit(solution)/shard_map/pallas_call | solution.py:73
  100.7 0.9 copy.80
  103.3 1.7 gather_fusion.1
  105.4 1.0 fusion.21
  106.4 0.7 copy.57
  107.1 48.8 %shard_map.116 = (bf16[32,2,48,128]{3,2,1,0:T(8,128)(2,1)}, f32[32,8,128]{2,1,0:T(8,128)}, f32[624,256]{1,0:T(8,128)}) custom-call(bf16[32,2,48,128]{3,2,1,0:T(8,128)(2,1)} %bitcast.122, f32[32,8,128]{2,1,0:T(8,128)} %bitcast.127, bf16[624,128]{1,0:T(8,128)(2,1)} %bitcast.125, bf16[4096,256]{1,0:T(8,128)(2,1)} %refs_1_.3), custom_call_target="tpu_custom_call" | custom-call | tf_op jit(solution)/shard_map/pallas_call | solution.py:205
  155.9 0.9 copy.79
  157.6 1.7 gather_fusion.3
  159.3 1.0 fusion.22
  160.3 40.3 %shard_map.117 = bf16[624,256]{1,0:T(8,128)(2,1)} custom-call(bf16[624,128]{1,0:T(8,128)(2,1)} %bitcast.126, bf16[4096,256]{1,0:T(8,128)(2,1)} %refs_1_.3, f32[624,256]{1,0:T(8,128)} %get-tuple-element.23.refs_2_), custom_call_target="tpu_custom_call" | custom-call | tf_op jit(solution)/shard_map/pallas_call | solution.py:205
  200.8 1.6 gather_fusion
  203.3 0.7 copy.84
  (46 shorter events, 5.8 us)
Async XLA Ops:
  0.6 1.6 copy-start
  4.9 50.6 %copy-start.4 = (bf16[1,2,152,256]{3,2,1,0:T(8,128)(2,1)S(1)}, bf16[1,2,152,256]{3,2,1,0:T(8,128)(2,1)}, u32[]{:S(2)}) copy-start(bf16[1,2,152,256]{3,2,1,0:T(8,128)(2,1)} %param.19) | copy-start | bytes 466948
  71.3 31.0 %copy-start.3 = (s32[13,48,48]{2,1,0:T(8,128)S(1)}, s32[13,48,48]{2,1,0:T(8,128)}, u32[]{:S(2)}) copy-start(s32[13,48,48]{2,1,0:T(8,128)} %param.16) | copy-start | bytes 359428
  71.3 31.2 %copy-start.1 = (bf16[13,2,48,256]{3,2,1,0:T(8,128)(2,1)S(1)}, bf16[13,2,48,256]{3,2,1,0:T(8,128)(2,1)}, u32[]{:S(2)}) copy-start(bf16[13,2,48,256]{3,2,1,0:T(8,128)(2,1)} %param.15) | copy-start | bytes 1916932
  160.3 40.3 %copy-start.5 = (s32[13,8]{0,1:T(8,128)S(1)}, s32[13,8]{0,1:T(8,128)}, u32[]{:S(2)}) copy-start(s32[13,8]{0,1:T(8,128)} %param.18) | copy-start | bytes 1252
  200.6 2.7 %copy-start.2 = (bf16[624,256]{1,0:T(8,128)(2,1)S(1)}, bf16[624,256]{1,0:T(8,128)(2,1)}, u32[]{:S(2)}) copy-start(bf16[624,256]{1,0:T(8,128)(2,1)} %shard_map.117) | copy-start | bytes 958468

commit v10 on v8

--- a/solution.py
+++ b/solution.py
@@ -99,41 +99,48 @@
         pl.semaphore_signal(barrier, inc=1, device_id={"tp": peer}, device_id_type=MESH)
     pl.semaphore_wait(barrier, 3)
     slots[me] = a_ref[...]
-    chains = ((0, 1, up, down), (1, -1, down, up))
+    far = n_z // 2
+    near = n_z - 1 - far
+    chains = ((0, 1, up, down, far), (0, -1, down, up, near), (1, 1, up, down, near), (1, -1, down, up, far))
     width = a_ref.shape[2]
     halves = slots.shape[1]
 
     def product(slot, half, block):
         row = pl.multiple_of((slot * halves + half) * width, width)
         return jnp.dot(block, w_ref[pl.ds(row, width), :], preferred_element_type=jnp.float32)
-
-    total = jnp.zeros(o_ref.shape, jnp.float32)
 
     def arrival(slot, half, sender):
         pltpu.make_async_remote_copy(
             src_ref=slots.at[slot, half],
             dst_ref=slots.at[slot, half],
-            send_sem=send_sem.at[half, 0],
+            send_sem=send_sem.at[0, 0, 0],
             recv_sem=recv_sem.at[slot, half],
             device_id={"tp": sender},
             device_id_type=MESH,
         ).wait_recv()
 
+    total = jnp.zeros(o_ref.shape, jnp.float32)
     sends = []
-    for step in range(n_z):
-        for half, direction, ahead, behind in chains:
+    for step in range(far + 1):
+        for chain, (half, direction, ahead, behind, hops) in enumerate(chains):
+            if step > hops or (step == 0 and direction < 0):
+                continue
             slot = lax.rem(z - step * direction + 2 * n_z, n_z) * 2 + core
             if step == 0:
                 source = a_ref.at[half]
             else:
                 arrival(slot, half, behind)
                 source = slots.at[slot, half]
-            targets = ([(half, ahead)] if step < n_z - 1 else []) + [(2 + half, sibling)]
+            targets = [(1, sibling)]
+            if step < hops:
+                targets = [(0, ahead)] + targets
+            if step == 0:
+                targets = targets + [(0, down)]
             for kind, peer in targets:
                 copy = pltpu.make_async_remote_copy(
                     src_ref=source,
                     dst_ref=slots.at[slot, half],
-                    send_sem=send_sem.at[kind, step],
+                    send_sem=send_sem.at[chain + (1 if peer is down and step == 0 else 0), kind, step],
                     recv_sem=recv_sem.at[slot, half],
                     device_id={"tp": peer},
                     device_id_type=MESH,
@@ -141,8 +148,10 @@
                 copy.start()
                 sends.append(copy)
             total = total + product(slot, half, source[...])
-    for step in range(n_z):
-        for half, direction, ahead, behind in chains:
+    for half, direction, ahead, behind, hops in chains:
+        for step in range(hops + 1):
+            if step == 0 and direction < 0:
+                continue
             slot = lax.rem(z - step * direction + 2 * n_z, n_z) * 2 + (1 - core)
             arrival(slot, half, sibling)
             total = total + product(slot, half, slots[slot, half])
@@ -161,7 +170,7 @@
         out_specs=pl.BlockSpec(memory_space=pltpu.VMEM),
         scratch_shapes=[
             pltpu.VMEM((tp_size, halves, rows, width), jnp.bfloat16),
-            pltpu.SemaphoreType.DMA((4, tp_size // 2)),
+            pltpu.SemaphoreType.DMA((4, 2, tp_size // 4 + 1)),
             pltpu.SemaphoreType.DMA((tp_size, halves)),
         ],
         compiler_params=pltpu.CompilerParams(collective_id=3, has_side_effects=True),

time: 180 us -> 170 us (0.944)
  Pallas kernels: 155 us -> 147 us
    pallas_call x1, Pallas kernels: 52.7 us -> 44.3 us  [gather_project(): pl.pallas_call(lambda *refs: gather_project_kernel(tp_size // 2, *refs),...]
where the time goes in v10:
time: 170 us
  Pallas kernels  147 us (86%)
  local copies, waits for them, and re-layouts  15.3 us (9%)
  other arithmetic  3.53 us (2%)
  between operations  2.22 us (1%)
  matrix products  1.77 us (1%)
    pallas_call x2, Pallas kernels, exchange(): pl.pallas_call(lambda *refs: exchange_kernel(n, count, paired, *refs), ou...  93.6 us
    pallas_call x1, Pallas kernels, gather_project(): pl.pallas_call(lambda *refs: gather_project_kernel(tp_size // 2, *refs),...  44.3 us
    pallas_call x1, Pallas kernels, prompt_attend(): pl.pallas_call(prompt_kernel, out_shape=[jax.ShapeDtypeStruct((n_rows, co...  9.2 us

profile of v10, /device:TPU:1, one launch (start us, length us, event | category | flops | bytes accessed | tf_op | source)
XLA Modules:
  0.0 169.9 jit_solution(11329286638359688473)
XLA Ops:
  0.6 0.9 convert_reduce_fusion
  1.6 0.7 multiply_add_fusion
  2.2 0.7 convolution_convert_fusion
  2.9 2.0 %copy.51 = bf16[64,48,256]{2,1,0:T(8,128)(2,1)} copy(bf16[64,48,256]{2,0,1:T(8,128)(2,1)S(1)} %convolution_convert_fusion) | data formatting | bytes 3145728 | tf_op jit(solution)/shard_map/convert_element_type | solution.py:284
  5.6 0.6 broadcast_in_dim.61.refs_2_
  6.2 48.4 %shard_map.113 = (bf16[32,2,48,256]{3,2,1,0:T(8,128)(2,1)}, bf16[1,2,152,256]{3,2,1,0:T(8,128)(2,1)}, f32[8,128]{1,0:T(8,128)}) custom-call(bf16[32,2,48,256]{3,2,1,0:T(8,128)(2,1)} %bitcast.94, bf16[1,2,152,256]{3,2,1,0:T(8,128)(2,1)} %refs_1_.2, f32[8,128]{1,0:T(8,128)} %broadcast_in_dim.61.refs_2_), custom_call_target="tpu_custom_call" | custom-call | tf_op jit(solution)/shard_map/pallas_call | solution.py:73
  54.6 0.9 slice_bitcast_fusion
  55.6 0.8 fusion.21
  56.4 1.2 slice.31
  58.2 0.7 convert_compare_fusion
  59.0 0.6 reshape.108.seen_ref
  59.5 9.2 %shard_map.114 = (bf16[3072,256]{1,0:T(8,128)(2,1)}, f32[8,3072]{1,0:T(8,128)}) custom-call(bf16[3072,256]{1,0:T(8,128)(2,1)} %bitcast.95, bf16[384,256]{1,0:T(8,128)(2,1)} %get-tuple-element.35.k_ref, bf16[384,256]{1,0:T(8,128)(2,1)} %get-tuple-element.36.v_ref, f32[1,384]{1,0:T(1,128)} %reshape.108.seen_ref), custom_call_target="tpu_custom_call" | custom-call | tf_op jit(solution)/shard_map/pallas_call | solution.py:216
  68.7 0.9 slice.32
  69.9 0.7 copy.68
  70.6 45.2 %shard_map.115 = (bf16[32,2,48,256]{3,2,1,0:T(8,128)(2,1)}, f32[32,8,128]{2,1,0:T(8,128)}) custom-call(bf16[32,2,48,256]{3,2,1,0:T(8,128)(2,1)} %bitcast.96, f32[32,8,128]{2,1,0:T(8,128)} %bitcast.99), custom_call_target="tpu_custom_call" | custom-call | tf_op jit(solution)/shard_map/pallas_call | solution.py:73
  115.8 0.9 copy.86
  117.0 0.6 gather_fusion.1
  118.6 2.0 %gather_fusion = bf16[13,48,256]{2,1,0:T(8,128)(2,1)S(1)} fusion(bf16[64,48,256]{2,1,0:T(8,128)(2,1)} %bitcast.105, s32[1024]{0:T(1024)S(1)} %pad_clamp_fusion), kind=kCustom, calls=%fused_computation | custom fusion | bytes 639028 | tf_op jit(solution)/shard_map/jit(_take)/gather | solution.py:309
  120.7 0.7 fusion.5
  121.4 0.7 copy.61
  122.2 44.3 %shard_map.116 = bf16[624,256]{1,0:T(8,128)(2,1)} custom-call(bf16[2,624,128]{2,1,0:T(8,128)(2,1)} %bitcast.98, bf16[4096,256]{1,0:T(8,128)(2,1)} %refs_1_.3), custom_call_target="tpu_custom_call" | custom-call | tf_op jit(solution)/shard_map/pallas_call | solution.py:166
  166.7 1.6 gather_fusion.2
  168.5 0.7 copy.64
  169.2 0.7 copy.90
  (41 shorter events, 2.0 us)
Async XLA Ops:
  0.6 1.6 copy-start
  4.9 50.6 %copy-start.4 = (bf16[1,2,152,256]{3,2,1,0:T(8,128)(2,1)S(1)}, bf16[1,2,152,256]{3,2,1,0:T(8,128)(2,1)}, u32[]{:S(2)}) copy-start(bf16[1,2,152,256]{3,2,1,0:T(8,128)(2,1)} %param.15) | copy-start | bytes 466948
  68.7 48.2 %copy-start.6 = (s32[13,1]{0,1:T(1,128)S(1)}, s32[13,1]{0,1:T(1,128)}, u32[]{:S(2)}) copy-start(s32[13,1]{0,1:T(1,128)} %param.13) | copy-start | bytes 160
  70.6 47.0 %copy-start.3 = (s32[13,48,48]{2,1,0:T(8,128)S(1)}, s32[13,48,48]{2,1,0:T(8,128)}, u32[]{:S(2)}) copy-start(s32[13,48,48]{2,1,0:T(8,128)} %param.12) | copy-start | bytes 359428
  70.6 47.3 %copy-start.1 = (bf16[13,2,48,256]{3,2,1,0:T(8,128)(2,1)S(1)}, bf16[13,2,48,256]{3,2,1,0:T(8,128)(2,1)}, u32[]{:S(2)}) copy-start(bf16[13,2,48,256]{3,2,1,0:T(8,128)(2,1)} %param.11) | copy-start | bytes 1916932
  121.4 45.1 %copy-start.5 = (s32[13,8]{0,1:T(8,128)S(1)}, s32[13,8]{0,1:T(8,128)}, u32[]{:S(2)}) copy-start(s32[13,8]{0,1:T(8,128)} %param.14) | copy-start | bytes 1252
  166.5 2.7 %copy-start.2 = (bf16[624,256]{1,0:T(8,128)(2,1)S(1)}, bf16[624,256]{1,0:T(8,128)(2,1)}, u32[]{:S(2)}) copy-start(bf16[624,256]{1,0:T(8,128)(2,1)} %shard_map.116) | copy-start | bytes 958468

commit v11 on v10

--- a/solution.py
+++ b/solution.py
@@ -197,7 +197,7 @@
         ) * (1.0 / math.sqrt(HD))
         scores = jnp.where(visible, scores, NEG_FILL)
         peaks = jnp.max(scores, axis=1, keepdims=True)
-        raw = jnp.where(visible, jnp.exp(scores - peaks), 0.0)
+        raw = jnp.exp(scores - peaks)
         totals = jnp.sum(raw, axis=1, keepdims=True)
         accum = jnp.dot(raw.astype(jnp.bfloat16), v_ref[:, cols], preferred_element_type=jnp.float32)
         o_ref[:, cols] = (accum / totals).astype(o_ref.dtype)
@@ -212,7 +212,7 @@
     key_rows = jnp.pad(key_rows, ((0, padded - n_keys), (0, 0)))
     value_rows = jnp.pad(value_rows, ((0, padded - n_keys), (0, 0)))
     seen_row = jnp.pad(seen.astype(jnp.float32), (0, padded - n_keys)).reshape(1, padded)
-    block = 384
+    block = 768
     return pl.pallas_call(
         prompt_kernel,
         out_shape=[

time: 170 us -> 168 us (0.988)
  Pallas kernels: 147 us -> 145 us
    pallas_call x1, Pallas kernels: 9.2 us -> 6.72 us  [prompt_attend(): pl.pallas_call(prompt_kernel, out_shape=[jax.ShapeDtypeStruct((n_rows, co...]
where the time goes in v11:
time: 168 us; the launch traced here: 167 us
  Pallas kernels  145 us (86%)
  local copies, waits for them, and re-layouts  15.3 us (9%)
  other arithmetic  3.53 us (2%)
  between operations  2.22 us (1%)
  matrix products  1.76 us (1%)
    pallas_call x2, Pallas kernels, exchange(): pl.pallas_call(lambda *refs: exchange_kernel(n, count, paired, *refs), ou...  93.6 us
    pallas_call x1, Pallas kernels, gather_project(): pl.pallas_call(lambda *refs: gather_project_kernel(tp_size // 2, *refs),...  44.3 us
    pallas_call x1, Pallas kernels, prompt_attend(): pl.pallas_call(prompt_kernel, out_shape=[jax.ShapeDtypeStruct((n_rows, co...  6.72 us

profile of v11, /device:TPU:1, one launch (start us, length us, event | category | flops | bytes accessed | tf_op | source)
XLA Modules:
  0.0 167.4 jit_solution(11400621175574236127)
XLA Ops:
  0.6 0.9 convert_reduce_fusion
  1.6 0.7 multiply_add_fusion
  2.2 0.7 convolution_convert_fusion
  2.9 2.0 %copy.51 = bf16[64,48,256]{2,1,0:T(8,128)(2,1)} copy(bf16[64,48,256]{2,0,1:T(8,128)(2,1)S(1)} %convolution_convert_fusion) | data formatting | bytes 3145728 | tf_op jit(solution)/shard_map/convert_element_type | solution.py:284
  5.6 0.6 broadcast_in_dim.61.refs_2_
  6.2 48.4 %shard_map.113 = (bf16[32,2,48,256]{3,2,1,0:T(8,128)(2,1)}, bf16[1,2,152,256]{3,2,1,0:T(8,128)(2,1)}, f32[8,128]{1,0:T(8,128)}) custom-call(bf16[32,2,48,256]{3,2,1,0:T(8,128)(2,1)} %bitcast.94, bf16[1,2,152,256]{3,2,1,0:T(8,128)(2,1)} %refs_1_.2, f32[8,128]{1,0:T(8,128)} %broadcast_in_dim.61.refs_2_), custom_call_target="tpu_custom_call" | custom-call | tf_op jit(solution)/shard_map/pallas_call | solution.py:73
  54.6 0.9 slice_bitcast_fusion
  55.6 0.8 fusion.21
  56.4 1.2 slice.31
  58.2 0.7 convert_compare_fusion
  59.0 0.6 reshape.108.seen_ref
  59.5 6.7 %shard_map.114 = (bf16[3072,256]{1,0:T(8,128)(2,1)}, f32[8,3072]{1,0:T(8,128)}) custom-call(bf16[3072,256]{1,0:T(8,128)(2,1)} %bitcast.95, bf16[384,256]{1,0:T(8,128)(2,1)} %get-tuple-element.35.k_ref, bf16[384,256]{1,0:T(8,128)(2,1)} %get-tuple-element.36.v_ref, f32[1,384]{1,0:T(1,128)} %reshape.108.seen_ref), custom_call_target="tpu_custom_call" | custom-call | tf_op jit(solution)/shard_map/pallas_call | solution.py:216
  66.3 0.9 slice.32
  67.4 0.7 copy.68
  68.1 45.2 %shard_map.115 = (bf16[32,2,48,256]{3,2,1,0:T(8,128)(2,1)}, f32[32,8,128]{2,1,0:T(8,128)}) custom-call(bf16[32,2,48,256]{3,2,1,0:T(8,128)(2,1)} %bitcast.96, f32[32,8,128]{2,1,0:T(8,128)} %bitcast.99), custom_call_target="tpu_custom_call" | custom-call | tf_op jit(solution)/shard_map/pallas_call | solution.py:73
  113.3 0.9 copy.86
  114.5 0.6 gather_fusion.1
  116.1 2.0 %gather_fusion = bf16[13,48,256]{2,1,0:T(8,128)(2,1)S(1)} fusion(bf16[64,48,256]{2,1,0:T(8,128)(2,1)} %bitcast.105, s32[1024]{0:T(1024)S(1)} %pad_clamp_fusion), kind=kCustom, calls=%fused_computation | custom fusion | bytes 639028 | tf_op jit(solution)/shard_map/jit(_take)/gather | solution.py:309
  118.2 0.7 fusion.5
  118.9 0.7 copy.61
  119.7 44.3 %shard_map.116 = bf16[624,256]{1,0:T(8,128)(2,1)} custom-call(bf16[2,624,128]{2,1,0:T(8,128)(2,1)} %bitcast.98, bf16[4096,256]{1,0:T(8,128)(2,1)} %refs_1_.3), custom_call_target="tpu_custom_call" | custom-call | tf_op jit(solution)/shard_map/pallas_call | solution.py:166
  164.2 1.6 gather_fusion.2
  166.1 0.7 copy.64
  166.7 0.7 copy.90
  (41 shorter events, 2.0 us)
Async XLA Ops:
  0.6 1.6 copy-start
  4.9 50.6 %copy-start.4 = (bf16[1,2,152,256]{3,2,1,0:T(8,128)(2,1)S(1)}, bf16[1,2,152,256]{3,2,1,0:T(8,128)(2,1)}, u32[]{:S(2)}) copy-start(bf16[1,2,152,256]{3,2,1,0:T(8,128)(2,1)} %param.15) | copy-start | bytes 466948
  66.3 48.2 %copy-start.6 = (s32[13,1]{0,1:T(1,128)S(1)}, s32[13,1]{0,1:T(1,128)}, u32[]{:S(2)}) copy-start(s32[13,1]{0,1:T(1,128)} %param.13) | copy-start | bytes 160
  68.1 47.0 %copy-start.3 = (s32[13,48,48]{2,1,0:T(8,128)S(1)}, s32[13,48,48]{2,1,0:T(8,128)}, u32[]{:S(2)}) copy-start(s32[13,48,48]{2,1,0:T(8,128)} %param.12) | copy-start | bytes 359428
  68.1 47.3 %copy-start.1 = (bf16[13,2,48,256]{3,2,1,0:T(8,128)(2,1)S(1)}, bf16[13,2,48,256]{3,2,1,0:T(8,128)(2,1)}, u32[]{:S(2)}) copy-start(bf16[13,2,48,256]{3,2,1,0:T(8,128)(2,1)} %param.11) | copy-start | bytes 1916932
  118.9 45.1 %copy-start.5 = (s32[13,8]{0,1:T(8,128)S(1)}, s32[13,8]{0,1:T(8,128)}, u32[]{:S(2)}) copy-start(s32[13,8]{0,1:T(8,128)} %param.14) | copy-start | bytes 1252
  164.0 2.7 %copy-start.2 = (bf16[624,256]{1,0:T(8,128)(2,1)S(1)}, bf16[624,256]{1,0:T(8,128)(2,1)}, u32[]{:S(2)}) copy-start(bf16[624,256]{1,0:T(8,128)(2,1)} %shard_map.116) | copy-start | bytes 958468

commit v12 on v11

--- a/solution.py
+++ b/solution.py
@@ -276,12 +276,11 @@
     earlier = jnp.arange(req_here)[None, :] < jnp.arange(req_here)[:, None]
     rank_index = jnp.sum(jnp.logical_and(same_target, earlier), axis=1)
     slot_index = target * per_group + rank_index
-    selector = (jnp.arange(n_slots, dtype=jnp.int32)[:, None] == slot_index[None, :]).astype(
-        jnp.bfloat16
-    )
-    outbound = jnp.einsum(
-        "sr,rtc->stc", selector, queries, preferred_element_type=jnp.float32
-    ).astype(jnp.bfloat16)
+    slot_source = (
+        jnp.full((n_slots,), req_here, jnp.int32).at[slot_index].set(jnp.arange(req_here, dtype=jnp.int32))
+    )
+    padded_queries = jnp.concatenate([queries, jnp.zeros((1,) + queries.shape[1:], queries.dtype)], 0)
+    outbound = jnp.take(padded_queries, slot_source, axis=0, mode="clip")
     outbound = outbound.reshape(groups, per_group, TREE, local_cols)
     (inbound,), (partner_cache, partner_len) = exchange([outbound], 0, (spill_cache, own_len))
     routed_rows = inbound.reshape(n_slots * TREE, local_cols)

time: 168 us -> 169 us (level)
    convert_element_type x1 -> x0, local copies, waits for them, and re-layouts: 2.03 us -> none  [local(): outbound = jnp.einsum('sr,rtc->stc', selector, queries, preferred_element...]
    gather x0 -> x1, local copies, waits for them, and re-layouts: none -> 1.81 us  [local(): outbound = jnp.take(padded_queries, slot_source, axis=0, mode='clip')]
where the time goes in v12:
time: 169 us; the launch traced here: 168 us
  Pallas kernels  145 us (86%)
  local copies, waits for them, and re-layouts  16.7 us (10%)
  other arithmetic  3.53 us (2%)
  between operations  2.23 us (1%)
    pallas_call x2, Pallas kernels, exchange(): pl.pallas_call(lambda *refs: exchange_kernel(n, count, paired, *refs), ou...  93.6 us
    pallas_call x1, Pallas kernels, gather_project(): pl.pallas_call(lambda *refs: gather_project_kernel(tp_size // 2, *refs),...  44.3 us
    pallas_call x1, Pallas kernels, prompt_attend(): pl.pallas_call(prompt_kernel, out_shape=[jax.ShapeDtypeStruct((n_rows, co...  6.73 us

profile of v12, /device:TPU:1, one launch (start us, length us, event | category | flops | bytes accessed | tf_op | source)
XLA Modules:
  0.0 168.1 jit_solution(4982207174258307353)
XLA Ops:
  0.6 0.9 convert_reduce_fusion
  1.5 0.7 and_bitcast_fusion
  2.2 0.6 scatter_custom_fusion
  2.8 1.0 concatenate.12
  3.8 1.8 %gather_fusion = bf16[64,48,256]{2,1,0:T(8,128)(2,1)} fusion(bf16[14,48,256]{2,1,0:T(8,128)(2,1)S(1)} %concatenate.12, s32[1024]{0:T(1024)S(1)} %pad_clamp_fusion.1), kind=kCustom, calls=%fused_computation | custom fusion | bytes 3145984 | tf_op jit(solution)/shard_map/jit(_take)/gather | solution.py:283
  6.3 0.6 broadcast_in_dim.70.refs_2_
  6.9 48.4 %shard_map.113 = (bf16[32,2,48,256]{3,2,1,0:T(8,128)(2,1)}, bf16[1,2,152,256]{3,2,1,0:T(8,128)(2,1)}, f32[8,128]{1,0:T(8,128)}) custom-call(bf16[32,2,48,256]{3,2,1,0:T(8,128)(2,1)} %bitcast.90, bf16[1,2,152,256]{3,2,1,0:T(8,128)(2,1)} %refs_1_.2, f32[8,128]{1,0:T(8,128)} %broadcast_in_dim.70.refs_2_), custom_call_target="tpu_custom_call" | custom-call | tf_op jit(solution)/shard_map/pallas_call | solution.py:73
  55.3 0.9 slice_bitcast_fusion
  56.3 0.8 fusion.20
  57.1 1.2 slice.31
  58.9 0.7 convert_compare_fusion
  60.2 6.7 %shard_map.114 = (bf16[3072,256]{1,0:T(8,128)(2,1)}, f32[8,3072]{1,0:T(8,128)}) custom-call(bf16[3072,256]{1,0:T(8,128)(2,1)} %bitcast.91, bf16[384,256]{1,0:T(8,128)(2,1)} %get-tuple-element.35.k_ref, bf16[384,256]{1,0:T(8,128)(2,1)} %get-tuple-element.36.v_ref, f32[1,384]{1,0:T(1,128)} %reshape.100.seen_ref), custom_call_target="tpu_custom_call" | custom-call | tf_op jit(solution)/shard_map/pallas_call | solution.py:216
  67.0 0.9 slice.32
  68.1 0.7 copy.60
  68.8 45.3 %shard_map.115 = (bf16[32,2,48,256]{3,2,1,0:T(8,128)(2,1)}, f32[32,8,128]{2,1,0:T(8,128)}) custom-call(bf16[32,2,48,256]{3,2,1,0:T(8,128)(2,1)} %bitcast.92, f32[32,8,128]{2,1,0:T(8,128)} %bitcast.95), custom_call_target="tpu_custom_call" | custom-call | tf_op jit(solution)/shard_map/pallas_call | solution.py:73
  114.0 0.9 copy.76
  115.2 0.6 gather_fusion.2
  116.9 2.0 %gather_fusion.1 = bf16[13,48,256]{2,1,0:T(8,128)(2,1)S(1)} fusion(bf16[64,48,256]{2,1,0:T(8,128)(2,1)} %bitcast.101, s32[1024]{0:T(1024)S(1)} %pad_clamp_fusion), kind=kCustom, calls=%fused_computation.1 | custom fusion | bytes 639028 | tf_op jit(solution)/shard_map/jit(_take)/gather | solution.py:308
  118.9 0.7 fusion.5
  119.7 0.7 copy.53
  120.5 44.3 %shard_map.116 = bf16[624,256]{1,0:T(8,128)(2,1)} custom-call(bf16[2,624,128]{2,1,0:T(8,128)(2,1)} %bitcast.94, bf16[4096,256]{1,0:T(8,128)(2,1)} %refs_1_.3), custom_call_target="tpu_custom_call" | custom-call | tf_op jit(solution)/shard_map/pallas_call | solution.py:166
  164.9 1.6 gather_fusion.3
  166.8 0.7 copy.56
  167.4 0.7 copy.80
  (41 shorter events, 2.6 us)
Async XLA Ops:
  5.7 50.6 %copy-start.4 = (bf16[1,2,152,256]{3,2,1,0:T(8,128)(2,1)S(1)}, bf16[1,2,152,256]{3,2,1,0:T(8,128)(2,1)}, u32[]{:S(2)}) copy-start(bf16[1,2,152,256]{3,2,1,0:T(8,128)(2,1)} %param.15) | copy-start | bytes 466948
  68.8 47.0 %copy-start.2 = (s32[13,48,48]{2,1,0:T(8,128)S(1)}, s32[13,48,48]{2,1,0:T(8,128)}, u32[]{:S(2)}) copy-start(s32[13,48,48]{2,1,0:T(8,128)} %param.12) | copy-start | bytes 359428
  68.8 47.3 %copy-start = (bf16[13,2,48,256]{3,2,1,0:T(8,128)(2,1)S(1)}, bf16[13,2,48,256]{3,2,1,0:T(8,128)(2,1)}, u32[]{:S(2)}) copy-start(bf16[13,2,48,256]{3,2,1,0:T(8,128)(2,1)} %param.11) | copy-start | bytes 1916932
  115.2 1.0 copy-start.3
  119.7 45.0 %copy-start.5 = (s32[13,8]{0,1:T(8,128)S(1)}, s32[13,8]{0,1:T(8,128)}, u32[]{:S(2)}) copy-start(s32[13,8]{0,1:T(8,128)} %param.14) | copy-start | bytes 1252
  164.7 2.7 %copy-start.1 = (bf16[624,256]{1,0:T(8,128)(2,1)S(1)}, bf16[624,256]{1,0:T(8,128)(2,1)}, u32[]{:S(2)}) copy-start(bf16[624,256]{1,0:T(8,128)(2,1)} %shard_map.116) | copy-start | bytes 958468

commit v13 on v11

--- a/solution.py
+++ b/solution.py
@@ -212,7 +212,7 @@
     key_rows = jnp.pad(key_rows, ((0, padded - n_keys), (0, 0)))
     value_rows = jnp.pad(value_rows, ((0, padded - n_keys), (0, 0)))
     seen_row = jnp.pad(seen.astype(jnp.float32), (0, padded - n_keys)).reshape(1, padded)
-    block = 768
+    block = 1536
     return pl.pallas_call(
         prompt_kernel,
         out_shape=[

time: 168 us -> 168 us (level)
  no operation moved by 1% of the time
where the time goes in v13:
time: 168 us; the launch traced here: 167 us
  Pallas kernels  144 us (86%)
  local copies, waits for them, and re-layouts  15.3 us (9%)
  other arithmetic  3.53 us (2%)
  between operations  2.22 us (1%)
  matrix products  1.76 us (1%)
    pallas_call x2, Pallas kernels, exchange(): pl.pallas_call(lambda *refs: exchange_kernel(n, count, paired, *refs), ou...  93.6 us
    pallas_call x1, Pallas kernels, gather_project(): pl.pallas_call(lambda *refs: gather_project_kernel(tp_size // 2, *refs),...  44.3 us
    pallas_call x1, Pallas kernels, prompt_attend(): pl.pallas_call(prompt_kernel, out_shape=[jax.ShapeDtypeStruct((n_rows, co...  6.41 us

profile of v13, /device:TPU:1, one launch (start us, length us, event | category | flops | bytes accessed | tf_op | source)
XLA Modules:
  0.0 167.1 jit_solution(14061934053931464281)
XLA Ops:
  0.6 0.9 convert_reduce_fusion
  1.6 0.7 multiply_add_fusion
  2.2 0.7 convolution_convert_fusion
  2.9 2.0 %copy.51 = bf16[64,48,256]{2,1,0:T(8,128)(2,1)} copy(bf16[64,48,256]{2,0,1:T(8,128)(2,1)S(1)} %convolution_convert_fusion) | data formatting | bytes 3145728 | tf_op jit(solution)/shard_map/convert_element_type | solution.py:284
  5.6 0.6 broadcast_in_dim.61.refs_2_
  6.2 48.4 %shard_map.113 = (bf16[32,2,48,256]{3,2,1,0:T(8,128)(2,1)}, bf16[1,2,152,256]{3,2,1,0:T(8,128)(2,1)}, f32[8,128]{1,0:T(8,128)}) custom-call(bf16[32,2,48,256]{3,2,1,0:T(8,128)(2,1)} %bitcast.94, bf16[1,2,152,256]{3,2,1,0:T(8,128)(2,1)} %refs_1_.2, f32[8,128]{1,0:T(8,128)} %broadcast_in_dim.61.refs_2_), custom_call_target="tpu_custom_call" | custom-call | tf_op jit(solution)/shard_map/pallas_call | solution.py:73
  54.6 0.9 slice_bitcast_fusion
  55.6 0.8 fusion.21
  56.4 1.2 slice.31
  58.2 0.7 convert_compare_fusion
  59.0 0.6 reshape.108.seen_ref
  59.5 6.4 %shard_map.114 = (bf16[3072,256]{1,0:T(8,128)(2,1)}, f32[8,3072]{1,0:T(8,128)}) custom-call(bf16[3072,256]{1,0:T(8,128)(2,1)} %bitcast.95, bf16[384,256]{1,0:T(8,128)(2,1)} %get-tuple-element.35.k_ref, bf16[384,256]{1,0:T(8,128)(2,1)} %get-tuple-element.36.v_ref, f32[1,384]{1,0:T(1,128)} %reshape.108.seen_ref), custom_call_target="tpu_custom_call" | custom-call | tf_op jit(solution)/shard_map/pallas_call | solution.py:216
  65.9 0.9 slice.32
  67.1 0.7 copy.68
  67.8 45.2 %shard_map.115 = (bf16[32,2,48,256]{3,2,1,0:T(8,128)(2,1)}, f32[32,8,128]{2,1,0:T(8,128)}) custom-call(bf16[32,2,48,256]{3,2,1,0:T(8,128)(2,1)} %bitcast.96, f32[32,8,128]{2,1,0:T(8,128)} %bitcast.99), custom_call_target="tpu_custom_call" | custom-call | tf_op jit(solution)/shard_map/pallas_call | solution.py:73
  113.0 0.9 copy.86
  114.2 0.6 gather_fusion.1
  115.8 2.0 %gather_fusion = bf16[13,48,256]{2,1,0:T(8,128)(2,1)S(1)} fusion(bf16[64,48,256]{2,1,0:T(8,128)(2,1)} %bitcast.105, s32[1024]{0:T(1024)S(1)} %pad_clamp_fusion), kind=kCustom, calls=%fused_computation | custom fusion | bytes 639028 | tf_op jit(solution)/shard_map/jit(_take)/gather | solution.py:309
  117.9 0.7 fusion.5
  118.6 0.7 copy.61
  119.4 44.3 %shard_map.116 = bf16[624,256]{1,0:T(8,128)(2,1)} custom-call(bf16[2,624,128]{2,1,0:T(8,128)(2,1)} %bitcast.98, bf16[4096,256]{1,0:T(8,128)(2,1)} %refs_1_.3), custom_call_target="tpu_custom_call" | custom-call | tf_op jit(solution)/shard_map/pallas_call | solution.py:166
  163.9 1.6 gather_fusion.2
  165.7 0.7 copy.64
  166.4 0.7 copy.90
  (41 shorter events, 2.0 us)
Async XLA Ops:
  0.6 1.6 copy-start
  4.9 50.6 %copy-start.4 = (bf16[1,2,152,256]{3,2,1,0:T(8,128)(2,1)S(1)}, bf16[1,2,152,256]{3,2,1,0:T(8,128)(2,1)}, u32[]{:S(2)}) copy-start(bf16[1,2,152,256]{3,2,1,0:T(8,128)(2,1)} %param.15) | copy-start | bytes 466948
  65.9 48.2 %copy-start.6 = (s32[13,1]{0,1:T(1,128)S(1)}, s32[13,1]{0,1:T(1,128)}, u32[]{:S(2)}) copy-start(s32[13,1]{0,1:T(1,128)} %param.13) | copy-start | bytes 160
  67.8 47.0 %copy-start.3 = (s32[13,48,48]{2,1,0:T(8,128)S(1)}, s32[13,48,48]{2,1,0:T(8,128)}, u32[]{:S(2)}) copy-start(s32[13,48,48]{2,1,0:T(8,128)} %param.12) | copy-start | bytes 359428
  67.8 47.3 %copy-start.1 = (bf16[13,2,48,256]{3,2,1,0:T(8,128)(2,1)S(1)}, bf16[13,2,48,256]{3,2,1,0:T(8,128)(2,1)}, u32[]{:S(2)}) copy-start(bf16[13,2,48,256]{3,2,1,0:T(8,128)(2,1)} %param.11) | copy-start | bytes 1916932
  118.6 45.1 %copy-start.5 = (s32[13,8]{0,1:T(8,128)S(1)}, s32[13,8]{0,1:T(8,128)}, u32[]{:S(2)}) copy-start(s32[13,8]{0,1:T(8,128)} %param.14) | copy-start | bytes 1252
  163.7 2.7 %copy-start.2 = (bf16[624,256]{1,0:T(8,128)(2,1)S(1)}, bf16[624,256]{1,0:T(8,128)(2,1)}, u32[]{:S(2)}) copy-start(bf16[624,256]{1,0:T(8,128)(2,1)} %shard_map.116) | copy-start | bytes 958468

commit v14 on v11

--- a/solution.py
+++ b/solution.py
@@ -303,11 +303,14 @@
         1,
     )
     back_out = back_out.reshape(n_slots, TREE, local_cols)
-    back_lse = back_lse.reshape(groups, lse_tile)[:, :lse_width]
-    back_lse = jnp.moveaxis(back_lse.reshape(groups, heads_here, per_group, TREE), 1, 3)
-    back_lse = back_lse.reshape(n_slots, TREE, heads_here)
+    lse_index = (
+        (slot_index // per_group)[:, None, None] * lse_tile
+        + jnp.arange(heads_here, dtype=jnp.int32)[None, None, :] * (per_group * TREE)
+        + (slot_index % per_group)[:, None, None] * TREE
+        + jnp.arange(TREE, dtype=jnp.int32)[None, :, None]
+    )
     remote_out = split_heads(jnp.take(back_out, slot_index, axis=0)).astype(jnp.float32)
-    remote_lse = jnp.take(back_lse, slot_index, axis=0)
+    remote_lse = jnp.take(back_lse.reshape(groups * lse_tile), lse_index, mode="clip")
 
     tree_max, tree_total, tree_accum = tree_attend(
         queries, tree_cache[:, 0], tree_cache[:, 1], tree_mask == 1

time: 168 us -> 175 us (1.042)
  local copies, waits for them, and re-layouts: 15.3 us -> 22.2 us
    gather x1 -> x3, local copies, waits for them, and re-layouts: 0.58 us -> 7.49 us  [local(): jnp.take(back_lse.reshape(groups * lse_tile), lse_index, mode='clip')]
where the time goes in v14:
time: 175 us; the launch traced here: 174 us
  Pallas kernels  144 us (82%)
  local copies, waits for them, and re-layouts  22.2 us (13%)
  other arithmetic  3.62 us (2%)
  between operations  2.24 us (1%)
  matrix products  1.77 us (1%)
    pallas_call x2, Pallas kernels, exchange(): pl.pallas_call(lambda *refs: exchange_kernel(n, count, paired, *refs), ou...  93.6 us
    pallas_call x1, Pallas kernels, gather_project(): pl.pallas_call(lambda *refs: gather_project_kernel(tp_size // 2, *refs),...  44.2 us
    gather x3, local copies, waits for them, and re-layouts, local(): jnp.take(back_lse.reshape(groups * lse_tile), lse_index, mode='clip')  7.49 us
    pallas_call x1, Pallas kernels, prompt_attend(): pl.pallas_call(prompt_kernel, out_shape=[jax.ShapeDtypeStruct((n_rows, co...  6.72 us

profile of v14, /device:TPU:1, one launch (start us, length us, event | category | flops | bytes accessed | tf_op | source)
XLA Modules:
  0.0 174.3 jit_solution(209185891279501797)
XLA Ops:
  0.6 0.9 convert_reduce_fusion
  1.6 0.7 fusion.32
  2.2 0.7 convolution_convert_fusion
  2.9 2.0 %copy.54 = bf16[64,48,256]{2,1,0:T(8,128)(2,1)} copy(bf16[64,48,256]{2,0,1:T(8,128)(2,1)S(1)} %convolution_convert_fusion) | data formatting | bytes 3145728 | tf_op jit(solution)/shard_map/convert_element_type | solution.py:284
  5.6 0.6 broadcast_in_dim.57.refs_2_
  6.2 48.4 %shard_map.113 = (bf16[32,2,48,256]{3,2,1,0:T(8,128)(2,1)}, bf16[1,2,152,256]{3,2,1,0:T(8,128)(2,1)}, f32[8,128]{1,0:T(8,128)}) custom-call(bf16[32,2,48,256]{3,2,1,0:T(8,128)(2,1)} %bitcast.95, bf16[1,2,152,256]{3,2,1,0:T(8,128)(2,1)} %refs_1_.2, f32[8,128]{1,0:T(8,128)} %broadcast_in_dim.57.refs_2_), custom_call_target="tpu_custom_call" | custom-call | tf_op jit(solution)/shard_map/pallas_call | solution.py:73
  54.6 0.9 slice_bitcast_fusion
  55.6 0.8 fusion.21
  56.4 1.2 slice.28
  58.2 0.7 convert_compare_fusion
  59.0 0.6 reshape.200.seen_ref
  59.6 6.7 %shard_map.114 = (bf16[3072,256]{1,0:T(8,128)(2,1)}, f32[8,3072]{1,0:T(8,128)}) custom-call(bf16[3072,256]{1,0:T(8,128)(2,1)} %bitcast.96, bf16[384,256]{1,0:T(8,128)(2,1)} %get-tuple-element.37.k_ref, bf16[384,256]{1,0:T(8,128)(2,1)} %get-tuple-element.38.v_ref, f32[1,384]{1,0:T(1,128)} %reshape.200.seen_ref), custom_call_target="tpu_custom_call" | custom-call | tf_op jit(solution)/shard_map/pallas_call | solution.py:216
  66.3 0.9 slice.29
  67.4 0.7 copy.71
  68.1 45.2 %shard_map.115 = (bf16[32,2,48,256]{3,2,1,0:T(8,128)(2,1)}, f32[32,8,128]{2,1,0:T(8,128)}) custom-call(bf16[32,2,48,256]{3,2,1,0:T(8,128)(2,1)} %bitcast.97, f32[32,8,128]{2,1,0:T(8,128)} %bitcast.100), custom_call_target="tpu_custom_call" | custom-call | tf_op jit(solution)/shard_map/pallas_call | solution.py:73
  113.6 0.5 copy-done.1
  114.2 7.1 %gather_fusion.1 = f32[1248]{0:T(1024)S(1)} fusion(f32[32768]{0:T(1024)S(1)} %bitcast.94, s32[2048]{0:T(1024)S(1)} %pad_clamp_fusion), kind=kCustom, calls=%fused_computation.1 | custom fusion | bytes 14976 | tf_op jit(solution)/shard_map/jit(_take)/gather | solution.py:313
  123.1 2.0 %gather_fusion = bf16[13,48,256]{2,1,0:T(8,128)(2,1)S(1)} fusion(bf16[64,48,256]{2,1,0:T(8,128)(2,1)} %bitcast.102, s32[1024]{0:T(1024)S(1)} %pad_clamp_fusion.1), kind=kCustom, calls=%fused_computation | custom fusion | bytes 639028 | tf_op jit(solution)/shard_map/jit(_take)/gather | solution.py:312
  125.2 0.7 fusion.5
  125.9 0.7 copy.64
  126.7 44.2 %shard_map.116 = bf16[624,256]{1,0:T(8,128)(2,1)} custom-call(bf16[2,624,128]{2,1,0:T(8,128)(2,1)} %bitcast.99, bf16[4096,256]{1,0:T(8,128)(2,1)} %refs_1_.3), custom_call_target="tpu_custom_call" | custom-call | tf_op jit(solution)/shard_map/pallas_call | solution.py:166
  171.1 1.6 gather_fusion.2
  172.9 0.7 copy.67
  173.6 0.7 copy.90
  (46 shorter events, 2.9 us)
Async XLA Ops:
  0.6 1.6 copy-start
  5.0 50.6 %copy-start.5 = (bf16[1,2,152,256]{3,2,1,0:T(8,128)(2,1)S(1)}, bf16[1,2,152,256]{3,2,1,0:T(8,128)(2,1)}, u32[]{:S(2)}) copy-start(bf16[1,2,152,256]{3,2,1,0:T(8,128)(2,1)} %param.15) | copy-start | bytes 466948
  113.3 0.9 copy-start.1
  114.2 7.5 %copy-start.4 = (s32[13,48,48]{2,1,0:T(8,128)S(1)}, s32[13,48,48]{2,1,0:T(8,128)}, u32[]{:S(2)}) copy-start(s32[13,48,48]{2,1,0:T(8,128)} %param.12) | copy-start | bytes 359428
  121.3 1.1 copy-start.2
  122.4 0.7 copy-start.7
  125.9 45.0 %copy-start.6 = (s32[13,8]{0,1:T(8,128)S(1)}, s32[13,8]{0,1:T(8,128)}, u32[]{:S(2)}) copy-start(s32[13,8]{0,1:T(8,128)} %param.14) | copy-start | bytes 1252
  170.9 2.7 %copy-start.3 = (bf16[624,256]{1,0:T(8,128)(2,1)S(1)}, bf16[624,256]{1,0:T(8,128)(2,1)}, u32[]{:S(2)}) copy-start(bf16[624,256]{1,0:T(8,128)(2,1)} %shard_map.116) | copy-start | bytes 958468

commit v15 on v11

--- a/solution.py
+++ b/solution.py
@@ -104,60 +104,71 @@
     chains = ((0, 1, up, down, far), (0, -1, down, up, near), (1, 1, up, down, near), (1, -1, down, up, far))
     width = a_ref.shape[2]
     halves = slots.shape[1]
+    rows = a_ref.shape[1]
+    first = -(-rows // 32) * 16
+    pieces = ((0, first), (first, rows - first))
 
     def product(slot, half, block):
         row = pl.multiple_of((slot * halves + half) * width, width)
         return jnp.dot(block, w_ref[pl.ds(row, width), :], preferred_element_type=jnp.float32)
 
-    def arrival(slot, half, sender):
+    def arrival(slot, half, piece, sender):
+        begin, size = pieces[piece]
         pltpu.make_async_remote_copy(
-            src_ref=slots.at[slot, half],
-            dst_ref=slots.at[slot, half],
-            send_sem=send_sem.at[0, 0, 0],
-            recv_sem=recv_sem.at[slot, half],
+            src_ref=slots.at[slot, half, pl.ds(begin, size)],
+            dst_ref=slots.at[slot, half, pl.ds(begin, size)],
+            send_sem=send_sem.at[0, 0, 0, 0],
+            recv_sem=recv_sem.at[slot, half, piece],
             device_id={"tp": sender},
             device_id_type=MESH,
         ).wait_recv()
 
-    total = jnp.zeros(o_ref.shape, jnp.float32)
+    totals = [jnp.zeros((size, o_ref.shape[1]), jnp.float32) for _, size in pieces]
     sends = []
     for step in range(far + 1):
-        for chain, (half, direction, ahead, behind, hops) in enumerate(chains):
-            if step > hops or (step == 0 and direction < 0):
-                continue
-            slot = lax.rem(z - step * direction + 2 * n_z, n_z) * 2 + core
-            if step == 0:
-                source = a_ref.at[half]
-            else:
-                arrival(slot, half, behind)
-                source = slots.at[slot, half]
-            targets = [(1, sibling)]
-            if step < hops:
-                targets = [(0, ahead)] + targets
-            if step == 0:
-                targets = targets + [(0, down)]
-            for kind, peer in targets:
-                copy = pltpu.make_async_remote_copy(
-                    src_ref=source,
-                    dst_ref=slots.at[slot, half],
-                    send_sem=send_sem.at[chain + (1 if peer is down and step == 0 else 0), kind, step],
-                    recv_sem=recv_sem.at[slot, half],
-                    device_id={"tp": peer},
-                    device_id_type=MESH,
+        for piece, (begin, size) in enumerate(pieces):
+            part = pl.ds(begin, size)
+            for chain, (half, direction, ahead, behind, hops) in enumerate(chains):
+                if step > hops or (step == 0 and direction < 0):
+                    continue
+                slot = lax.rem(z - step * direction + 2 * n_z, n_z) * 2 + core
+                if step == 0:
+                    source = a_ref.at[half, part]
+                else:
+                    arrival(slot, half, piece, behind)
+                    source = slots.at[slot, half, part]
+                targets = [(1, sibling)]
+                if step < hops:
+                    targets = [(0, ahead)] + targets
+                if step == 0:
+                    targets = targets + [(0, down)]
+                for kind, peer in targets:
+                    lane = chain + (1 if peer is down and step == 0 else 0)
+                    copy = pltpu.make_async_remote_copy(
+                        src_ref=source,
+                        dst_ref=slots.at[slot, half, part],
+                        send_sem=send_sem.at[lane, piece, kind, step],
+                        recv_sem=recv_sem.at[slot, half, piece],
+                        device_id={"tp": peer},
+                        device_id_type=MESH,
+                    )
+                    copy.start()
+                    sends.append(copy)
+                totals[piece] = totals[piece] + product(slot, half, source[...])
+    for piece, (begin, size) in enumerate(pieces):
+        for half, direction, ahead, behind, hops in chains:
+            for step in range(hops + 1):
+                if step == 0 and direction < 0:
+                    continue
+                slot = lax.rem(z - step * direction + 2 * n_z, n_z) * 2 + (1 - core)
+                arrival(slot, half, piece, sibling)
+                totals[piece] = totals[piece] + product(
+                    slot, half, slots[slot, half, pl.ds(begin, size)]
                 )
-                copy.start()
-                sends.append(copy)
-            total = total + product(slot, half, source[...])
-    for half, direction, ahead, behind, hops in chains:
-        for step in range(hops + 1):
-            if step == 0 and direction < 0:
-                continue
-            slot = lax.rem(z - step * direction + 2 * n_z, n_z) * 2 + (1 - core)
-            arrival(slot, half, sibling)
-            total = total + product(slot, half, slots[slot, half])
     for copy in sends:
         copy.wait_send()
-    o_ref[...] = total.astype(o_ref.dtype)
+    for piece, (begin, size) in enumerate(pieces):
+        o_ref[pl.ds(begin, size), :] = totals[piece].astype(o_ref.dtype)
 
 
 def gather_project(attn, weight):
@@ -170,8 +181,8 @@
         out_specs=pl.BlockSpec(memory_space=pltpu.VMEM),
         scratch_shapes=[
             pltpu.VMEM((tp_size, halves, rows, width), jnp.bfloat16),
-            pltpu.SemaphoreType.DMA((4, 2, tp_size // 4 + 1)),
-            pltpu.SemaphoreType.DMA((tp_size, halves)),
+            pltpu.SemaphoreType.DMA((4, 2, 2, tp_size // 4 + 1)),
+            pltpu.SemaphoreType.DMA((tp_size, halves, 2)),
         ],
         compiler_params=pltpu.CompilerParams(collective_id=3, has_side_effects=True),
     )(attn, weight)

time: 168 us -> 168 us (level)
  no operation moved by 1% of the time
where the time goes in v15:
time: 168 us
  Pallas kernels  145 us (86%)
  local copies, waits for them, and re-layouts  15.3 us (9%)
  other arithmetic  3.53 us (2%)
  between operations  2.22 us (1%)
  matrix products  1.76 us (1%)
    pallas_call x2, Pallas kernels, exchange(): pl.pallas_call(lambda *refs: exchange_kernel(n, count, paired, *refs), ou...  93.6 us
    pallas_call x1, Pallas kernels, gather_project(): pl.pallas_call(lambda *refs: gather_project_kernel(tp_size // 2, *refs),...  44.6 us
    pallas_call x1, Pallas kernels, prompt_attend(): pl.pallas_call(prompt_kernel, out_shape=[jax.ShapeDtypeStruct((n_rows, co...  6.72 us

profile of v15, /device:TPU:1, one launch (start us, length us, event | category | flops | bytes accessed | tf_op | source)
XLA Modules:
  0.0 167.7 jit_solution(5291748308300744096)
XLA Ops:
  0.6 0.9 convert_reduce_fusion
  1.6 0.7 multiply_add_fusion
  2.2 0.7 convolution_convert_fusion
  2.9 2.0 %copy.51 = bf16[64,48,256]{2,1,0:T(8,128)(2,1)} copy(bf16[64,48,256]{2,0,1:T(8,128)(2,1)S(1)} %convolution_convert_fusion) | data formatting | bytes 3145728 | tf_op jit(solution)/shard_map/convert_element_type | solution.py:295
  5.6 0.6 broadcast_in_dim.61.refs_2_
  6.2 48.4 %shard_map.113 = (bf16[32,2,48,256]{3,2,1,0:T(8,128)(2,1)}, bf16[1,2,152,256]{3,2,1,0:T(8,128)(2,1)}, f32[8,128]{1,0:T(8,128)}) custom-call(bf16[32,2,48,256]{3,2,1,0:T(8,128)(2,1)} %bitcast.94, bf16[1,2,152,256]{3,2,1,0:T(8,128)(2,1)} %refs_1_.2, f32[8,128]{1,0:T(8,128)} %broadcast_in_dim.61.refs_2_), custom_call_target="tpu_custom_call" | custom-call | tf_op jit(solution)/shard_map/pallas_call | solution.py:73
  54.6 0.9 slice_bitcast_fusion
  55.6 0.8 fusion.21
  56.4 1.2 slice.31
  58.2 0.7 convert_compare_fusion
  59.0 0.6 reshape.108.seen_ref
  59.5 6.7 %shard_map.114 = (bf16[3072,256]{1,0:T(8,128)(2,1)}, f32[8,3072]{1,0:T(8,128)}) custom-call(bf16[3072,256]{1,0:T(8,128)(2,1)} %bitcast.95, bf16[384,256]{1,0:T(8,128)(2,1)} %get-tuple-element.35.k_ref, bf16[384,256]{1,0:T(8,128)(2,1)} %get-tuple-element.36.v_ref, f32[1,384]{1,0:T(1,128)} %reshape.108.seen_ref), custom_call_target="tpu_custom_call" | custom-call | tf_op jit(solution)/shard_map/pallas_call | solution.py:227
  66.3 0.9 slice.32
  67.4 0.7 copy.68
  68.1 45.2 %shard_map.115 = (bf16[32,2,48,256]{3,2,1,0:T(8,128)(2,1)}, f32[32,8,128]{2,1,0:T(8,128)}) custom-call(bf16[32,2,48,256]{3,2,1,0:T(8,128)(2,1)} %bitcast.96, f32[32,8,128]{2,1,0:T(8,128)} %bitcast.99), custom_call_target="tpu_custom_call" | custom-call | tf_op jit(solution)/shard_map/pallas_call | solution.py:73
  113.3 0.9 copy.86
  114.5 0.6 gather_fusion.1
  116.1 2.0 %gather_fusion = bf16[13,48,256]{2,1,0:T(8,128)(2,1)S(1)} fusion(bf16[64,48,256]{2,1,0:T(8,128)(2,1)} %bitcast.105, s32[1024]{0:T(1024)S(1)} %pad_clamp_fusion), kind=kCustom, calls=%fused_computation | custom fusion | bytes 639028 | tf_op jit(solution)/shard_map/jit(_take)/gather | solution.py:320
  118.2 0.7 fusion.5
  118.9 0.7 copy.61
  119.7 44.6 %shard_map.116 = bf16[624,256]{1,0:T(8,128)(2,1)} custom-call(bf16[2,624,128]{2,1,0:T(8,128)(2,1)} %bitcast.98, bf16[4096,256]{1,0:T(8,128)(2,1)} %refs_1_.3), custom_call_target="tpu_custom_call" | custom-call | tf_op jit(solution)/shard_map/pallas_call | solution.py:177
  164.5 1.6 gather_fusion.2
  166.3 0.7 copy.64
  167.0 0.7 copy.90
  (41 shorter events, 2.0 us)
Async XLA Ops:
  0.6 1.6 copy-start
  4.9 50.6 %copy-start.4 = (bf16[1,2,152,256]{3,2,1,0:T(8,128)(2,1)S(1)}, bf16[1,2,152,256]{3,2,1,0:T(8,128)(2,1)}, u32[]{:S(2)}) copy-start(bf16[1,2,152,256]{3,2,1,0:T(8,128)(2,1)} %param.15) | copy-start | bytes 466948
  66.3 48.2 %copy-start.6 = (s32[13,1]{0,1:T(1,128)S(1)}, s32[13,1]{0,1:T(1,128)}, u32[]{:S(2)}) copy-start(s32[13,1]{0,1:T(1,128)} %param.13) | copy-start | bytes 160
  68.1 47.0 %copy-start.3 = (s32[13,48,48]{2,1,0:T(8,128)S(1)}, s32[13,48,48]{2,1,0:T(8,128)}, u32[]{:S(2)}) copy-start(s32[13,48,48]{2,1,0:T(8,128)} %param.12) | copy-start | bytes 359428
  68.1 47.3 %copy-start.1 = (bf16[13,2,48,256]{3,2,1,0:T(8,128)(2,1)S(1)}, bf16[13,2,48,256]{3,2,1,0:T(8,128)(2,1)}, u32[]{:S(2)}) copy-start(bf16[13,2,48,256]{3,2,1,0:T(8,128)(2,1)} %param.11) | copy-start | bytes 1916932
  118.9 45.3 %copy-start.5 = (s32[13,8]{0,1:T(8,128)S(1)}, s32[13,8]{0,1:T(8,128)}, u32[]{:S(2)}) copy-start(s32[13,8]{0,1:T(8,128)} %param.14) | copy-start | bytes 1252
  164.3 2.7 %copy-start.2 = (bf16[624,256]{1,0:T(8,128)(2,1)S(1)}, bf16[624,256]{1,0:T(8,128)(2,1)}, u32[]{:S(2)}) copy-start(bf16[624,256]{1,0:T(8,128)(2,1)} %shard_map.116) | copy-start | bytes 958468

commit v16 on v11

--- a/solution.py
+++ b/solution.py
@@ -44,11 +44,6 @@
         remote.start()
         copies.append(remote)
     for index in range(count):
-        local = pltpu.make_async_copy(
-            sources[index].at[me], targets[index].at[me], local_sem.at[index]
-        )
-        local.start()
-        copies.append(local)
         for offset in range(1, n):
             peer = lax.rem(me + offset, n)
             remote = pltpu.make_async_remote_copy(
@@ -84,7 +79,12 @@
         ],
         compiler_params=pltpu.CompilerParams(collective_id=tag, has_side_effects=True),
     )(*every)
-    return outs[:count], outs[count:]
+    me = lax.axis_index("rep")
+    placed = [
+        lax.dynamic_update_index_in_dim(out, lax.dynamic_index_in_dim(a, me, 0), me, 0)
+        for out, a in zip(outs[:count], arrays)
+    ]
+    return placed, outs[count:]
 
 
 def gather_project_kernel(n_z, a_ref, w_ref, o_ref, slots, send_sem, recv_sem):

time: 168 us -> 172 us (1.024)
  local copies, waits for them, and re-layouts: 15.3 us -> 19.5 us
    dynamic_update_slice x0 -> x3, local copies, waits for them, and re-layouts: none -> 4.2 us  [exchange(): lax.dynamic_update_index_in_dim(out, lax.dynamic_index_in_dim(a, me, 0),...]
where the time goes in v16:
time: 172 us
  Pallas kernels  145 us (84%)
  local copies, waits for them, and re-layouts  19.5 us (11%)
  other arithmetic  3.54 us (2%)
  between operations  2.22 us (1%)
  matrix products  1.78 us (1%)
    pallas_call x2, Pallas kernels, exchange(): pl.pallas_call(lambda *refs: exchange_kernel(n, count, paired, *refs), ou...  93.5 us
    pallas_call x1, Pallas kernels, gather_project(): pl.pallas_call(lambda *refs: gather_project_kernel(tp_size // 2, *refs),...  44.4 us
    pallas_call x1, Pallas kernels, prompt_attend(): pl.pallas_call(prompt_kernel, out_shape=[jax.ShapeDtypeStruct((n_rows, co...  6.73 us
    dynamic_update_slice x3, local copies, waits for them, and re-layouts, exchange(): lax.dynamic_update_index_in_dim(out, lax.dynamic_index_in_dim(a, me, 0),...  4.2 us

profile of v16, /device:TPU:1, one launch (start us, length us, event | category | flops | bytes accessed | tf_op | source)
XLA Modules:
  0.0 171.6 jit_solution(4294727868051110947)
XLA Ops:
  0.6 0.9 convert_reduce_fusion
  1.6 0.7 multiply_add_fusion
  2.2 0.7 convolution_convert_fusion
  2.9 2.0 %copy.51 = bf16[64,48,256]{2,1,0:T(8,128)(2,1)} copy(bf16[64,48,256]{2,0,1:T(8,128)(2,1)S(1)} %convolution_convert_fusion) | data formatting | bytes 3145728 | tf_op jit(solution)/shard_map/convert_element_type | solution.py:284
  6.2 48.4 %shard_map.113 = (bf16[32,2,48,256]{3,2,1,0:T(8,128)(2,1)}, bf16[1,2,152,256]{3,2,1,0:T(8,128)(2,1)}, f32[8,128]{1,0:T(8,128)}) custom-call(bf16[32,2,48,256]{3,2,1,0:T(8,128)(2,1)} %bitcast.94, bf16[1,2,152,256]{3,2,1,0:T(8,128)(2,1)} %refs_1_.2, f32[8,128]{1,0:T(8,128)} %broadcast_in_dim.61.refs_2_), custom_call_target="tpu_custom_call" | custom-call | tf_op jit(solution)/shard_map/pallas_call | solution.py:68
  54.6 1.4 dynamic-slice_dynamic-update-slice_fusion.1
  56.0 0.9 slice_bitcast_fusion
  57.0 0.8 fusion.21
  57.8 1.2 slice.31
  59.6 0.7 convert_compare_fusion
  61.0 6.7 %shard_map.114 = (bf16[3072,256]{1,0:T(8,128)(2,1)}, f32[8,3072]{1,0:T(8,128)}) custom-call(bf16[3072,256]{1,0:T(8,128)(2,1)} %bitcast.98, bf16[384,256]{1,0:T(8,128)(2,1)} %get-tuple-element.35.k_ref, bf16[384,256]{1,0:T(8,128)(2,1)} %get-tuple-element.36.v_ref, f32[1,384]{1,0:T(1,128)} %reshape.108.seen_ref), custom_call_target="tpu_custom_call" | custom-call | tf_op jit(solution)/shard_map/pallas_call | solution.py:216
  67.7 0.9 slice.32
  68.8 0.7 copy.68
  69.5 45.1 %shard_map.115 = (bf16[32,2,48,256]{3,2,1,0:T(8,128)(2,1)}, f32[32,8,128]{2,1,0:T(8,128)}) custom-call(bf16[32,2,48,256]{3,2,1,0:T(8,128)(2,1)} %bitcast.96, f32[32,8,128]{2,1,0:T(8,128)} %bitcast.101), custom_call_target="tpu_custom_call" | custom-call | tf_op jit(solution)/shard_map/pallas_call | solution.py:68
  114.7 1.5 dynamic-slice_dynamic-update-slice_fusion
  116.2 2.0 %gather_fusion = bf16[13,48,256]{2,1,0:T(8,128)(2,1)S(1)} fusion(bf16[64,48,256]{2,1,0:T(8,128)(2,1)} %bitcast.108, s32[1024]{0:T(1024)S(1)} %pad_clamp_fusion), kind=kCustom, calls=%fused_computation | custom fusion | bytes 639028 | tf_op jit(solution)/shard_map/jit(_take)/gather | solution.py:309
  118.2 1.3 dynamic-slice_dynamic-update-slice_fusion.2
  119.5 0.9 copy.86
  122.3 0.7 fusion.5
  123.1 0.7 copy.61
  123.8 44.4 %shard_map.116 = bf16[624,256]{1,0:T(8,128)(2,1)} custom-call(bf16[2,624,128]{2,1,0:T(8,128)(2,1)} %bitcast.100, bf16[4096,256]{1,0:T(8,128)(2,1)} %refs_1_.3), custom_call_target="tpu_custom_call" | custom-call | tf_op jit(solution)/shard_map/pallas_call | solution.py:166
  168.4 1.6 gather_fusion.2
  170.3 0.7 copy.64
  170.9 0.7 copy.93
  (44 shorter events, 3.8 us)
Async XLA Ops:
  0.6 1.6 copy-start
  5.0 52.0 %copy-start.4 = (bf16[1,2,152,256]{3,2,1,0:T(8,128)(2,1)S(1)}, bf16[1,2,152,256]{3,2,1,0:T(8,128)(2,1)}, u32[]{:S(2)}) copy-start(bf16[1,2,152,256]{3,2,1,0:T(8,128)(2,1)} %param.15) | copy-start | bytes 466948
  67.7 48.5 %copy-start.6 = (s32[13,1]{0,1:T(1,128)S(1)}, s32[13,1]{0,1:T(1,128)}, u32[]{:S(2)}) copy-start(s32[13,1]{0,1:T(1,128)} %param.13) | copy-start | bytes 160
  69.5 51.7 %copy-start.3 = (s32[13,48,48]{2,1,0:T(8,128)S(1)}, s32[13,48,48]{2,1,0:T(8,128)}, u32[]{:S(2)}) copy-start(s32[13,48,48]{2,1,0:T(8,128)} %param.12) | copy-start | bytes 359428
  114.7 6.8 %copy-start.1 = (bf16[13,2,48,256]{3,2,1,0:T(8,128)(2,1)S(1)}, bf16[13,2,48,256]{3,2,1,0:T(8,128)(2,1)}, u32[]{:S(2)}) copy-start(bf16[13,2,48,256]{3,2,1,0:T(8,128)(2,1)} %param.11) | copy-start | bytes 1916932
  123.1 45.1 %copy-start.5 = (s32[13,8]{0,1:T(8,128)S(1)}, s32[13,8]{0,1:T(8,128)}, u32[]{:S(2)}) copy-start(s32[13,8]{0,1:T(8,128)} %param.14) | copy-start | bytes 1252
  168.2 2.7 %copy-start.2 = (bf16[624,256]{1,0:T(8,128)(2,1)S(1)}, bf16[624,256]{1,0:T(8,128)(2,1)}, u32[]{:S(2)}) copy-start(bf16[624,256]{1,0:T(8,128)(2,1)} %shard_map.116) | copy-start | bytes 958468
